TPU v7x, 32 devices: a whole 2x2x4 slice. The times are simulated.
32 devices in a mesh: groups: 2 (over y), width: 4 (over z), hidden: 2 (over x), batch: 2 (over core).
Axes of the slice: x: 2, y: 2, z: 4, core: 2. Of those that a mesh axis runs over, the one named last changes fastest.
Arguments:
- inputs: bfloat16 [2, 32, 16384], P(None, 'groups', 'width'), parts along dimension 1, may hold values from -42 to 42
- norm_gain: float32 [16384], P('width'), may hold values from 0.25 to 1.75
- wq_packed: int32 [16384, 4096], P('width', 'hidden'), may hold values from 0 to 255, as said below
- wq_scales: float32 [128, 8192], P('width', 'hidden'), may hold values from 0.002578125 to 0.01015625
- key_weight: bfloat16 [16384, 512], P('width', 'hidden'), may hold values from -0.046875 to 0.046875
- value_weight: bfloat16 [16384, 512], P('width', 'hidden'), may hold values from -0.046875 to 0.046875
- wo_weight: bfloat16 [8192, 16384], P('hidden', 'width'), may hold values from -0.3125 to 0.3125
- key_cache: bfloat16 [32, 1024, 512], P(('groups', 'width', 'batch'), None, 'hidden'), parts along dimension 0, may hold values from -6 to 6
- value_cache: bfloat16 [32, 1024, 512], P(('groups', 'width', 'batch'), None, 'hidden'), parts along dimension 0, may hold values from -6 to 6
- lengths: int32 [32], P(('groups', 'width', 'batch')), parts along dimension 0, may hold values from 256 to 1022, as said below
Outputs:
- attended: bfloat16 [2, 32, 16384], P(None, ('groups', 'hidden', 'batch'), 'width'), parts along dimension 1
There are 2 independent parts, one for each index of `groups`. A program takes and returns all parts, laid end to end along the dimension named above; an argument that names none is the same for every part. Nothing has to cross between parts.
Inputs may be any that keep to these rules, and one draw needn't show every extreme that they name: `wq_packed`: each word holds two 4-bit codes, bits 4 c to 4 c + 3 for column 2 j + c. `lengths`: some sequence has exactly 1022 filled slots.
All inputs are finite; a program needn't handle non-finite values.
Results may differ from a plain program's by a relative error of at most 0.0091.
Values may be sent and summed in bfloat16 or wider, within the bound.
No kernel may reach another device: no remote copies, remote signals or barrier semaphores. Data moves between devices by JAX's collectives and lax.ppermute only.
A program may use at most 448 MiB of HBM per device.

v0:
```python
import jax
import jax.numpy as jnp
from jax import lax
from jax.sharding import PartitionSpec as P

D = 16384
HEAD = 128
STEPS = 2


def unpack_weights(packed, scales, bits, per_word):
    shifts = jnp.arange(per_word, dtype=jnp.int32) * bits
    codes = packed[:, :, None] >> shifts & (1 << bits) - 1
    values = (codes - (1 << bits - 1)).astype(jnp.float32)
    values = values.reshape(packed.shape[0], packed.shape[1] * per_word)
    group_rows = packed.shape[0] // scales.shape[0]
    values = values.reshape(scales.shape[0], group_rows, values.shape[1]) * scales[:, None, :]
    return values.reshape(packed.shape[0], -1)


def rotate_heads(field, positions):
    half = field.shape[-1] // 2
    freq = 500000.0 ** (-2.0 * jnp.arange(half, dtype=jnp.float32) / field.shape[-1])
    angle = positions.astype(jnp.float32)[:, None] * freq[None, :]
    cosine = jnp.cos(angle)[:, None, :]
    sine = jnp.sin(angle)[:, None, :]
    first = field[..., :half]
    second = field[..., half:]
    return jnp.concatenate(
        [first * cosine - second * sine, second * cosine + first * sine], axis=-1
    )


def on_device(
    inputs,
    norm_gain,
    wq_packed,
    wq_scales,
    key_weight,
    value_weight,
    wo_weight,
    key_cache,
    value_cache,
    lengths,
):
    high = lax.Precision.HIGHEST
    w_query = unpack_weights(wq_packed, wq_scales, 4, 2)
    w_output = wo_weight.astype(jnp.float32)
    w_joined = jnp.concatenate(
        [w_query, key_weight.astype(jnp.float32), value_weight.astype(jnp.float32)], axis=1
    )
    seq_local = lengths.shape[0]
    slots = key_cache.shape[1]
    kv_local = key_weight.shape[1] // HEAD
    q_local = w_query.shape[1] // HEAD
    repeat = q_local // kv_local
    cols_local = inputs.shape[2]
    keys_all = key_cache
    values_all = value_cache
    slot_ids = jnp.arange(slots, dtype=jnp.int32)
    results = []
    for step in range(STEPS):
        rows = inputs[step].astype(jnp.float32)
        width_count = lax.axis_size("width")
        batch_count = lax.axis_size("batch")
        arranged = rows.reshape(width_count, batch_count, seq_local, cols_local)
        rows = lax.dynamic_index_in_dim(arranged, lax.axis_index("batch"), 1, keepdims=False)
        rows = rows.reshape(width_count * seq_local, cols_local)
        squares = jnp.sum(rows * rows, axis=1)
        total = lax.psum(squares, "width")
        scale = lax.rsqrt(total / D + 1e-05)
        normed = rows * scale[:, None] * norm_gain[None, :]
        partial_value = jnp.dot(
            normed, w_joined, precision=high, preferred_element_type=jnp.float32
        )
        terms = (partial_value,)
        summed = (lax.psum_scatter(terms[0], "width", scatter_dimension=0, tiled=True),)
        projected = summed[0]
        positions = lengths + step
        q_cols = q_local * HEAD
        kv_cols = kv_local * HEAD
        queries = rotate_heads(
            projected[:, :q_cols].reshape(seq_local, q_local, HEAD), positions
        ).astype(jnp.bfloat16)
        keys_new = rotate_heads(
            projected[:, q_cols : q_cols + kv_cols].reshape(seq_local, kv_local, HEAD), positions
        )
        keys_new = keys_new.reshape(seq_local, kv_cols).astype(jnp.bfloat16)
        values_new = projected[:, q_cols + kv_cols :].astype(jnp.bfloat16)
        written = slot_ids[None, :, None] == positions[:, None, None]
        keys_all = jnp.where(written, keys_new[:, None, :], keys_all)
        values_all = jnp.where(written, values_new[:, None, :], values_all)
        query_heads = queries.reshape(seq_local, kv_local, repeat, HEAD)
        key_heads = keys_all.reshape(seq_local, slots, kv_local, HEAD)
        value_heads = values_all.reshape(seq_local, slots, kv_local, HEAD)
        scores = jnp.einsum(
            "bgrd,bsgd->bgrs", query_heads, key_heads, preferred_element_type=jnp.float32
        ) * HEAD ** (-0.5)
        valid = slot_ids[None, None, None, :] <= positions[:, None, None, None]
        scores = jnp.where(valid, scores, -1e30)
        peak = jnp.max(scores, axis=-1, keepdims=True)
        weights = jnp.exp(scores - peak)
        total_weight = jnp.sum(weights, axis=-1, keepdims=True)
        probs = (weights / total_weight).astype(jnp.bfloat16)
        mixed = jnp.einsum(
            "bgrs,bsgd->bgrd", probs, value_heads, preferred_element_type=jnp.float32
        )
        mixed = mixed.reshape(seq_local, q_cols).astype(jnp.bfloat16)
        out_terms = jnp.dot(
            lax.all_gather(mixed, ("width", "batch"), axis=0, tiled=True).astype(jnp.float32),
            w_output,
            precision=high,
            preferred_element_type=jnp.float32,
        )
        head_sums = lax.psum_scatter(out_terms, "hidden", scatter_dimension=0, tiled=True)
        share = head_sums.shape[0] // lax.axis_size("batch")
        attended = lax.dynamic_slice_in_dim(head_sums, lax.axis_index("batch") * share, share, 0)
        results.append(attended.astype(jnp.bfloat16))
    return jnp.stack(results)


def solution(mesh):
    in_specs = (
        P(None, "groups", "width"),
        P("width"),
        P("width", "hidden"),
        P("width", "hidden"),
        P("width", "hidden"),
        P("width", "hidden"),
        P("hidden", "width"),
        P(("groups", "width", "batch"), None, "hidden"),
        P(("groups", "width", "batch"), None, "hidden"),
        P(("groups", "width", "batch")),
    )
    out_specs = P(None, ("groups", "hidden", "batch"), "width")
    return jax.shard_map(
        on_device, mesh=mesh, in_specs=in_specs, out_specs=out_specs, check_vma=False
    )
```

profile of v0, /device:TPU:0, one launch (start us, length us, event | category | flops | bytes accessed | tf_op | source)
XLA Modules:
  0.0 575.9 jit_solution(8795833345152713637)
XLA Ops:
  6.5 1.0 slice_convert_fusion.1
  8.2 13.4 %all-reduce.2 = (f32[8]{0:T(128)S(1)}, f32[8]{0:T(128)S(1)}) all-reduce(f32[8]{0:T(128)S(1)} %reduce_sum.44, f32[8]{0:T(128)S(1)} %reduce_sum.41), channel_id=1, replica_groups=mesh['groups'=2,'width'=4,'hidden'=2,'batch'=2] {'width'}, use_global_device_ids=true, to_apply=%region_7.8 | all-reduce | flops 16 | bytes 128 | tf_op jit(solution)/shard_map/psum | solution.py:70
  22.2 0.7 reshape.281
  22.9 31.1 %copy.23 = s32[4096,2048]{0,1:T(8,128)} copy(s32[4096,2048]{1,0:T(8,128)} %param.12) | data formatting | bytes 67108864 | tf_op args[2]
  54.0 39.8 %shift_right_arithmetic.21 = s32[4096,2048,2]{0,2,1:T(2,128)} broadcast(s32[4096,2048]{0,1:T(8,128)} %copy.23), dimensions={0,1} | broadcast | bytes 100663296 | tf_op jit(solution)/shard_map/shift_right_arithmetic | solution.py:13
  93.8 78.3 %shift_right_arithmetic.22 = s32[4096,4096]{0,1:T(8,128)} reshape(s32[4096,2048,2]{0,2,1:T(2,128)} %shift_right_arithmetic.21) | data formatting | bytes 134217728 | tf_op jit(solution)/shard_map/shift_right_arithmetic | solution.py:13
  173.3 4.1 copy.25
  177.4 4.0 convert_element_type.85
  181.4 4.1 copy.26
  185.5 4.1 convert_element_type.86
  189.7 41.1 %mul.120 = f32[32,128,4096]{1,0,2:T(8,128)} broadcast(f32[32,4096]{0,1:T(8,128)S(1)} %copy.24), dimensions={0,2} | broadcast | bytes 67633152 | tf_op jit(solution)/shard_map/mul | solution.py:17
  230.7 79.0 %bitcast_multiply_fusion = f32[4096,4096]{0,1:T(8,128)} fusion(f32[512,8,32,128]{3,2,1,0:T(8,128)} %bitcast.17, s32[4096,4096]{0,1:T(8,128)} %shift_right_arithmetic.22, s32[4096]{0:T(1024)S(1)} %shift_right_arithmetic.24), kind=kLoop, calls=%fused_computation.3 | loop fusion | flops 83886080 | bytes 201342976 | tf_op jit(solution)/shard_map/mul | solution.py:17
  309.8 78.8 %fusion.3 = f32[8,4608]{1,0:T(8,128)} fusion(f32[4096,256]{0,1:T(8,128)} %convert_element_type.86, f32[4096,256]{0,1:T(8,128)} %convert_element_type.85, f32[4096,4096]{0,1:T(8,128)} %bitcast_multiply_fusion, f32[8,4096]{1,0:T(8,128)S(1)} %copy-done.5, f32[4096]{0:T(1024)S(1)} %copy-done.7, f32[8]{0:T(128)S(1)} %copy-done.9), kind=kOutput, calls=%fused_computation.5 | convolution fusion | flops 1849753600 | bytes 75792416 | tf_op jit(solution)/shard_map/dot_general | solution.py:73
  388.6 65.2 %fusion.2 = f32[8,4608]{1,0:T(8,128)} fusion(f32[4096,256]{0,1:T(8,128)S(1)} %copy-done.1, f32[4096,256]{0,1:T(8,128)S(1)} %copy-done, f32[4096,4096]{0,1:T(8,128)} %bitcast_multiply_fusion, f32[8,4096]{1,0:T(8,128)S(1)} %reshape.286, f32[8]{0:T(128)S(1)} %add_rsqrt_fusion, f32[4096]{0:T(1024)S(1)} %copy-done.7), kind=kOutput, calls=%fused_computation.4 | convolution fusion | flops 1849753600 | bytes 75792416 | tf_op jit(solution)/shard_map/dot_general | solution.py:73
  455.4 32.9 %all-reduce.6.cloned.1.call-done = (f32[8,4608]{1,0:T(8,128)}, f32[8,4608]{1,0:T(8,128)}) async-done(((f32[8,4608]{1,0:T(8,128)}, f32[8,4608]{1,0:T(8,128)}), (f32[8,4608]{1,0:T(8,128)}, f32[8,4608]{1,0:T(8,128)})) %all-reduce.6.cloned.1.call-update) | async-done | bytes 294928
  488.3 0.8 dynamic-slice.8
  489.0 0.8 dynamic-slice.5
  489.8 0.8 dynamic-slice.14
  490.6 0.8 dynamic-slice.15
  491.4 0.9 dynamic-slice_bitcast_fusion.1
  492.3 0.9 dynamic-slice_bitcast_fusion
  493.7 2.4 fusion.19
  496.7 1.6 convolution_convert_fusion.1
  498.3 14.0 %all-gather = bf16[8,2,4096]{2,1,0:T(2,128)(2,1)S(1)} all-gather(bf16[1,2,4096]{2,1,0:T(2,128)(2,1)S(1)} %reshape.293), channel_id=1, replica_groups=mesh['groups'=2,'width'=4,'hidden'=2,'batch'=2] {'width','batch'}, dimensions={0}, use_global_device_ids=true | all-gather | bytes 147456 | tf_op jit(solution)/shard_map/all_gather | solution.py:110
  512.3 13.8 %fusion.48 = f32[16,4096]{1,0:T(8,128)} fusion(bf16[16,4096]{1,0:T(8,128)(2,1)S(1)} %reshape.294, bf16[4096,4096]{1,0:T(8,128)(2,1)} %param.16), kind=kOutput, calls=%fused_computation.100 | convolution fusion | flops 536870912 | bytes 33947648 | tf_op jit(solution)/shard_map/dot_general | solution.py:109
  526.9 1.6 convolution_convert_fusion
  528.5 14.0 %all-gather.1 = bf16[8,2,4096]{2,1,0:T(2,128)(2,1)S(1)} all-gather(bf16[1,2,4096]{2,1,0:T(2,128)(2,1)S(1)} %reshape.295), channel_id=1, replica_groups=mesh['groups'=2,'width'=4,'hidden'=2,'batch'=2] {'width','batch'}, dimensions={0}, use_global_device_ids=true | all-gather | bytes 147456 | tf_op jit(solution)/shard_map/all_gather | solution.py:110
  542.5 13.5 %fusion.49 = f32[16,4096]{1,0:T(8,128)} fusion(bf16[16,4096]{1,0:T(8,128)(2,1)S(1)} %reshape.296, bf16[4096,4096]{1,0:T(8,128)(2,1)} %param.16), kind=kOutput, calls=%fused_computation.101 | convolution fusion | flops 536870912 | bytes 33947648 | tf_op jit(solution)/shard_map/dot_general | solution.py:109
  556.1 0.9 fusion.30
  557.1 10.7 %reduce-scatter.5.cloned.1.call-done = f32[8,4096]{1,0:T(8,128)} async-done(((f32[16,4096]{1,0:T(8,128)}), f32[8,4096]{1,0:T(8,128)}) %reduce-scatter.5.cloned.1.call-update) | async-done | bytes 131088 | tf_op jit(solution)/shard_map/reduce_scatter | solution.py:115
  567.7 0.9 fusion.31
  568.7 0.7 pad_maximum_fusion.3
  (64 shorter events, 5.4 us)
Async XLA Ops:
  6.5 481.7 %all-reduce.6.cloned.1.call-start = ((), (), s32[]{:S(2)}) async-start(), calls=%async_computation.4 | async-start | bytes 589824
  93.8 78.3 %copy-start.4 = (f32[32,4096]{1,0:T(8,128)S(1)}, f32[32,4096]{1,0:T(8,128)}, u32[]{:S(2)}) copy-start(f32[32,4096]{1,0:T(8,128)} %param.13) | copy-start | bytes 1572868
  230.7 79.0 %copy-start.5 = (f32[8,4096]{1,0:T(8,128)S(1)}, f32[8,4096]{1,0:T(8,128)}, u32[]{:S(2)}) copy-start(f32[8,4096]{1,0:T(8,128)} %reshape.281) | copy-start | bytes 393220
  230.7 79.0 %copy-start.7 = (f32[4096]{0:T(1024)S(1)}, f32[4096]{0:T(1024)}, u32[]{:S(2)}) copy-start(f32[4096]{0:T(1024)} %param.11) | copy-start | bytes 49156
  230.7 79.0 %copy-start.9 = (f32[8]{0:T(128)S(1)}, f32[8]{0:T(128)}, u32[]{:S(2)}) copy-start(f32[8]{0:T(128)} %add_rsqrt_fusion.1) | copy-start | bytes 100
  309.8 78.8 %copy-start = (f32[4096,256]{0,1:T(8,128)S(1)}, f32[4096,256]{0,1:T(8,128)}, u32[]{:S(2)}) copy-start(f32[4096,256]{0,1:T(8,128)} %convert_element_type.85) | copy-start | bytes 12582916
  309.8 78.8 %copy-start.1 = (f32[4096,256]{0,1:T(8,128)S(1)}, f32[4096,256]{0,1:T(8,128)}, u32[]{:S(2)}) copy-start(f32[4096,256]{0,1:T(8,128)} %convert_element_type.86) | copy-start | bytes 12582916
  388.5 65.4 %copy-start.6 = (s32[2]{0:T(128)S(1)}, s32[2]{0:T(128)}, u32[]{:S(2)}) copy-start(s32[2]{0:T(128)} %param.19) | copy-start | bytes 28
  388.5 65.5 %copy-start.8 = (u32[32]{0:T(128)S(1)}, u32[32]{0:T(128)}, u32[]{:S(2)}) copy-start(u32[32]{0:T(128)} %constant.51) | copy-start | bytes 388
  388.5 105.1 %copy-start.2 = (bf16[2,1024,256]{2,1,0:T(8,128)(2,1)S(1)}, bf16[2,1024,256]{2,1,0:T(8,128)(2,1)}, u32[]{:S(2)}) copy-start(bf16[2,1024,256]{2,1,0:T(8,128)(2,1)} %param.18) | copy-start | bytes 3145732
  388.6 105.1 %copy-start.3 = (bf16[2,1024,256]{2,1,0:T(8,128)(2,1)S(1)}, bf16[2,1024,256]{2,1,0:T(8,128)(2,1)}, u32[]{:S(2)}) copy-start(bf16[2,1024,256]{2,1,0:T(8,128)(2,1)} %param.17) | copy-start | bytes 3145732
  453.8 102.3 %reduce-scatter.3.cloned.1.call-start = ((), (), s32[]{:S(2)}) async-start(), calls=%async_computation.2 | async-start | bytes 393216 | tf_op jit(solution)/shard_map/reduce_scatter | solution.py:115
  526.1 41.6 %reduce-scatter.5.cloned.1.call-start = ((), (), s32[]{:S(2)}) async-start(), calls=%async_computation.3 | async-start | bytes 393216 | tf_op jit(solution)/shard_map/reduce_scatter | solution.py:115
Sparse Core Ops, SparseCore 0:
  454.0 34.2 all-reduce.5
  526.3 11.4 reduce-scatter.2
  556.2 11.4 reduce-scatter.4
where the time goes:
time: 579 us; the launch traced here: 576 us
  local copies, waits for them, and re-layouts  209 us (36%)
  matrix products  175 us (30%)
  other arithmetic  93 us (16%)
  waiting for transfers between devices  43.6 us (8%)
  blocking collectives  41.4 us (7%)
  between operations  14 us (2%)
    dot_general x2, matrix products, on_device(): jnp.dot(normed, w_joined, precision=high, preferred_element_type=jnp.floa...  144 us
    shift_right_arithmetic x4, local copies, waits for them, and re-layouts, unpack_weights(): codes = packed[:, :, None] >> shifts & (1 << bits) - 1  119 us
    mul x1, other arithmetic, unpack_weights(): values.reshape(scales.shape[0], group_rows, values.shape[1])  79 us
    unnamed x35, local copies, waits for them, and re-layouts  42.6 us
    mul x1, local copies, waits for them, and re-layouts, unpack_weights(): values.reshape(scales.shape[0], group_rows, values.shape[1])  41.1 us
    unnamed x4, waiting for transfers between devices  32.9 us
    all_gather x2, blocking collectives, on_device(): lax.all_gather(mixed, ('width', 'batch'), axis=0, tiled=True)  28 us
    dot_general x2, matrix products, on_device(): jnp.dot(lax.all_gather(mixed, ('width', 'batch'), axis=0, tiled=True).ast...  27.3 us
  transfers between devices with their start and end apart: 3, of which 2 were waited for; matrix products, arithmetic and copies ran while one was open for 3% of the time, Pallas kernels for 0%

commit v1 on v0

--- a/solution.py
+++ b/solution.py
@@ -1,11 +1,17 @@
 import jax
 import jax.numpy as jnp
 from jax import lax
+from jax.experimental import pallas as pl
+from jax.experimental.pallas import tpu as pltpu
 from jax.sharding import PartitionSpec as P
 
 D = 16384
 HEAD = 128
 STEPS = 2
+EPS = 1e-05
+BF16 = jnp.bfloat16
+F32 = jnp.float32
+VMEM_LIMIT = 60 * 1024 * 1024
 
 
 def unpack_weights(packed, scales, bits, per_word):
@@ -31,7 +37,7 @@
     )
 
 
-def on_device(
+def general(
     inputs,
     norm_gain,
     wq_packed,
@@ -68,14 +74,12 @@
         rows = rows.reshape(width_count * seq_local, cols_local)
         squares = jnp.sum(rows * rows, axis=1)
         total = lax.psum(squares, "width")
-        scale = lax.rsqrt(total / D + 1e-05)
+        scale = lax.rsqrt(total / D + EPS)
         normed = rows * scale[:, None] * norm_gain[None, :]
         partial_value = jnp.dot(
             normed, w_joined, precision=high, preferred_element_type=jnp.float32
         )
-        terms = (partial_value,)
-        summed = (lax.psum_scatter(terms[0], "width", scatter_dimension=0, tiled=True),)
-        projected = summed[0]
+        projected = lax.psum_scatter(partial_value, "width", scatter_dimension=0, tiled=True)
         positions = lengths + step
         q_cols = q_local * HEAD
         kv_cols = kv_local * HEAD
@@ -119,7 +123,361 @@
     return jnp.stack(results)
 
 
+def split3(value):
+    hi = value.astype(BF16)
+    rest = value - hi.astype(F32)
+    mid = rest.astype(BF16)
+    low = (rest - mid.astype(F32)).astype(BF16)
+    return hi, mid, low
+
+
+def project_kernel(
+    x_ref, gain_ref, wq_ref, scale_ref, kw_ref, vw_ref, own_ref, *rest
+):
+    nw = len(rest) - 5
+    sends = rest[: nw - 1]
+    se_ref, so_ref, acc_ref, ss_ref, kv_ref, arr_ref = rest[nw - 1 :]
+    k = pl.program_id(0)
+    steps, seqs, depth = x_ref.shape
+    rows = steps * seqs
+    words = wq_ref.shape[1]
+    groups = se_ref.shape[0]
+    per_block = groups // pl.num_programs(0)
+    group = depth // per_block
+
+    @pl.when(k == 0)
+    def _():
+        acc_ref[...] = jnp.zeros_like(acc_ref)
+        ss_ref[...] = jnp.zeros_like(ss_ref)
+        kv_ref[...] = jnp.zeros_like(kv_ref)
+        row = lax.broadcasted_iota(jnp.int32, (256, 256), 0)
+        col = lax.broadcasted_iota(jnp.int32, (256, 256), 1)
+        pick = jnp.where(row == 2 * (col & 127) + (col >> 7), 1.0, 0.0).astype(BF16)
+        for c in range(words // 128):
+            terms = split3(scale_ref[:, c * 256 : (c + 1) * 256])
+            parts = [jnp.dot(term, pick, preferred_element_type=F32) for term in terms]
+            both = parts[0] + (parts[1] + parts[2])
+            se_ref[:, c * 128 : (c + 1) * 128] = both[:, :128]
+            so_ref[:, c * 128 : (c + 1) * 128] = both[:, 128:]
+
+    x = x_ref[...].astype(F32).reshape(rows, depth)
+    y = x * gain_ref[...]
+    hi = y.astype(BF16)
+    low = (y - hi.astype(F32)).astype(BF16)
+    lhs = jnp.concatenate([hi, low], axis=0)
+    exact = hi.astype(F32) + low.astype(F32)
+    sums = [
+        8.0 * jnp.sum(exact[:, g * group : (g + 1) * group], axis=1, keepdims=True)
+        for g in range(per_block)
+    ]
+    squares = x * x
+    total = squares[:, :128]
+    for c in range(1, depth // 128):
+        total = total + squares[:, c * 128 : (c + 1) * 128]
+    ss_ref[...] += total
+
+    chunk = 256
+    for c in range(words // chunk):
+        cols = slice(c * chunk, (c + 1) * chunk)
+        even = jnp.zeros((rows, chunk), F32)
+        odd = jnp.zeros((rows, chunk), F32)
+        for g in range(per_block):
+            span = slice(g * group, (g + 1) * group)
+            word = wq_ref[span, cols]
+            both = word.astype(F32).astype(BF16)
+            upper = (word >> 4).astype(F32).astype(BF16)
+            left = lhs[:, span]
+            p = jnp.dot(left, both, preferred_element_type=F32)
+            u = jnp.dot(left, upper, preferred_element_type=F32)
+            p = p[:rows] + p[rows:]
+            u = u[:rows] + u[rows:]
+            at = pl.ds(k * per_block + g, 1)
+            even = even + (p - 16.0 * u - sums[g]) * se_ref[at, cols]
+            odd = odd + (u - sums[g]) * so_ref[at, cols]
+        acc_ref[:, cols] += even
+        acc_ref[:, words + c * chunk : words + (c + 1) * chunk] += odd
+    key = jnp.dot(lhs, kw_ref[...], preferred_element_type=F32)
+    val = jnp.dot(lhs, vw_ref[...], preferred_element_type=F32)
+    kv_ref[:, :HEAD] += key[:rows] + key[rows:]
+    kv_ref[:, HEAD:] += val[:rows] + val[rows:]
+
+    @pl.when(k == pl.num_programs(0) - 1)
+    def _():
+        each = seqs // nw
+        lane = lax.broadcasted_iota(jnp.int32, (rows, 128), 1)
+        a, m, l = split3(jnp.sum(ss_ref[...], axis=1, keepdims=True))
+        a, m, l = a.astype(F32), m.astype(F32), l.astype(F32)
+        norm = jnp.where(lane == 0, a, jnp.where(lane == 1, m, jnp.where(lane == 2, l, 0.0)))
+        for v in range(nw):
+            for t in range(steps):
+                src = slice(t * seqs + v * each, t * seqs + (v + 1) * each)
+                dst = slice(t * each, (t + 1) * each)
+                arr_ref[v, dst, : 2 * words] = acc_ref[src, :]
+                arr_ref[v, dst, 2 * words : 2 * words + 2 * HEAD] = kv_ref[src, :]
+                arr_ref[v, dst, 2 * words + 2 * HEAD :] = norm[src]
+        me = lax.axis_index("width")
+        own_ref[...] = arr_ref[me]
+        for s in range(1, nw):
+            sends[s - 1][...] = arr_ref[lax.rem(me + s, nw)].astype(BF16)
+
+
+def project(inputs, norm_gain, wq_packed, wq_scales, key_weight, value_weight, nw, nb):
+    steps, seqs, depth = inputs.shape
+    rows = steps * seqs
+    words = wq_packed.shape[1] // nb
+    groups = wq_scales.shape[0]
+    block = 512
+    cols = 2 * words + 3 * HEAD
+    out_rows = rows // nw
+    mine = lambda k: (k, lax.axis_index("batch"))
+    return pl.pallas_call(
+        project_kernel,
+        grid=(depth // block,),
+        in_specs=[
+            pl.BlockSpec((steps, seqs, block), lambda k: (0, 0, k)),
+            pl.BlockSpec((1, block), lambda k: (0, k)),
+            pl.BlockSpec((block, words), mine),
+            pl.BlockSpec((groups, 2 * words), lambda k: (0, lax.axis_index("batch"))),
+            pl.BlockSpec((block, HEAD), mine),
+            pl.BlockSpec((block, HEAD), mine),
+        ],
+        out_specs=[pl.BlockSpec((out_rows, cols), lambda k: (0, 0))] * nw,
+        out_shape=[jax.ShapeDtypeStruct((out_rows, cols), F32)]
+        + [jax.ShapeDtypeStruct((out_rows, cols), BF16)] * (nw - 1),
+        scratch_shapes=[
+            pltpu.VMEM((groups, words), F32),
+            pltpu.VMEM((groups, words), F32),
+            pltpu.VMEM((rows, 2 * words), F32),
+            pltpu.VMEM((rows, 128), F32),
+            pltpu.VMEM((rows, 2 * HEAD), F32),
+            pltpu.VMEM((nw, out_rows, cols), F32),
+        ],
+        compiler_params=pltpu.CompilerParams(vmem_limit_bytes=VMEM_LIMIT),
+        name="project",
+    )(inputs, norm_gain.reshape(1, -1), wq_packed, wq_scales, key_weight, value_weight)
+
+
+def attend_kernel(heads, nw, len_ref, own_ref, *rest):
+    parts = rest[: nw - 1]
+    (table_ref, k_own, k_mate, v_own, v_mate, out_ref, k_buf, v_buf, q_ref, m_ref, sems) = rest[nw - 1 :]
+    each, slots, _ = k_own.shape
+    b = lax.axis_index("batch")
+    column = pl.ds(pl.multiple_of(b * HEAD, HEAD), HEAD)
+    copies = []
+    for n, (src, buf, place) in enumerate(
+        ((k_own, k_buf, b), (k_mate, k_buf, 1 - b), (v_own, v_buf, b), (v_mate, v_buf, 1 - b))
+    ):
+        copy = pltpu.make_async_copy(
+            src.at[:, :, column], buf.at[pl.ds(place * each, each)], sems.at[n]
+        )
+        copy.start()
+        copies.append(copy)
+
+    rows = own_ref.shape[0]
+    seqs = rows // STEPS
+    half = heads * HEAD // 2
+    total = own_ref[...]
+    for part in parts:
+        total = total + part[...].astype(F32)
+    squares = jnp.sum(total[:, 2 * half + 2 * HEAD :], axis=1, keepdims=True)
+    total = total * lax.rsqrt(squares / D + EPS)
+
+    lane = lax.broadcasted_iota(jnp.int32, (rows, HEAD), 1)
+    left = lane < HEAD // 2
+    tiles = []
+    for m in range(heads // 2):
+        e = total[:, m * HEAD : (m + 1) * HEAD]
+        o = total[:, half + m * HEAD : half + (m + 1) * HEAD]
+        tiles.append(jnp.where(left, e, pltpu.roll(o, HEAD // 2, 1)))
+        tiles.append(jnp.where(left, pltpu.roll(e, HEAD // 2, 1), o))
+    cos_q, sin_q = table_ref[0], table_ref[1]
+    cos_k, sin_k = table_ref[2], table_ref[3]
+    near = (lane & (HEAD // 2 - 1)) < HEAD // 4
+    turned = []
+    for q in tiles:
+        other = jnp.where(near, pltpu.roll(q, HEAD - HEAD // 4, 1), pltpu.roll(q, HEAD // 4, 1))
+        turned.append(q * cos_q + other * sin_q)
+    q_all = jnp.concatenate(turned, axis=0).astype(BF16)
+    row = lax.broadcasted_iota(jnp.int32, (HEAD, HEAD), 0)
+    col = lax.broadcasted_iota(jnp.int32, (HEAD, HEAD), 1)
+    order = jnp.where(col == 2 * (row & (HEAD // 2 - 1)) + row // (HEAD // 2), 1.0, 0.0).astype(BF16)
+    q_ref[...] = jnp.dot(q_all, order, preferred_element_type=F32)
+    k_new = total[:, 2 * half : 2 * half + HEAD]
+    k_new = (k_new * cos_k + pltpu.roll(k_new, HEAD // 2, 1) * sin_k).astype(BF16).astype(F32)
+    v_new = total[:, 2 * half + HEAD : 2 * half + 2 * HEAD].astype(BF16).astype(F32)
+
+    for copy in copies:
+        copy.wait()
+
+    slot = lax.broadcasted_iota(jnp.int32, (STEPS * heads, slots), 1)
+    later = lax.broadcasted_iota(jnp.int32, (STEPS * heads, 1), 0) >= heads
+    for j in range(seqs):
+        q = jnp.concatenate(
+            [q_ref[pl.ds(t * seqs + j, heads, stride=rows), :] for t in range(STEPS)], axis=0
+        )
+        scores = lax.dot_general(
+            q.astype(BF16), k_buf[j], (((1,), (1,)), ((), ())), preferred_element_type=F32
+        ) * HEAD ** (-0.5)
+        scores = jnp.where(slot < len_ref[j], scores, -1e30)
+        first = jnp.sum(q * k_new[j : j + 1], axis=1, keepdims=True) * HEAD ** (-0.5)
+        second = jnp.sum(q * k_new[seqs + j : seqs + j + 1], axis=1, keepdims=True) * HEAD ** (-0.5)
+        second = jnp.where(later, second, -1e30)
+        peak = jnp.maximum(jnp.max(scores, axis=1, keepdims=True), jnp.maximum(first, second))
+        weights = jnp.exp(scores - peak)
+        first = jnp.exp(first - peak)
+        second = jnp.exp(second - peak)
+        inverse = 1.0 / (jnp.sum(weights, axis=1, keepdims=True) + first + second)
+        probs = (weights * inverse).astype(BF16)
+        mixed = jnp.dot(probs, v_buf[j], preferred_element_type=F32)
+        mixed = mixed + (first * inverse).astype(BF16).astype(F32) * v_new[j : j + 1]
+        mixed = mixed + (second * inverse).astype(BF16).astype(F32) * v_new[seqs + j : seqs + j + 1]
+        for t in range(STEPS):
+            m_ref[pl.ds(t * seqs + j, heads, stride=rows), :] = mixed[t * heads : (t + 1) * heads]
+    for n in range(heads):
+        out_ref[:, n * HEAD : (n + 1) * HEAD] = m_ref[n * rows : (n + 1) * rows, :].astype(BF16)
+
+
+def attend(own, parts, table, lengths, k_own, k_mate, v_own, v_mate, heads):
+    rows = own.shape[0]
+    each, slots, _ = k_own.shape
+    nw = len(parts) + 1
+    vmem = pl.BlockSpec(memory_space=pltpu.VMEM)
+    hbm = pl.BlockSpec(memory_space=pl.ANY)
+    body = lambda *refs: attend_kernel(heads, nw, *refs)
+    return pl.pallas_call(
+        body,
+        in_specs=[pl.BlockSpec(memory_space=pltpu.SMEM)] + [vmem] * (nw + 1) + [hbm] * 4,
+        out_specs=vmem,
+        out_shape=jax.ShapeDtypeStruct((rows, heads * HEAD), BF16),
+        scratch_shapes=[
+            pltpu.VMEM((2 * each, slots, HEAD), BF16),
+            pltpu.VMEM((2 * each, slots, HEAD), BF16),
+            pltpu.VMEM((heads * rows, HEAD), F32),
+            pltpu.VMEM((heads * rows, HEAD), F32),
+            pltpu.SemaphoreType.DMA((4,)),
+        ],
+        compiler_params=pltpu.CompilerParams(vmem_limit_bytes=VMEM_LIMIT),
+        name="attend",
+    )(lengths, own, *parts, table, k_own, k_mate, v_own, v_mate)
+
+
+def output_kernel(nw, *refs):
+    pieces = refs[:nw]
+    wo_ref = refs[nw]
+    outs = refs[nw + 1 : 2 * nw + 1]
+    lhs_ref, acc_ref = refs[2 * nw + 1 :]
+    rows, depth = pieces[0].shape
+
+    @pl.when(pl.program_id(0) == 0)
+    def _():
+        me = lax.axis_index("width")
+        for s in range(nw):
+            lhs_ref[lax.rem(me + nw - s, nw)] = pieces[s][...].astype(F32)
+
+    lhs = lhs_ref[...].reshape(nw * rows, depth).astype(BF16)
+    acc = jnp.dot(lhs, wo_ref[...], preferred_element_type=F32)
+    acc_ref[...] = acc.reshape(acc_ref.shape)
+    me = lax.axis_index("hidden") * lax.axis_size("batch") + lax.axis_index("batch")
+    outs[0][...] = acc_ref[me]
+    for s in range(1, nw):
+        outs[s][...] = acc_ref[me ^ s].astype(BF16)
+
+
+def output(pieces, wo_weight):
+    nw = len(pieces)
+    rows, depth = pieces[0].shape
+    cols = wo_weight.shape[1]
+    block = 512
+    body = lambda *refs: output_kernel(nw, *refs)
+    return pl.pallas_call(
+        body,
+        grid=(cols // block,),
+        in_specs=[pl.BlockSpec((rows, depth), lambda n: (0, 0))] * nw
+        + [pl.BlockSpec((depth, block), lambda n: (lax.axis_index("batch"), n))],
+        out_specs=[pl.BlockSpec((rows, block), lambda n: (0, n))] * nw,
+        out_shape=[jax.ShapeDtypeStruct((rows, cols), F32)]
+        + [jax.ShapeDtypeStruct((rows, cols), BF16)] * (nw - 1),
+        scratch_shapes=[
+            pltpu.VMEM((nw, rows, depth), F32),
+            pltpu.VMEM((nw, rows, block), F32),
+        ],
+        compiler_params=pltpu.CompilerParams(vmem_limit_bytes=VMEM_LIMIT),
+        name="output",
+    )(*pieces, wo_weight)
+
+
+def rotary_tables(positions):
+    lane = jnp.arange(HEAD, dtype=jnp.int32)
+    parity = 2 * (lane % (HEAD // 2)) + lane // (HEAD // 2)
+    out = []
+    for dim in (parity, lane):
+        pair = (dim % (HEAD // 2)).astype(F32)
+        freq = 500000.0 ** (-2.0 * pair / HEAD)
+        angle = positions.astype(F32)[:, None] * freq[None, :]
+        sign = jnp.where(dim < HEAD // 2, -1.0, 1.0)[None, :]
+        out += [jnp.cos(angle), jnp.sin(angle) * sign]
+    return jnp.stack(out)
+
+
+def split_heads(
+    inputs,
+    norm_gain,
+    wq_packed,
+    wq_scales,
+    key_weight,
+    value_weight,
+    wo_weight,
+    key_cache,
+    value_cache,
+    lengths,
+):
+    nw, nh, nb = lax.axis_size("width"), lax.axis_size("hidden"), lax.axis_size("batch")
+    swap = [(0, 1), (1, 0)]
+    k_mate = lax.ppermute(key_cache, "batch", swap)
+    v_mate = lax.ppermute(value_cache, "batch", swap)
+    len_mate = lax.ppermute(lengths, "batch", swap)
+    first = lax.axis_index("batch") == 0
+    len_all = jnp.where(
+        first, jnp.concatenate([lengths, len_mate]), jnp.concatenate([len_mate, lengths])
+    )
+    positions = jnp.concatenate([len_all + step for step in range(STEPS)])
+    table = rotary_tables(positions)
+
+    own, *sends = project(
+        inputs, norm_gain, wq_packed, wq_scales, key_weight, value_weight, nw, nb
+    )
+    parts = [
+        lax.ppermute(piece, "width", [(i, (i + s) % nw) for i in range(nw)])
+        for s, piece in enumerate(sends, 1)
+    ]
+    heads = 2 * wq_packed.shape[1] // nb // HEAD
+    mixed = attend(own, parts, table, len_all, key_cache, k_mate, value_cache, v_mate, heads)
+    pieces = [mixed] + [
+        lax.ppermute(mixed, "width", [(i, (i + s) % nw) for i in range(nw)]) for s in range(1, nw)
+    ]
+    head_own, *head_sends = output(pieces, wo_weight)
+    sums = head_own
+    for s, piece in enumerate(head_sends, 1):
+        got = lax.ppermute(piece, ("hidden", "batch"), [(i, i ^ s) for i in range(nh * nb)])
+        sums = sums + got.astype(F32)
+    return sums.reshape(STEPS, -1, sums.shape[1]).astype(BF16)
+
+
 def solution(mesh):
+    sizes = mesh.shape
+
+    def on_device(*args):
+        kv_local = args[4].shape[1] // HEAD
+        fits = (
+            sizes["batch"] == 2
+            and kv_local == 2
+            and sizes["width"] == sizes["hidden"] * sizes["batch"]
+            and args[0].shape[1] // sizes["width"] == 2 * args[9].shape[0]
+            and args[0].shape[2] % 512 == 0
+            and STEPS * args[0].shape[1] // sizes["width"] % 8 == 0
+        )
+        return split_heads(*args) if fits else general(*args)
+
     in_specs = (
         P(None, "groups", "width"),
         P("width"),

time: 579 us -> 57 us (0.10)
  local copies, waits for them, and re-layouts: 209 us -> 2.57 us
  matrix products: 175 us -> 0 us
  other arithmetic: 93 us -> 1.83 us
  blocking collectives: 41.4 us -> 0 us
  waiting for transfers between devices: 43.6 us -> 11.3 us
  Pallas kernels: 0 us -> 27.4 us
  between operations: 14 us -> 0.09 us
  starting transfers between devices: 0.09 us -> 13.4 us
    dot_general x8 -> x0, matrix products: 175 us -> none  [the longest x2 144 us: on_device(): jnp.dot(normed, w_joined, precision=high, preferred_element_type=jnp.floa...]
    shift_right_arithmetic x4 -> x0, local copies, waits for them, and re-layouts: 119 us -> none  [unpack_weights(): codes = packed[:, :, None] >> shifts & (1 << bits) - 1]
    mul x2 -> x0, other arithmetic: 79 us -> none  [the longest x1 79 us: unpack_weights(): values.reshape(scales.shape[0], group_rows, values.shape[1])]
    mul x1 -> x0, local copies, waits for them, and re-layouts: 41.1 us -> none  [unpack_weights(): values.reshape(scales.shape[0], group_rows, values.shape[1])]
    unnamed x35 -> x20, local copies, waits for them, and re-layouts: 42.6 us -> 1.91 us
    unnamed x4 -> x0, waiting for transfers between devices: 32.9 us -> none
    all_gather x2 -> x0, blocking collectives: 28 us -> none  [on_device(): lax.all_gather(mixed, ('width', 'batch'), axis=0, tiled=True)]
    pallas_call x0 -> x3, Pallas kernels: none -> 27.4 us  [the longest x1 12.3 us: project(): pl.pallas_call(project_kernel, grid=(depth // block,), in_specs=[pl.Block...]
  transfers between devices with their start and end apart: 3 -> 12, of which waited for: 2 -> 7; matrix products, arithmetic and copies ran while one was open for 3% -> 2% of each run, Pallas kernels for 0% -> 22%
where the time goes in v1:
time: 57 us; the launch traced here: 56.6 us
  Pallas kernels  27.4 us (48%)
  starting transfers between devices  13.4 us (24%)
  waiting for transfers between devices  11.3 us (20%)
  local copies, waits for them, and re-layouts  2.57 us (5%)
  other arithmetic  1.83 us (3%)
    pallas_call x1, Pallas kernels, project(): pl.pallas_call(project_kernel, grid=(depth // block,), in_specs=[pl.Block...  12.3 us
    pallas_call x1, Pallas kernels, output(): pl.pallas_call(body, grid=(cols // block,), in_specs=[pl.BlockSpec((rows,...  10.2 us
    ppermute x3, starting transfers between devices, split_heads(): lax.ppermute(piece, 'width', [(i, (i + s) % nw) for i in range(nw)])  6.66 us
    ppermute x3, waiting for transfers between devices, split_heads(): lax.ppermute(mixed, 'width', [(i, (i + s) % nw) for i in range(nw)])  5.28 us
    pallas_call x1, Pallas kernels, attend(): pl.pallas_call(body, in_specs=[pl.BlockSpec(memory_space=pltpu.SMEM)] + [...  4.93 us
    ppermute x3, waiting for transfers between devices, split_heads(): lax.ppermute(piece, ('hidden', 'batch'), [(i, i ^ s) for i in range(nh *...  4.04 us
    ppermute x3, starting transfers between devices, split_heads(): lax.ppermute(mixed, 'width', [(i, (i + s) % nw) for i in range(nw)])  3.84 us
    ppermute x3, waiting for transfers between devices, split_heads(): lax.ppermute(piece, 'width', [(i, (i + s) % nw) for i in range(nw)])  1.95 us
  transfers between devices with their start and end apart: 12, of which 7 were waited for; matrix products, arithmetic and copies ran while one was open for 2% of the time, Pallas kernels for 22%

profile of v1, /device:TPU:0, one launch (start us, length us, event | category | flops | bytes accessed | tf_op | source)
XLA Modules:
  0.0 56.6 jit_solution(8500449332467106429)
XLA Ops:
  0.0 0.5 collective-permute-start.4
  0.5 0.1 collective-permute-start.5
  0.5 0.4 collective-permute-start
  1.0 12.3 %project.1 = (f32[8,2432]{1,0:T(8,128)}, bf16[8,2432]{1,0:T(8,128)(2,1)}, bf16[8,2432]{1,0:T(8,128)(2,1)}, bf16[8,2432]{1,0:T(8,128)(2,1)}) custom-call(bf16[2,16,4096]{2,1,0:T(8,128)(2,1)} %x_ref.1, f32[1,4096]{1,0:T(1,128)} %bitcast.1, s32[4096,2048]{1,0:T(8,128)} %wq_ref.1, f32[32,4096]{1,0:T(8,128)} %scale_ref.1, bf16[4096,256]{1,0:T(8,128)(2,1)} %kw_ref.1, ...), custom_call_target="tpu_custom_call" | custom-call | tf_op jit(solution)/shard_map/project/pallas_call | solution.py:233
  13.3 2.7 %collective-permute-start.1 = (bf16[8,2432]{1,0:T(8,128)(2,1)}, bf16[8,2432]{1,0:T(8,128)(2,1)S(1)}, u32[]{:S(2)}, u32[]{:S(2)}) collective-permute-start(bf16[8,2432]{1,0:T(8,128)(2,1)} %get-tuple-element.14), channel_id=1, source_target_pairs={{0,4},{4,8},{8,12},{12,0},{1,5},{5,9},{9,13},{13,1},{2,6},{6,10},{... | collective-permute-start | bytes 116744 | tf_op jit(solution)/shard_map/ppermute | solution.py:450
  15.9 2.6 %collective-permute-start.2 = (bf16[8,2432]{1,0:T(8,128)(2,1)}, bf16[8,2432]{1,0:T(8,128)(2,1)S(1)}, u32[]{:S(2)}, u32[]{:S(2)}) collective-permute-start(bf16[8,2432]{1,0:T(8,128)(2,1)} %get-tuple-element.15), channel_id=1, source_target_pairs={{0,8},{4,12},{8,0},{12,4},{1,9},{5,13},{9,1},{13,5},{2,10},{6,14},... | collective-permute-start | bytes 116744 | tf_op jit(solution)/shard_map/ppermute | solution.py:450
  18.6 0.0 collective-permute-done
  18.6 1.4 %collective-permute-start.3 = (bf16[8,2432]{1,0:T(8,128)(2,1)}, bf16[8,2432]{1,0:T(8,128)(2,1)S(1)}, u32[]{:S(2)}, u32[]{:S(2)}) collective-permute-start(bf16[8,2432]{1,0:T(8,128)(2,1)} %get-tuple-element.16), channel_id=1, source_target_pairs={{0,12},{4,0},{8,4},{12,8},{1,13},{5,1},{9,5},{13,9},{2,14},{6,2},{... | collective-permute-start | bytes 116744 | tf_op jit(solution)/shard_map/ppermute | solution.py:450
  20.0 0.1 broadcast_add_fusion
  20.1 0.1 add_convert_fusion.1
  20.1 0.1 multiply_cosine_fusion.1
  20.3 0.6 %pad_maximum_fusion.refs_5_ = f32[4,8,128]{2,1,0:T(8,128)} fusion(f32[1,8,128]{2,1,0:T(8,128)S(1)} %get-tuple-element.27, f32[1,8,128]{2,1,0:T(8,128)S(1)} %get-tuple-element.28, f32[1,8,128]{2,1,0:T(8,128)S(1)} %get-tuple-element.24, f32[1,8,128]{2,1,0:T(8,128)S(1)} %get-tuple-element.23), kind=kLoop, calls=%fused_computation.1 | loop fusion | flops 12288 | bytes 32768 | tf_op jit(solution)/shard_map/stack | solution.py:419
  20.9 1.3 %collective-permute-done.2.refs_3_ = bf16[8,2432]{1,0:T(8,128)(2,1)S(1)} collective-permute-done((bf16[8,2432]{1,0:T(8,128)(2,1)}, bf16[8,2432]{1,0:T(8,128)(2,1)S(1)}, u32[]{:S(2)}, u32[]{:S(2)}) %collective-permute-start.2) | collective-permute-done | bytes 38944 | tf_op jit(solution)/shard_map/ppermute | solution.py:450
  22.2 0.6 %collective-permute-done.3.refs_4_ = bf16[8,2432]{1,0:T(8,128)(2,1)S(1)} collective-permute-done((bf16[8,2432]{1,0:T(8,128)(2,1)}, bf16[8,2432]{1,0:T(8,128)(2,1)S(1)}, u32[]{:S(2)}, u32[]{:S(2)}) %collective-permute-start.3) | collective-permute-done | bytes 38944 | tf_op jit(solution)/shard_map/ppermute | solution.py:450
  22.9 0.6 copy-done.4
  23.4 0.4 copy-done
  23.8 0.3 copy-done.1
  24.2 4.9 %attend.1.refs_0_ = bf16[8,2048]{1,0:T(8,128)(2,1)} custom-call(s32[4]{0:T(128)} %copy-done.8, f32[8,2432]{1,0:T(8,128)} %get-tuple-element.13.refs_1_, bf16[8,2432]{1,0:T(8,128)(2,1)} %copy-done.2, bf16[8,2432]{1,0:T(8,128)(2,1)} %copy-done.3, bf16[8,2432]{1,0:T(8,128)(2,1)} %copy-done.4, f32[4,8,128]{2,1,0:T(8,128)} %pad_maximum_fusion.refs_5_, ...), custom_call_target="tpu_custom_call" | custom-call | tf_op jit(solution)/shard_map/attend/pallas_call | solution.py:347
  29.1 3.2 %collective-permute-start.8 = (bf16[8,2048]{1,0:T(8,128)(2,1)}, bf16[8,2048]{1,0:T(8,128)(2,1)S(1)}, u32[]{:S(2)}, u32[]{:S(2)}) collective-permute-start(bf16[8,2048]{1,0:T(8,128)(2,1)} %attend.1.refs_0_), channel_id=1, source_target_pairs={{0,12},{4,0},{8,4},{12,8},{1,13},{5,1},{9,5},{13,9},{2,14},{6,2},{... | collective-permute-start | bytes 98312 | tf_op jit(solution)/shard_map/ppermute | solution.py:456
  32.3 0.6 %collective-permute-start.6 = (bf16[8,2048]{1,0:T(8,128)(2,1)}, bf16[8,2048]{1,0:T(8,128)(2,1)S(1)}, u32[]{:S(2)}, u32[]{:S(2)}) collective-permute-start(bf16[8,2048]{1,0:T(8,128)(2,1)} %attend.1.refs_0_), channel_id=1, source_target_pairs={{0,4},{4,8},{8,12},{12,0},{1,5},{5,9},{9,13},{13,1},{2,6},{6,10},{... | collective-permute-start | bytes 98312 | tf_op jit(solution)/shard_map/ppermute | solution.py:456
  32.9 1.3 %collective-permute-done.8.refs_3_ = bf16[8,2048]{1,0:T(8,128)(2,1)S(1)} collective-permute-done((bf16[8,2048]{1,0:T(8,128)(2,1)}, bf16[8,2048]{1,0:T(8,128)(2,1)S(1)}, u32[]{:S(2)}, u32[]{:S(2)}) %collective-permute-start.8) | collective-permute-done | bytes 32800 | tf_op jit(solution)/shard_map/ppermute | solution.py:456
  34.2 3.1 %collective-permute-done.7.refs_2_ = bf16[8,2048]{1,0:T(8,128)(2,1)S(1)} collective-permute-done((bf16[8,2048]{1,0:T(8,128)(2,1)}, bf16[8,2048]{1,0:T(8,128)(2,1)S(1)}, u32[]{:S(2)}, u32[]{:S(2)}) %collective-permute-start.7) | collective-permute-done | bytes 32800 | tf_op jit(solution)/shard_map/ppermute | solution.py:456
  37.3 0.9 %collective-permute-done.6.refs_1_ = bf16[8,2048]{1,0:T(8,128)(2,1)S(1)} collective-permute-done((bf16[8,2048]{1,0:T(8,128)(2,1)}, bf16[8,2048]{1,0:T(8,128)(2,1)S(1)}, u32[]{:S(2)}, u32[]{:S(2)}) %collective-permute-start.6) | collective-permute-done | bytes 32800 | tf_op jit(solution)/shard_map/ppermute | solution.py:456
  38.2 0.6 %copy-done.7 = bf16[8,2048]{1,0:T(8,128)(2,1)} copy-done((bf16[8,2048]{1,0:T(8,128)(2,1)}, bf16[8,2048]{1,0:T(8,128)(2,1)S(1)}, u32[]{:S(2)}) %copy-start.7) | copy-done | bytes 32792
  38.8 10.2 %output.1 = (f32[8,4096]{1,0:T(8,128)}, bf16[8,4096]{1,0:T(8,128)(2,1)}, bf16[8,4096]{1,0:T(8,128)(2,1)}, bf16[8,4096]{1,0:T(8,128)(2,1)}) custom-call(bf16[8,2048]{1,0:T(8,128)(2,1)} %attend.1.refs_0_, bf16[8,2048]{1,0:T(8,128)(2,1)} %copy-done.7, bf16[8,2048]{1,0:T(8,128)(2,1)} %copy-done.6, bf16[8,2048]{1,0:T(8,128)(2,1)} %copy-done.5, ...), custom_call_target="tpu_custom_call" | custom-call | tf_op jit(solution)/shard_map/output/pallas_call | solution.py:392
  49.0 0.1 collective-permute-start.9
  49.1 1.6 %collective-permute-start.10 = (bf16[8,4096]{1,0:T(8,128)(2,1)}, bf16[8,4096]{1,0:T(8,128)(2,1)S(1)}, u32[]{:S(2)}, u32[]{:S(2)}) collective-permute-start(bf16[8,4096]{1,0:T(8,128)(2,1)} %get-tuple-element.19), channel_id=1, source_target_pairs={{0,2},{1,3},{2,0},{3,1},{4,6},{5,7},{6,4},{7,5},{8,10},{9,11},{10,... | collective-permute-start | bytes 196616 | tf_op jit(solution)/shard_map/ppermute | solution.py:461
  50.6 0.3 collective-permute-start.11
  50.9 2.9 %collective-permute-done.10 = bf16[8,4096]{1,0:T(8,128)(2,1)S(1)} collective-permute-done((bf16[8,4096]{1,0:T(8,128)(2,1)}, bf16[8,4096]{1,0:T(8,128)(2,1)S(1)}, u32[]{:S(2)}, u32[]{:S(2)}) %collective-permute-start.10) | collective-permute-done | bytes 65568 | tf_op jit(solution)/shard_map/ppermute | solution.py:461
  53.8 1.2 %collective-permute-done.11 = bf16[8,4096]{1,0:T(8,128)(2,1)S(1)} collective-permute-done((bf16[8,4096]{1,0:T(8,128)(2,1)}, bf16[8,4096]{1,0:T(8,128)(2,1)S(1)}, u32[]{:S(2)}, u32[]{:S(2)}) %collective-permute-start.11) | collective-permute-done | bytes 65568 | tf_op jit(solution)/shard_map/ppermute | solution.py:461
  55.0 0.9 %add_convert_fusion = bf16[8,4096]{1,0:T(8,128)(2,1)S(1)} fusion(bf16[8,4096]{1,0:T(8,128)(2,1)S(1)} %collective-permute-done.11, bf16[8,4096]{1,0:T(8,128)(2,1)S(1)} %collective-permute-done.10, f32[8,4096]{1,0:T(8,128)} %get-tuple-element.17, bf16[8,4096]{1,0:T(8,128)(2,1)S(1)} %collective-permute-done.9), kind=kLoop, calls=%fused_computation | loop fusion | flops 229376 | bytes 393216 | tf_op jit(solution)/shard_map/convert_element_type | solution.py:463
  55.9 0.7 %convert_element_type.44 = bf16[2,4,4096]{2,1,0:T(4,128)(2,1)} reshape(bf16[8,4096]{1,0:T(8,128)(2,1)S(1)} %add_convert_fusion) | data formatting | bytes 131072 | tf_op jit(solution)/shard_map/convert_element_type | solution.py:463
  (23 shorter events, 0.1 us)
Async XLA Ops:
  0.0 20.0 %copy-start.9 = (s32[2]{0:T(128)S(1)}, s32[2]{0:T(128)}, u32[]{:S(2)}) copy-start(s32[2]{0:T(128)} %param.19) | copy-start | bytes 28
  0.0 22.8 %collective-permute-start.4 = (bf16[2,1024,256]{2,1,0:T(8,128)(2,1)}, bf16[2,1024,256]{2,1,0:T(8,128)(2,1)S(1)}, u32[]{:S(2)}, u32[]{:S(2)}) collective-permute-start(bf16[2,1024,256]{2,1,0:T(8,128)(2,1)} %refs_6_.1), channel_id=1, source_target_pairs={{0,1},{1,0},{2,3},{3,2},{4,5},{5,4},{6,7},{7,6},{8,9},{9,8},{10,11... | collective-permute-start | bytes 3145736 | tf_op jit(solution)/shard_map/ppermute | solution.py:436
  0.5 22.4 %collective-permute-start.5 = (bf16[2,1024,256]{2,1,0:T(8,128)(2,1)}, bf16[2,1024,256]{2,1,0:T(8,128)(2,1)S(1)}, u32[]{:S(2)}, u32[]{:S(2)}) collective-permute-start(bf16[2,1024,256]{2,1,0:T(8,128)(2,1)} %refs_8_.1), channel_id=1, source_target_pairs={{0,1},{1,0},{2,3},{3,2},{4,5},{5,4},{6,7},{7,6},{8,9},{9,8},{10,11... | collective-permute-start | bytes 3145736 | tf_op jit(solution)/shard_map/ppermute | solution.py:437
  0.5 18.0 %collective-permute-start = (s32[2]{0:T(128)}, s32[2]{0:T(128)S(1)}, u32[]{:S(2)}, u32[]{:S(2)}) collective-permute-start(s32[2]{0:T(128)} %param.19), channel_id=1, source_target_pairs={{0,1},{1,0},{2,3},{3,2},{4,5},{5,4},{6,7},{7,6},{8,9},{9,8},{10,11... | collective-permute-start | bytes 32 | tf_op jit(solution)/shard_map/ppermute | solution.py:438
  13.3 7.6 %collective-permute-start.1 = (bf16[8,2432]{1,0:T(8,128)(2,1)}, bf16[8,2432]{1,0:T(8,128)(2,1)S(1)}, u32[]{:S(2)}, u32[]{:S(2)}) collective-permute-start(bf16[8,2432]{1,0:T(8,128)(2,1)} %get-tuple-element.14), channel_id=1, source_target_pairs={{0,4},{4,8},{8,12},{12,0},{1,5},{5,9},{9,13},{13,1},{2,6},{6,10},{... | collective-permute-start | bytes 116744 | tf_op jit(solution)/shard_map/ppermute | solution.py:450
  15.9 6.3 %collective-permute-start.2 = (bf16[8,2432]{1,0:T(8,128)(2,1)}, bf16[8,2432]{1,0:T(8,128)(2,1)S(1)}, u32[]{:S(2)}, u32[]{:S(2)}) collective-permute-start(bf16[8,2432]{1,0:T(8,128)(2,1)} %get-tuple-element.15), channel_id=1, source_target_pairs={{0,8},{4,12},{8,0},{12,4},{1,9},{5,13},{9,1},{13,5},{2,10},{6,14},... | collective-permute-start | bytes 116744 | tf_op jit(solution)/shard_map/ppermute | solution.py:450
  18.6 4.2 %collective-permute-start.3 = (bf16[8,2432]{1,0:T(8,128)(2,1)}, bf16[8,2432]{1,0:T(8,128)(2,1)S(1)}, u32[]{:S(2)}, u32[]{:S(2)}) collective-permute-start(bf16[8,2432]{1,0:T(8,128)(2,1)} %get-tuple-element.16), channel_id=1, source_target_pairs={{0,12},{4,0},{8,4},{12,8},{1,13},{5,1},{9,5},{13,9},{2,14},{6,2},{... | collective-permute-start | bytes 116744 | tf_op jit(solution)/shard_map/ppermute | solution.py:450
  20.1 2.8 %copy-start.8 = (s32[4]{0:T(128)}, s32[4]{0:T(128)S(1)}, u32[]{:S(2)}) copy-start(s32[4]{0:T(128)S(1)} %get-tuple-element.22.refs_0_) | copy-start | bytes 52
  20.9 2.0 %copy-start.2 = (bf16[8,2432]{1,0:T(8,128)(2,1)}, bf16[8,2432]{1,0:T(8,128)(2,1)S(1)}, u32[]{:S(2)}) copy-start(bf16[8,2432]{1,0:T(8,128)(2,1)S(1)} %collective-permute-done.1.refs_2_) | copy-start | bytes 116740
  22.2 0.7 %copy-start.3 = (bf16[8,2432]{1,0:T(8,128)(2,1)}, bf16[8,2432]{1,0:T(8,128)(2,1)S(1)}, u32[]{:S(2)}) copy-start(bf16[8,2432]{1,0:T(8,128)(2,1)S(1)} %collective-permute-done.2.refs_3_) | copy-start | bytes 116740
  22.8 0.6 %copy-start.4 = (bf16[8,2432]{1,0:T(8,128)(2,1)}, bf16[8,2432]{1,0:T(8,128)(2,1)S(1)}, u32[]{:S(2)}) copy-start(bf16[8,2432]{1,0:T(8,128)(2,1)S(1)} %collective-permute-done.3.refs_4_) | copy-start | bytes 116740
  22.8 1.0 %copy-start = (bf16[2,1024,256]{2,1,0:T(8,128)(2,1)}, bf16[2,1024,256]{2,1,0:T(8,128)(2,1)S(1)}, u32[]{:S(2)}) copy-start(bf16[2,1024,256]{2,1,0:T(8,128)(2,1)S(1)} %collective-permute-done.4.refs_7_) | copy-start | bytes 3145732
  22.8 1.3 %copy-start.1 = (bf16[2,1024,256]{2,1,0:T(8,128)(2,1)}, bf16[2,1024,256]{2,1,0:T(8,128)(2,1)S(1)}, u32[]{:S(2)}) copy-start(bf16[2,1024,256]{2,1,0:T(8,128)(2,1)S(1)} %collective-permute-done.5.refs_9_) | copy-start | bytes 3145732
  29.1 5.1 %collective-permute-start.8 = (bf16[8,2048]{1,0:T(8,128)(2,1)}, bf16[8,2048]{1,0:T(8,128)(2,1)S(1)}, u32[]{:S(2)}, u32[]{:S(2)}) collective-permute-start(bf16[8,2048]{1,0:T(8,128)(2,1)} %attend.1.refs_0_), channel_id=1, source_target_pairs={{0,12},{4,0},{8,4},{12,8},{1,13},{5,1},{9,5},{13,9},{2,14},{6,2},{... | collective-permute-start | bytes 98312 | tf_op jit(solution)/shard_map/ppermute | solution.py:456
  32.3 5.0 %collective-permute-start.7 = (bf16[8,2048]{1,0:T(8,128)(2,1)}, bf16[8,2048]{1,0:T(8,128)(2,1)S(1)}, u32[]{:S(2)}, u32[]{:S(2)}) collective-permute-start(bf16[8,2048]{1,0:T(8,128)(2,1)} %attend.1.refs_0_), channel_id=1, source_target_pairs={{0,8},{4,12},{8,0},{12,4},{1,9},{5,13},{9,1},{13,5},{2,10},{6,14},... | collective-permute-start | bytes 98312 | tf_op jit(solution)/shard_map/ppermute | solution.py:456
  32.3 5.9 %collective-permute-start.6 = (bf16[8,2048]{1,0:T(8,128)(2,1)}, bf16[8,2048]{1,0:T(8,128)(2,1)S(1)}, u32[]{:S(2)}, u32[]{:S(2)}) collective-permute-start(bf16[8,2048]{1,0:T(8,128)(2,1)} %attend.1.refs_0_), channel_id=1, source_target_pairs={{0,4},{4,8},{8,12},{12,0},{1,5},{5,9},{9,13},{13,1},{2,6},{6,10},{... | collective-permute-start | bytes 98312 | tf_op jit(solution)/shard_map/ppermute | solution.py:456
  34.2 4.0 %copy-start.5 = (bf16[8,2048]{1,0:T(8,128)(2,1)}, bf16[8,2048]{1,0:T(8,128)(2,1)S(1)}, u32[]{:S(2)}) copy-start(bf16[8,2048]{1,0:T(8,128)(2,1)S(1)} %collective-permute-done.8.refs_3_) | copy-start | bytes 98308
  37.3 0.9 %copy-start.6 = (bf16[8,2048]{1,0:T(8,128)(2,1)}, bf16[8,2048]{1,0:T(8,128)(2,1)S(1)}, u32[]{:S(2)}) copy-start(bf16[8,2048]{1,0:T(8,128)(2,1)S(1)} %collective-permute-done.7.refs_2_) | copy-start | bytes 98308
  38.2 0.6 %copy-start.7 = (bf16[8,2048]{1,0:T(8,128)(2,1)}, bf16[8,2048]{1,0:T(8,128)(2,1)S(1)}, u32[]{:S(2)}) copy-start(bf16[8,2048]{1,0:T(8,128)(2,1)S(1)} %collective-permute-done.6.refs_1_) | copy-start | bytes 98308
  49.0 1.9 %collective-permute-start.9 = (bf16[8,4096]{1,0:T(8,128)(2,1)}, bf16[8,4096]{1,0:T(8,128)(2,1)S(1)}, u32[]{:S(2)}, u32[]{:S(2)}) collective-permute-start(bf16[8,4096]{1,0:T(8,128)(2,1)} %get-tuple-element.18), channel_id=1, source_target_pairs={{0,1},{1,0},{2,3},{3,2},{4,5},{5,4},{6,7},{7,6},{8,9},{9,8},{10,11... | collective-permute-start | bytes 196616 | tf_op jit(solution)/shard_map/ppermute | solution.py:461
  49.1 4.7 %collective-permute-start.10 = (bf16[8,4096]{1,0:T(8,128)(2,1)}, bf16[8,4096]{1,0:T(8,128)(2,1)S(1)}, u32[]{:S(2)}, u32[]{:S(2)}) collective-permute-start(bf16[8,4096]{1,0:T(8,128)(2,1)} %get-tuple-element.19), channel_id=1, source_target_pairs={{0,2},{1,3},{2,0},{3,1},{4,6},{5,7},{6,4},{7,5},{8,10},{9,11},{10,... | collective-permute-start | bytes 196616 | tf_op jit(solution)/shard_map/ppermute | solution.py:461
  50.6 4.3 %collective-permute-start.11 = (bf16[8,4096]{1,0:T(8,128)(2,1)}, bf16[8,4096]{1,0:T(8,128)(2,1)S(1)}, u32[]{:S(2)}, u32[]{:S(2)}) collective-permute-start(bf16[8,4096]{1,0:T(8,128)(2,1)} %get-tuple-element.20), channel_id=1, source_target_pairs={{0,3},{1,2},{2,1},{3,0},{4,7},{5,6},{6,5},{7,4},{8,11},{9,10},{10,... | collective-permute-start | bytes 196616 | tf_op jit(solution)/shard_map/ppermute | solution.py:461

commit v2 on v1

--- a/solution.py
+++ b/solution.py
@@ -11,7 +11,14 @@
 EPS = 1e-05
 BF16 = jnp.bfloat16
 F32 = jnp.float32
-VMEM_LIMIT = 60 * 1024 * 1024
+MIB = 1024 * 1024
+PROJECT_LIMIT = 26 * MIB
+ATTEND_LIMIT = 10 * MIB
+OUTPUT_LIMIT = 10 * MIB
+FETCH_LIMIT = 1 * MIB
+HBM = pl.BlockSpec(memory_space=pltpu.HBM)
+ANY = pl.BlockSpec(memory_space=pl.ANY)
+VMEM = pl.BlockSpec(memory_space=pltpu.VMEM)
 
 
 def unpack_weights(packed, scales, bits, per_word):
@@ -132,93 +139,149 @@
 
 
 def project_kernel(
-    x_ref, gain_ref, wq_ref, scale_ref, kw_ref, vw_ref, own_ref, *rest
+    x_hbm, gain_hbm, wq_hbm, scale_hbm, kw_hbm, vw_hbm, own_ref, *rest
 ):
-    nw = len(rest) - 5
+    nw = len(rest) - 11
     sends = rest[: nw - 1]
-    se_ref, so_ref, acc_ref, ss_ref, kv_ref, arr_ref = rest[nw - 1 :]
-    k = pl.program_id(0)
+    (
+        x_ref, gain_ref, wq_ref, scale_ref, kv_ref, se_ref, so_ref, y_ref, acc_ref, ss_ref, sems,
+        block_sems,
+    ) = rest[nw - 1 :]
     steps, seqs, depth = x_ref.shape
     rows = steps * seqs
-    words = wq_ref.shape[1]
+    each = seqs // nw
+    blocks, block, words = wq_ref.shape
     groups = se_ref.shape[0]
-    per_block = groups // pl.num_programs(0)
-    group = depth // per_block
-
-    @pl.when(k == 0)
-    def _():
-        acc_ref[...] = jnp.zeros_like(acc_ref)
-        ss_ref[...] = jnp.zeros_like(ss_ref)
-        kv_ref[...] = jnp.zeros_like(kv_ref)
-        row = lax.broadcasted_iota(jnp.int32, (256, 256), 0)
-        col = lax.broadcasted_iota(jnp.int32, (256, 256), 1)
-        pick = jnp.where(row == 2 * (col & 127) + (col >> 7), 1.0, 0.0).astype(BF16)
-        for c in range(words // 128):
-            terms = split3(scale_ref[:, c * 256 : (c + 1) * 256])
-            parts = [jnp.dot(term, pick, preferred_element_type=F32) for term in terms]
-            both = parts[0] + (parts[1] + parts[2])
-            se_ref[:, c * 128 : (c + 1) * 128] = both[:, :128]
-            so_ref[:, c * 128 : (c + 1) * 128] = both[:, 128:]
-
-    x = x_ref[...].astype(F32).reshape(rows, depth)
-    y = x * gain_ref[...]
-    hi = y.astype(BF16)
-    low = (y - hi.astype(F32)).astype(BF16)
-    lhs = jnp.concatenate([hi, low], axis=0)
-    exact = hi.astype(F32) + low.astype(F32)
-    sums = [
-        8.0 * jnp.sum(exact[:, g * group : (g + 1) * group], axis=1, keepdims=True)
-        for g in range(per_block)
+    per_block = groups // blocks
+    group = block // per_block
+    b = lax.axis_index("batch")
+
+    def columns(n):
+        return pl.ds(pl.multiple_of(b * n, n), n)
+
+    def fetch(i):
+        return pltpu.make_async_copy(
+            wq_hbm.at[pl.ds(pl.multiple_of(i * block, block), block), columns(words)],
+            wq_ref.at[i],
+            block_sems.at[i],
+        )
+
+    scale_copy = pltpu.make_async_copy(scale_hbm.at[:, columns(2 * words)], scale_ref, sems.at[0])
+    others = [
+        pltpu.make_async_copy(gain_hbm, gain_ref, sems.at[1]),
+        pltpu.make_async_copy(x_hbm, x_ref, sems.at[4]),
     ]
-    squares = x * x
-    total = squares[:, :128]
-    for c in range(1, depth // 128):
-        total = total + squares[:, c * 128 : (c + 1) * 128]
-    ss_ref[...] += total
+    kvs = [
+        pltpu.make_async_copy(kw_hbm.at[:, columns(HEAD)], kv_ref.at[:, :HEAD], sems.at[2]),
+        pltpu.make_async_copy(vw_hbm.at[:, columns(HEAD)], kv_ref.at[:, HEAD:], sems.at[3]),
+    ]
+    scale_copy.start()
+    for copy in others:
+        copy.start()
+    for i in range(4):
+        fetch(i).start()
+
+    acc_ref[...] = jnp.zeros_like(acc_ref)
+    ss_ref[...] = jnp.zeros_like(ss_ref)
+    row = lax.broadcasted_iota(jnp.int32, (256, 256), 0)
+    col = lax.broadcasted_iota(jnp.int32, (256, 256), 1)
+    pick = jnp.where(row == 2 * (col & 127) + (col >> 7), 1.0, 0.0).astype(BF16)
+    scale_copy.wait()
+    for c in range(words // 128):
+        terms = split3(scale_ref[:, c * 256 : (c + 1) * 256])
+        parts = [jnp.dot(term, pick, preferred_element_type=F32) for term in terms]
+        both = parts[0] + (parts[1] + parts[2])
+        se_ref[:, c * 128 : (c + 1) * 128] = both[:, :128]
+        so_ref[:, c * 128 : (c + 1) * 128] = both[:, 128:]
+    for copy in others:
+        copy.wait()
 
     chunk = 256
-    for c in range(words // chunk):
-        cols = slice(c * chunk, (c + 1) * chunk)
-        even = jnp.zeros((rows, chunk), F32)
-        odd = jnp.zeros((rows, chunk), F32)
-        for g in range(per_block):
-            span = slice(g * group, (g + 1) * group)
-            word = wq_ref[span, cols]
-            both = word.astype(F32).astype(BF16)
-            upper = (word >> 4).astype(F32).astype(BF16)
-            left = lhs[:, span]
-            p = jnp.dot(left, both, preferred_element_type=F32)
-            u = jnp.dot(left, upper, preferred_element_type=F32)
-            p = p[:rows] + p[rows:]
-            u = u[:rows] + u[rows:]
-            at = pl.ds(k * per_block + g, 1)
-            even = even + (p - 16.0 * u - sums[g]) * se_ref[at, cols]
-            odd = odd + (u - sums[g]) * so_ref[at, cols]
-        acc_ref[:, cols] += even
-        acc_ref[:, words + c * chunk : words + (c + 1) * chunk] += odd
-    key = jnp.dot(lhs, kw_ref[...], preferred_element_type=F32)
-    val = jnp.dot(lhs, vw_ref[...], preferred_element_type=F32)
-    kv_ref[:, :HEAD] += key[:rows] + key[rows:]
-    kv_ref[:, HEAD:] += val[:rows] + val[rows:]
-
-    @pl.when(k == pl.num_programs(0) - 1)
-    def _():
-        each = seqs // nw
-        lane = lax.broadcasted_iota(jnp.int32, (rows, 128), 1)
-        a, m, l = split3(jnp.sum(ss_ref[...], axis=1, keepdims=True))
-        a, m, l = a.astype(F32), m.astype(F32), l.astype(F32)
-        norm = jnp.where(lane == 0, a, jnp.where(lane == 1, m, jnp.where(lane == 2, l, 0.0)))
-        for v in range(nw):
-            for t in range(steps):
-                src = slice(t * seqs + v * each, t * seqs + (v + 1) * each)
-                dst = slice(t * each, (t + 1) * each)
-                arr_ref[v, dst, : 2 * words] = acc_ref[src, :]
-                arr_ref[v, dst, 2 * words : 2 * words + 2 * HEAD] = kv_ref[src, :]
-                arr_ref[v, dst, 2 * words + 2 * HEAD :] = norm[src]
-        me = lax.axis_index("width")
-        own_ref[...] = arr_ref[me]
-        for s in range(1, nw):
-            sends[s - 1][...] = arr_ref[lax.rem(me + s, nw)].astype(BF16)
+
+    def step(i, carry):
+        here = pl.ds(pl.multiple_of(i * block, block), block)
+        x = x_ref[:, :, here].astype(F32)
+        x = jnp.concatenate(
+            [x[t, v * each : (v + 1) * each] for v in range(nw) for t in range(steps)], axis=0
+        )
+        y = x * gain_ref[:, here]
+        hi = y.astype(BF16)
+        low = (y - hi.astype(F32)).astype(BF16)
+        lhs = jnp.concatenate([hi, low], axis=0)
+        y_ref[i] = lhs
+        squares = x * x
+        ss_ref[...] += sum(squares[:, c * 128 : (c + 1) * 128] for c in range(block // 128))
+        sums = [
+            8.0 * jnp.sum(y[:, g * group : (g + 1) * group], axis=1, keepdims=True)
+            for g in range(per_block)
+        ]
+        fetch(i).wait()
+
+        @pl.when(i + 4 < blocks)
+        def _():
+            fetch(i + 4).start()
+
+        @pl.when(i == 1)
+        def _():
+            for copy in kvs:
+                copy.start()
+
+        for c in range(words // chunk):
+            cols = slice(c * chunk, (c + 1) * chunk)
+            even = jnp.zeros((rows, chunk), F32)
+            odd = jnp.zeros((rows, chunk), F32)
+            for g in range(per_block):
+                span = slice(g * group, (g + 1) * group)
+                word = wq_ref[i, span, cols]
+                both = word.astype(F32).astype(BF16)
+                upper = (word >> 4).astype(F32).astype(BF16)
+                left = lhs[:, span]
+                p = jnp.dot(left, both, preferred_element_type=F32)
+                u = jnp.dot(left, upper, preferred_element_type=F32)
+                p = p[:rows] + p[rows:]
+                u = u[:rows] + u[rows:]
+                at = pl.ds(i * per_block + g, 1)
+                even = even + (p - 16.0 * u - sums[g]) * se_ref[at, cols]
+                odd = odd + (u - sums[g]) * so_ref[at, cols]
+            acc_ref[:, cols] += even
+            acc_ref[:, words + c * chunk : words + (c + 1) * chunk] += odd
+        return carry
+
+    def step_kv(i, carry):
+        step(i, carry)
+        new = jnp.zeros((2 * rows, 2 * HEAD), F32)
+        for n in range(2):
+            j = 2 * i - blocks + n
+            at = pl.ds(pl.multiple_of(j * block, block), block)
+            new = new + jnp.dot(y_ref[j], kv_ref[at], preferred_element_type=F32)
+        acc_ref[:, 2 * words : 2 * words + 2 * HEAD] += new[:rows] + new[rows:]
+        return carry
+
+    lax.fori_loop(0, blocks // 2, step, 0, unroll=2)
+    for copy in kvs:
+        copy.wait()
+    lax.fori_loop(blocks // 2, blocks - 1, step_kv, 0)
+    step_kv(blocks - 1, 0)
+    lane = lax.broadcasted_iota(jnp.int32, (rows, 128), 1)
+    a, m, l = split3(jnp.sum(ss_ref[...], axis=1, keepdims=True))
+    a, m, l = a.astype(F32), m.astype(F32), l.astype(F32)
+    acc_ref[:, 2 * words + 2 * HEAD :] = jnp.where(
+        lane == 0, a, jnp.where(lane == 1, m, jnp.where(lane == 2, l, 0.0))
+    )
+
+    me = lax.axis_index("width")
+    share = rows // nw
+
+    def piece(s):
+        return acc_ref[pl.ds(pl.multiple_of(lax.rem(me + s, nw) * share, share), share)]
+
+    own_ref[...] = piece(0)
+    for s in range(1, nw):
+        sends[s - 1][...] = piece(s).astype(BF16)
+
+
+def in_hbm(array):
+    return pltpu.with_memory_space_constraint(array, pltpu.HBM)
 
 
 def project(inputs, norm_gain, wq_packed, wq_scales, key_weight, value_weight, nw, nb):
@@ -226,52 +289,94 @@
     rows = steps * seqs
     words = wq_packed.shape[1] // nb
     groups = wq_scales.shape[0]
-    block = 512
+    block = 256
+    blocks = depth // block
     cols = 2 * words + 3 * HEAD
     out_rows = rows // nw
-    mine = lambda k: (k, lax.axis_index("batch"))
     return pl.pallas_call(
         project_kernel,
-        grid=(depth // block,),
-        in_specs=[
-            pl.BlockSpec((steps, seqs, block), lambda k: (0, 0, k)),
-            pl.BlockSpec((1, block), lambda k: (0, k)),
-            pl.BlockSpec((block, words), mine),
-            pl.BlockSpec((groups, 2 * words), lambda k: (0, lax.axis_index("batch"))),
-            pl.BlockSpec((block, HEAD), mine),
-            pl.BlockSpec((block, HEAD), mine),
-        ],
-        out_specs=[pl.BlockSpec((out_rows, cols), lambda k: (0, 0))] * nw,
+        in_specs=[HBM] * 6,
+        out_specs=[VMEM] * nw,
         out_shape=[jax.ShapeDtypeStruct((out_rows, cols), F32)]
         + [jax.ShapeDtypeStruct((out_rows, cols), BF16)] * (nw - 1),
         scratch_shapes=[
+            pltpu.VMEM((steps, seqs, depth), BF16),
+            pltpu.VMEM((1, depth), F32),
+            pltpu.VMEM((blocks, block, words), jnp.int32),
+            pltpu.VMEM((groups, 2 * words), F32),
+            pltpu.VMEM((depth, 2 * HEAD), BF16),
             pltpu.VMEM((groups, words), F32),
             pltpu.VMEM((groups, words), F32),
-            pltpu.VMEM((rows, 2 * words), F32),
+            pltpu.VMEM((blocks, 2 * rows, block), BF16),
+            pltpu.VMEM((rows, cols), F32),
             pltpu.VMEM((rows, 128), F32),
-            pltpu.VMEM((rows, 2 * HEAD), F32),
-            pltpu.VMEM((nw, out_rows, cols), F32),
+            pltpu.SemaphoreType.DMA((5,)),
+            pltpu.SemaphoreType.DMA((blocks,)),
         ],
-        compiler_params=pltpu.CompilerParams(vmem_limit_bytes=VMEM_LIMIT),
+        compiler_params=pltpu.CompilerParams(vmem_limit_bytes=PROJECT_LIMIT),
         name="project",
-    )(inputs, norm_gain.reshape(1, -1), wq_packed, wq_scales, key_weight, value_weight)
-
-
-def attend_kernel(heads, nw, len_ref, own_ref, *rest):
+    )(
+        *map(
+            in_hbm,
+            (inputs, norm_gain.reshape(1, -1), wq_packed, wq_scales, key_weight, value_weight),
+        )
+    )
+
+
+def weight_copies(src, dst, start, depth, sems):
+    first = lax.axis_index("batch") * depth + start
+    count = sems.shape[0]
+    each = dst.shape[0] // count
+    return [
+        pltpu.make_async_copy(
+            src.at[pl.ds(pl.multiple_of(first + n * each, each), each)],
+            dst.at[pl.ds(n * each, each)],
+            sems.at[n],
+        )
+        for n in range(count)
+    ]
+
+
+def fetch_weight(wo_weight, start, size, depth, after):
+    def body(src, after, dst, sems):
+        del after
+        copies = weight_copies(src, dst, start, depth, sems)
+        for copy in copies:
+            copy.start()
+        for copy in copies:
+            copy.wait()
+
+    return pl.pallas_call(
+        body,
+        in_specs=[HBM, ANY],
+        out_specs=VMEM,
+        out_shape=pltpu.VMEM((size, wo_weight.shape[1]), BF16),
+        scratch_shapes=[pltpu.SemaphoreType.DMA((size // 256,))],
+        compiler_params=pltpu.CompilerParams(vmem_limit_bytes=FETCH_LIMIT),
+        name="fetch",
+    )(in_hbm(wo_weight), after)
+
+
+def attend_kernel(heads, nw, start, len_ref, own_ref, *rest):
     parts = rest[: nw - 1]
-    (table_ref, k_own, k_mate, v_own, v_mate, out_ref, k_buf, v_buf, q_ref, m_ref, sems) = rest[nw - 1 :]
+    (
+        table_ref, k_own, k_mate, v_own, v_mate, wo_hbm, _, out_ref, wo_ref, k_buf, v_buf, q_ref,
+        m_ref, sems, wo_sems,
+    ) = rest[nw - 1 :]
     each, slots, _ = k_own.shape
     b = lax.axis_index("batch")
     column = pl.ds(pl.multiple_of(b * HEAD, HEAD), HEAD)
-    copies = []
-    for n, (src, buf, place) in enumerate(
-        ((k_own, k_buf, b), (k_mate, k_buf, 1 - b), (v_own, v_buf, b), (v_mate, v_buf, 1 - b))
-    ):
-        copy = pltpu.make_async_copy(
+    copies = [
+        pltpu.make_async_copy(
             src.at[:, :, column], buf.at[pl.ds(place * each, each)], sems.at[n]
         )
+        for n, (src, buf, place) in enumerate(
+            ((k_own, k_buf, b), (k_mate, k_buf, 1 - b), (v_own, v_buf, b), (v_mate, v_buf, 1 - b))
+        )
+    ]
+    incoming = weight_copies(wo_hbm, wo_ref, start, heads * HEAD, wo_sems)
+    for copy in copies + incoming:
         copy.start()
-        copies.append(copy)
 
     rows = own_ref.shape[0]
     seqs = rows // STEPS
@@ -335,75 +440,84 @@
             m_ref[pl.ds(t * seqs + j, heads, stride=rows), :] = mixed[t * heads : (t + 1) * heads]
     for n in range(heads):
         out_ref[:, n * HEAD : (n + 1) * HEAD] = m_ref[n * rows : (n + 1) * rows, :].astype(BF16)
-
-
-def attend(own, parts, table, lengths, k_own, k_mate, v_own, v_mate, heads):
+    for copy in incoming:
+        copy.wait()
+
+
+def attend(own, parts, table, lengths, k_own, k_mate, v_own, v_mate, wo_weight, start, size, after, heads):
     rows = own.shape[0]
     each, slots, _ = k_own.shape
     nw = len(parts) + 1
-    vmem = pl.BlockSpec(memory_space=pltpu.VMEM)
-    hbm = pl.BlockSpec(memory_space=pl.ANY)
-    body = lambda *refs: attend_kernel(heads, nw, *refs)
+    body = lambda *refs: attend_kernel(heads, nw, start, *refs)
     return pl.pallas_call(
         body,
-        in_specs=[pl.BlockSpec(memory_space=pltpu.SMEM)] + [vmem] * (nw + 1) + [hbm] * 4,
-        out_specs=vmem,
-        out_shape=jax.ShapeDtypeStruct((rows, heads * HEAD), BF16),
+        in_specs=[pl.BlockSpec(memory_space=pltpu.SMEM)] + [VMEM] * (nw + 1) + [ANY] * 4 + [HBM, ANY],
+        out_specs=[VMEM, VMEM],
+        out_shape=[
+            jax.ShapeDtypeStruct((rows, heads * HEAD), BF16),
+            pltpu.VMEM((size, wo_weight.shape[1]), BF16),
+        ],
         scratch_shapes=[
             pltpu.VMEM((2 * each, slots, HEAD), BF16),
             pltpu.VMEM((2 * each, slots, HEAD), BF16),
             pltpu.VMEM((heads * rows, HEAD), F32),
             pltpu.VMEM((heads * rows, HEAD), F32),
             pltpu.SemaphoreType.DMA((4,)),
+            pltpu.SemaphoreType.DMA((size // 256,)),
         ],
-        compiler_params=pltpu.CompilerParams(vmem_limit_bytes=VMEM_LIMIT),
+        compiler_params=pltpu.CompilerParams(vmem_limit_bytes=ATTEND_LIMIT),
+
         name="attend",
-    )(lengths, own, *parts, table, k_own, k_mate, v_own, v_mate)
-
-
-def output_kernel(nw, *refs):
+    )(lengths, own, *parts, table, in_hbm(k_own), k_mate, in_hbm(v_own), v_mate, in_hbm(wo_weight), after)
+
+
+def output_kernel(nw, count, *refs):
     pieces = refs[:nw]
-    wo_ref = refs[nw]
-    outs = refs[nw + 1 : 2 * nw + 1]
-    lhs_ref, acc_ref = refs[2 * nw + 1 :]
+    weights = refs[nw : nw + count]
+    outs = refs[nw + count : 2 * nw + count]
+    piece_ref, acc_ref = refs[2 * nw + count :]
     rows, depth = pieces[0].shape
-
-    @pl.when(pl.program_id(0) == 0)
-    def _():
-        me = lax.axis_index("width")
-        for s in range(nw):
-            lhs_ref[lax.rem(me + nw - s, nw)] = pieces[s][...].astype(F32)
-
-    lhs = lhs_ref[...].reshape(nw * rows, depth).astype(BF16)
-    acc = jnp.dot(lhs, wo_ref[...], preferred_element_type=F32)
-    acc_ref[...] = acc.reshape(acc_ref.shape)
+    cols = weights[0].shape[1]
+    place = lax.axis_index("width")
+    for s in range(nw):
+        piece_ref[lax.rem(place + nw - s, nw)] = pieces[s][...].astype(F32)
+    lhs = piece_ref[...].reshape(nw * rows, depth).astype(BF16)
+    block = 512
+    for n in range(cols // block):
+        span = slice(n * block, (n + 1) * block)
+        acc = jnp.zeros((nw * rows, block), F32)
+        first = 0
+        for w_ref in weights:
+            last = first + w_ref.shape[0]
+            acc = acc + jnp.dot(lhs[:, first:last], w_ref[:, span], preferred_element_type=F32)
+            first = last
+        acc_ref[:, :, span] = acc.reshape(nw, rows, block)
     me = lax.axis_index("hidden") * lax.axis_size("batch") + lax.axis_index("batch")
-    outs[0][...] = acc_ref[me]
-    for s in range(1, nw):
-        outs[s][...] = acc_ref[me ^ s].astype(BF16)
-
-
-def output(pieces, wo_weight):
-    nw = len(pieces)
+    for s in range(nw):
+        value = acc_ref[me ^ s].astype(outs[s].dtype)
+        for t in range(STEPS):
+            outs[s][t] = value[t * rows // STEPS : (t + 1) * rows // STEPS]
+
+
+def output(pieces, weights):
+    nw, count = len(pieces), len(weights)
     rows, depth = pieces[0].shape
-    cols = wo_weight.shape[1]
-    block = 512
-    body = lambda *refs: output_kernel(nw, *refs)
+    cols = weights[0].shape[1]
+    body = lambda *refs: output_kernel(nw, count, *refs)
+    shape = (STEPS, rows // STEPS, cols)
     return pl.pallas_call(
         body,
-        grid=(cols // block,),
-        in_specs=[pl.BlockSpec((rows, depth), lambda n: (0, 0))] * nw
-        + [pl.BlockSpec((depth, block), lambda n: (lax.axis_index("batch"), n))],
-        out_specs=[pl.BlockSpec((rows, block), lambda n: (0, n))] * nw,
-        out_shape=[jax.ShapeDtypeStruct((rows, cols), F32)]
-        + [jax.ShapeDtypeStruct((rows, cols), BF16)] * (nw - 1),
+        in_specs=[VMEM] * (nw + count),
+        out_specs=[VMEM] * nw,
+        out_shape=[jax.ShapeDtypeStruct(shape, F32)]
+        + [jax.ShapeDtypeStruct(shape, BF16)] * (nw - 1),
         scratch_shapes=[
             pltpu.VMEM((nw, rows, depth), F32),
-            pltpu.VMEM((nw, rows, block), F32),
+            pltpu.VMEM((nw, rows, cols), F32),
         ],
-        compiler_params=pltpu.CompilerParams(vmem_limit_bytes=VMEM_LIMIT),
+        compiler_params=pltpu.CompilerParams(vmem_limit_bytes=OUTPUT_LIMIT),
         name="output",
-    )(*pieces, wo_weight)
+    )(*pieces, *weights)
 
 
 def rotary_tables(positions):
@@ -446,21 +560,30 @@
     own, *sends = project(
         inputs, norm_gain, wq_packed, wq_scales, key_weight, value_weight, nw, nb
     )
+    own, k_mate, v_mate, *sends = lax.optimization_barrier((own, k_mate, v_mate, *sends))
     parts = [
         lax.ppermute(piece, "width", [(i, (i + s) % nw) for i in range(nw)])
         for s, piece in enumerate(sends, 1)
     ]
     heads = 2 * wq_packed.shape[1] // nb // HEAD
-    mixed = attend(own, parts, table, len_all, key_cache, k_mate, value_cache, v_mate, heads)
+    depth = heads * HEAD
+    early, late = depth // 4, depth // 4
+    middle = depth - early - late
+    w_early = fetch_weight(wo_weight, 0, early, depth, own)
+    mixed, w_middle = attend(
+        own, parts, table, len_all, key_cache, k_mate, value_cache, v_mate, wo_weight, early, middle,
+        w_early, heads,
+    )
+    w_late = fetch_weight(wo_weight, early + middle, late, depth, mixed)
     pieces = [mixed] + [
         lax.ppermute(mixed, "width", [(i, (i + s) % nw) for i in range(nw)]) for s in range(1, nw)
     ]
-    head_own, *head_sends = output(pieces, wo_weight)
+    head_own, *head_sends = output(pieces, [w_early, w_middle, w_late])
     sums = head_own
     for s, piece in enumerate(head_sends, 1):
         got = lax.ppermute(piece, ("hidden", "batch"), [(i, i ^ s) for i in range(nh * nb)])
         sums = sums + got.astype(F32)
-    return sums.reshape(STEPS, -1, sums.shape[1]).astype(BF16)
+    return sums.astype(BF16)
 
 
 def solution(mesh):

time: 57 us -> 42.5 us (0.75)
  Pallas kernels: 27.4 us -> 21 us
  waiting for transfers between devices: 11.3 us -> 6.94 us
  local copies, waits for them, and re-layouts: 2.57 us -> 0.01 us
  other arithmetic: 1.83 us -> 1 us
    pallas_call x2 -> x4, Pallas kernels: 22.5 us -> 16.5 us  [the longest x1 8.98 us: project(): pl.pallas_call(project_kernel, in_specs=[HBM] * 6, out_specs=[VMEM] * nw,...]
    ppermute x3, waiting for transfers between devices: 5.28 us -> 2.82 us  [split_heads(): lax.ppermute(mixed, 'width', [(i, (i + s) % nw) for i in range(nw)])]
    unnamed x20 -> x2, local copies, waits for them, and re-layouts: 1.91 us -> 0.01 us
    ppermute x3, waiting for transfers between devices: 1.95 us -> 0.37 us  [split_heads(): lax.ppermute(piece, 'width', [(i, (i + s) % nw) for i in range(nw)])]
    convert_element_type x1 -> x0, local copies, waits for them, and re-layouts: 0.66 us -> none  [split_heads(): return sums.reshape(STEPS, -1, sums.shape[1]).astype(BF16)]
    another operation x1, other arithmetic: 0.6 us -> 0.01 us  [rotary_tables(): return jnp.stack(out)]
  transfers between devices with their start and end apart: 12 -> 12, of which waited for: 7 -> 5; matrix products, arithmetic and copies ran while one was open for 2% -> 1% of each run, Pallas kernels for 22% -> 32%
where the time goes in v2:
time: 42.5 us; the launch traced here: 42.4 us
  Pallas kernels  21 us (49%)
  starting transfers between devices  13.3 us (31%)
  waiting for transfers between devices  6.94 us (16%)
  other arithmetic  1 us (2%)
    pallas_call x1, Pallas kernels, project(): pl.pallas_call(project_kernel, in_specs=[HBM] * 6, out_specs=[VMEM] * nw,...  8.98 us
    ppermute x3, starting transfers between devices, split_heads(): lax.ppermute(piece, 'width', [(i, (i + s) % nw) for i in range(nw)])  6.57 us
    pallas_call x1, Pallas kernels, attend(): pl.pallas_call(body, in_specs=[pl.BlockSpec(memory_space=pltpu.SMEM)] + [...  4.56 us
    pallas_call x2, Pallas kernels, fetch_weight(): pl.pallas_call(body, in_specs=[HBM, ANY], out_specs=VMEM, out_shape=pltpu...  4.48 us
    ppermute x3, starting transfers between devices, split_heads(): lax.ppermute(mixed, 'width', [(i, (i + s) % nw) for i in range(nw)])  3.84 us
    ppermute x3, waiting for transfers between devices, split_heads(): lax.ppermute(piece, ('hidden', 'batch'), [(i, i ^ s) for i in range(nh *...  3.74 us
    pallas_call x1, Pallas kernels, output(): pl.pallas_call(body, in_specs=[VMEM] * (nw + count), out_specs=[VMEM] * n...  3 us
    ppermute x3, waiting for transfers between devices, split_heads(): lax.ppermute(mixed, 'width', [(i, (i + s) % nw) for i in range(nw)])  2.82 us
  transfers between devices with their start and end apart: 12, of which 5 were waited for; matrix products, arithmetic and copies ran while one was open for 1% of the time, Pallas kernels for 32%

profile of v2, /device:TPU:0, one launch (start us, length us, event | category | flops | bytes accessed | tf_op | source)
XLA Modules:
  0.0 42.4 jit_solution(5023223207588019666)
XLA Ops:
  0.0 0.5 %collective-permute-start.1 = (bf16[2,1024,256]{2,1,0:T(8,128)(2,1)}, bf16[2,1024,256]{2,1,0:T(8,128)(2,1)S(1)}, u32[]{:S(2)}, u32[]{:S(2)}) collective-permute-start(bf16[2,1024,256]{2,1,0:T(8,128)(2,1)} %refs_6_.1), channel_id=1, source_target_pairs={{0,1},{1,0},{2,3},{3,2},{4,5},{5,4},{6,7},{7,6},{8,9},{9,8},{10,11... | collective-permute-start | bytes 3145736 | tf_op jit(solution)/shard_map/ppermute | solution.py:550
  0.5 0.1 collective-permute-start.2
  0.5 0.5 %collective-permute-start = (s32[2]{0:T(128)}, s32[2]{0:T(128)S(1)}, u32[]{:S(2)}, u32[]{:S(2)}) collective-permute-start(s32[2]{0:T(128)} %param.19), channel_id=1, source_target_pairs={{0,1},{1,0},{2,3},{3,2},{4,5},{5,4},{6,7},{7,6},{8,9},{9,8},{10,11... | collective-permute-start | bytes 32 | tf_op jit(solution)/shard_map/ppermute | solution.py:552
  1.0 9.0 %project.1 = (f32[8,2432]{1,0:T(8,128)S(1)}, bf16[8,2432]{1,0:T(8,128)(2,1)S(1)}, bf16[8,2432]{1,0:T(8,128)(2,1)S(1)}, bf16[8,2432]{1,0:T(8,128)(2,1)S(1)}) custom-call(bf16[2,16,4096]{2,1,0:T(8,128)(2,1)} %x_hbm.1, f32[1,4096]{1,0:T(1,128)} %bitcast.1, s32[4096,2048]{1,0:T(8,128)} %wq_hbm.1, f32[32,4096]{1,0:T(8,128)} %scale_hbm.1, ...), custom_call_target="tpu_custom_call" | custom-call | tf_op jit(solution)/shard_map/project/pallas_call | solution.py:296
  10.0 0.0 collective-permute-done
  10.0 0.1 broadcast_add_fusion
  10.1 0.1 add_convert_fusion.1
  10.2 0.1 multiply_cosine_fusion.1
  10.3 0.0 collective-permute-done.1.refs_7_
  10.3 0.0 collective-permute-done.2.refs_9_
  10.3 2.6 %collective-permute-start.3 = (bf16[8,2432]{1,0:T(8,128)(2,1)S(1)}, bf16[8,2432]{1,0:T(8,128)(2,1)S(1)}, u32[]{:S(2)}, u32[]{:S(2)}) collective-permute-start(bf16[8,2432]{1,0:T(8,128)(2,1)S(1)} %get-tuple-element.26), channel_id=1, source_target_pairs={{0,4},{4,8},{8,12},{12,0},{1,5},{5,9},{9,13},{13,1},{2,6},{6,10},{... | collective-permute-start | bytes 116744 | tf_op jit(solution)/shard_map/ppermute | solution.py:565
  12.9 2.6 %collective-permute-start.4 = (bf16[8,2432]{1,0:T(8,128)(2,1)S(1)}, bf16[8,2432]{1,0:T(8,128)(2,1)S(1)}, u32[]{:S(2)}, u32[]{:S(2)}) collective-permute-start(bf16[8,2432]{1,0:T(8,128)(2,1)S(1)} %get-tuple-element.27), channel_id=1, source_target_pairs={{0,8},{4,12},{8,0},{12,4},{1,9},{5,13},{9,1},{13,5},{2,10},{6,14},... | collective-permute-start | bytes 116744 | tf_op jit(solution)/shard_map/ppermute | solution.py:565
  15.5 1.3 %collective-permute-start.5 = (bf16[8,2432]{1,0:T(8,128)(2,1)S(1)}, bf16[8,2432]{1,0:T(8,128)(2,1)S(1)}, u32[]{:S(2)}, u32[]{:S(2)}) collective-permute-start(bf16[8,2432]{1,0:T(8,128)(2,1)S(1)} %get-tuple-element.28), channel_id=1, source_target_pairs={{0,12},{4,0},{8,4},{12,8},{1,13},{5,1},{9,5},{13,9},{2,14},{6,2},{... | collective-permute-start | bytes 116744 | tf_op jit(solution)/shard_map/ppermute | solution.py:565
  16.9 2.2 %fetch.2.refs_11_.refs_4_ = bf16[512,4096]{1,0:T(8,128)(2,1)S(1)} custom-call(bf16[4096,4096]{1,0:T(8,128)(2,1)} %src.3, f32[8,2432]{1,0:T(8,128)S(1)} %get-tuple-element.25.after.refs_1_), custom_call_target="tpu_custom_call" | custom-call | tf_op jit(solution)/shard_map/fetch/pallas_call | solution.py:349
  19.1 0.0 collective-permute-done.3.refs_2_
  19.1 0.0 collective-permute-done.4.refs_3_
  19.2 0.4 collective-permute-done.5.refs_4_
  19.5 4.6 %attend.1 = (bf16[8,2048]{1,0:T(8,128)(2,1)S(1)}, bf16[1024,4096]{1,0:T(8,128)(2,1)S(1)}) custom-call(s32[4]{0:T(128)S(1)} %get-tuple-element.38.refs_0_, f32[8,2432]{1,0:T(8,128)S(1)} %get-tuple-element.25.after.refs_1_, bf16[8,2432]{1,0:T(8,128)(2,1)S(1)} %collective-permute-done.3.refs_2_, bf16[8,2432]{1,0:T(8,128)(2,1)S(1)} %collective-permute-done.4.refs_3_, ...), custom_call_target="tpu_custom_call" | custom-call | tf_op jit(solution)/shard_map/attend/pallas_call | solution.py:452
  24.1 3.2 %collective-permute-start.8 = (bf16[8,2048]{1,0:T(8,128)(2,1)S(1)}, bf16[8,2048]{1,0:T(8,128)(2,1)S(1)}, u32[]{:S(2)}, u32[]{:S(2)}) collective-permute-start(bf16[8,2048]{1,0:T(8,128)(2,1)S(1)} %get-tuple-element.31.after.refs_0_), channel_id=1, source_target_pairs={{0,12},{4,0},{8,4},{12,8},{1,13},{5,1},{9,5},{13,9},{2,14},{6,2},{... | collective-permute-start | bytes 98312 | tf_op jit(solution)/shard_map/ppermute | solution.py:579
  27.3 0.6 %collective-permute-start.6 = (bf16[8,2048]{1,0:T(8,128)(2,1)S(1)}, bf16[8,2048]{1,0:T(8,128)(2,1)S(1)}, u32[]{:S(2)}, u32[]{:S(2)}) collective-permute-start(bf16[8,2048]{1,0:T(8,128)(2,1)S(1)} %get-tuple-element.31.after.refs_0_), channel_id=1, source_target_pairs={{0,4},{4,8},{8,12},{12,0},{1,5},{5,9},{9,13},{13,1},{2,6},{6,10},{... | collective-permute-start | bytes 98312 | tf_op jit(solution)/shard_map/ppermute | solution.py:579
  27.9 2.2 %fetch.3.refs_6_ = bf16[512,4096]{1,0:T(8,128)(2,1)S(1)} custom-call(bf16[4096,4096]{1,0:T(8,128)(2,1)} %src.3, bf16[8,2048]{1,0:T(8,128)(2,1)S(1)} %get-tuple-element.31.after.refs_0_), custom_call_target="tpu_custom_call" | custom-call | tf_op jit(solution)/shard_map/fetch/pallas_call | solution.py:349
  30.2 0.0 collective-permute-done.8.refs_3_
  30.2 1.9 %collective-permute-done.7.refs_2_ = bf16[8,2048]{1,0:T(8,128)(2,1)S(1)} collective-permute-done((bf16[8,2048]{1,0:T(8,128)(2,1)S(1)}, bf16[8,2048]{1,0:T(8,128)(2,1)S(1)}, u32[]{:S(2)}, u32[]{:S(2)}) %collective-permute-start.7) | collective-permute-done | bytes 32800 | tf_op jit(solution)/shard_map/ppermute | solution.py:579
  32.1 0.9 %collective-permute-done.6.refs_1_ = bf16[8,2048]{1,0:T(8,128)(2,1)S(1)} collective-permute-done((bf16[8,2048]{1,0:T(8,128)(2,1)S(1)}, bf16[8,2048]{1,0:T(8,128)(2,1)S(1)}, u32[]{:S(2)}, u32[]{:S(2)}) %collective-permute-start.6) | collective-permute-done | bytes 32800 | tf_op jit(solution)/shard_map/ppermute | solution.py:579
  33.0 3.0 %output.1 = (f32[2,4,4096]{2,1,0:T(4,128)S(1)}, bf16[2,4,4096]{2,1,0:T(4,128)(2,1)S(1)}, bf16[2,4,4096]{2,1,0:T(4,128)(2,1)S(1)}, bf16[2,4,4096]{2,1,0:T(4,128)(2,1)S(1)}) custom-call(bf16[8,2048]{1,0:T(8,128)(2,1)S(1)} %get-tuple-element.31.after.refs_0_, bf16[8,2048]{1,0:T(8,128)(2,1)S(1)} %collective-permute-done.6.refs_1_, ...), custom_call_target="tpu_custom_call" | custom-call | tf_op jit(solution)/shard_map/output/pallas_call | solution.py:508
  36.0 0.1 collective-permute-start.9
  36.1 1.6 %collective-permute-start.10 = (bf16[2,4,4096]{2,1,0:T(4,128)(2,1)S(1)}, bf16[2,4,4096]{2,1,0:T(4,128)(2,1)S(1)}, u32[]{:S(2)}, u32[]{:S(2)}) collective-permute-start(bf16[2,4,4096]{2,1,0:T(4,128)(2,1)S(1)} %get-tuple-element.35), channel_id=1, source_target_pairs={{0,2},{1,3},{2,0},{3,1},{4,6},{5,7},{6,4},{7,5},{8,10},{9,11},{10,... | collective-permute-start | bytes 196616 | tf_op jit(solution)/shard_map/ppermute | solution.py:584
  37.6 0.3 collective-permute-start.11
  38.0 0.0 collective-permute-done.9
  38.0 2.6 %collective-permute-done.10 = bf16[2,4,4096]{2,1,0:T(4,128)(2,1)S(1)} collective-permute-done((bf16[2,4,4096]{2,1,0:T(4,128)(2,1)S(1)}, bf16[2,4,4096]{2,1,0:T(4,128)(2,1)S(1)}, u32[]{:S(2)}, u32[]{:S(2)}) %collective-permute-start.10) | collective-permute-done | bytes 65568 | tf_op jit(solution)/shard_map/ppermute | solution.py:584
  40.6 1.1 %collective-permute-done.11 = bf16[2,4,4096]{2,1,0:T(4,128)(2,1)S(1)} collective-permute-done((bf16[2,4,4096]{2,1,0:T(4,128)(2,1)S(1)}, bf16[2,4,4096]{2,1,0:T(4,128)(2,1)S(1)}, u32[]{:S(2)}, u32[]{:S(2)}) %collective-permute-start.11) | collective-permute-done | bytes 65568 | tf_op jit(solution)/shard_map/ppermute | solution.py:584
  41.7 0.7 %add_convert_fusion = bf16[2,4,4096]{2,1,0:T(4,128)(2,1)} fusion(bf16[2,4,4096]{2,1,0:T(4,128)(2,1)S(1)} %collective-permute-done.11, bf16[2,4,4096]{2,1,0:T(4,128)(2,1)S(1)} %collective-permute-done.10, f32[2,4,4096]{2,1,0:T(4,128)S(1)} %get-tuple-element.33, bf16[2,4,4096]{2,1,0:T(4,128)(2,1)S(1)} %collective-permute-done.9), kind=kLoop, calls=%fused_computation | loop fusion | flops 229376 | bytes 393216 | tf_op jit(solution)/shard_map/convert_element_type | solution.py:586
  (6 shorter events, 0.0 us)
Async XLA Ops:
  0.0 10.3 %collective-permute-start.1 = (bf16[2,1024,256]{2,1,0:T(8,128)(2,1)}, bf16[2,1024,256]{2,1,0:T(8,128)(2,1)S(1)}, u32[]{:S(2)}, u32[]{:S(2)}) collective-permute-start(bf16[2,1024,256]{2,1,0:T(8,128)(2,1)} %refs_6_.1), channel_id=1, source_target_pairs={{0,1},{1,0},{2,3},{3,2},{4,5},{5,4},{6,7},{7,6},{8,9},{9,8},{10,11... | collective-permute-start | bytes 3145736 | tf_op jit(solution)/shard_map/ppermute | solution.py:550
  0.5 9.9 %collective-permute-start.2 = (bf16[2,1024,256]{2,1,0:T(8,128)(2,1)}, bf16[2,1024,256]{2,1,0:T(8,128)(2,1)S(1)}, u32[]{:S(2)}, u32[]{:S(2)}) collective-permute-start(bf16[2,1024,256]{2,1,0:T(8,128)(2,1)} %refs_8_.1), channel_id=1, source_target_pairs={{0,1},{1,0},{2,3},{3,2},{4,5},{5,4},{6,7},{7,6},{8,9},{9,8},{10,11... | collective-permute-start | bytes 3145736 | tf_op jit(solution)/shard_map/ppermute | solution.py:551
  0.5 9.5 %collective-permute-start = (s32[2]{0:T(128)}, s32[2]{0:T(128)S(1)}, u32[]{:S(2)}, u32[]{:S(2)}) collective-permute-start(s32[2]{0:T(128)} %param.19), channel_id=1, source_target_pairs={{0,1},{1,0},{2,3},{3,2},{4,5},{5,4},{6,7},{7,6},{8,9},{9,8},{10,11... | collective-permute-start | bytes 32 | tf_op jit(solution)/shard_map/ppermute | solution.py:552
  1.0 9.0 %copy-start = (s32[2]{0:T(128)S(1)}, s32[2]{0:T(128)}, u32[]{:S(2)}) copy-start(s32[2]{0:T(128)} %param.19) | copy-start | bytes 28
  10.3 8.8 %collective-permute-start.3 = (bf16[8,2432]{1,0:T(8,128)(2,1)S(1)}, bf16[8,2432]{1,0:T(8,128)(2,1)S(1)}, u32[]{:S(2)}, u32[]{:S(2)}) collective-permute-start(bf16[8,2432]{1,0:T(8,128)(2,1)S(1)} %get-tuple-element.26), channel_id=1, source_target_pairs={{0,4},{4,8},{8,12},{12,0},{1,5},{5,9},{9,13},{13,1},{2,6},{6,10},{... | collective-permute-start | bytes 116744 | tf_op jit(solution)/shard_map/ppermute | solution.py:565
  12.9 6.2 %collective-permute-start.4 = (bf16[8,2432]{1,0:T(8,128)(2,1)S(1)}, bf16[8,2432]{1,0:T(8,128)(2,1)S(1)}, u32[]{:S(2)}, u32[]{:S(2)}) collective-permute-start(bf16[8,2432]{1,0:T(8,128)(2,1)S(1)} %get-tuple-element.27), channel_id=1, source_target_pairs={{0,8},{4,12},{8,0},{12,4},{1,9},{5,13},{9,1},{13,5},{2,10},{6,14},... | collective-permute-start | bytes 116744 | tf_op jit(solution)/shard_map/ppermute | solution.py:565
  15.5 4.0 %collective-permute-start.5 = (bf16[8,2432]{1,0:T(8,128)(2,1)S(1)}, bf16[8,2432]{1,0:T(8,128)(2,1)S(1)}, u32[]{:S(2)}, u32[]{:S(2)}) collective-permute-start(bf16[8,2432]{1,0:T(8,128)(2,1)S(1)} %get-tuple-element.28), channel_id=1, source_target_pairs={{0,12},{4,0},{8,4},{12,8},{1,13},{5,1},{9,5},{13,9},{2,14},{6,2},{... | collective-permute-start | bytes 116744 | tf_op jit(solution)/shard_map/ppermute | solution.py:565
  24.1 6.1 %collective-permute-start.8 = (bf16[8,2048]{1,0:T(8,128)(2,1)S(1)}, bf16[8,2048]{1,0:T(8,128)(2,1)S(1)}, u32[]{:S(2)}, u32[]{:S(2)}) collective-permute-start(bf16[8,2048]{1,0:T(8,128)(2,1)S(1)} %get-tuple-element.31.after.refs_0_), channel_id=1, source_target_pairs={{0,12},{4,0},{8,4},{12,8},{1,13},{5,1},{9,5},{13,9},{2,14},{6,2},{... | collective-permute-start | bytes 98312 | tf_op jit(solution)/shard_map/ppermute | solution.py:579
  27.3 4.8 %collective-permute-start.7 = (bf16[8,2048]{1,0:T(8,128)(2,1)S(1)}, bf16[8,2048]{1,0:T(8,128)(2,1)S(1)}, u32[]{:S(2)}, u32[]{:S(2)}) collective-permute-start(bf16[8,2048]{1,0:T(8,128)(2,1)S(1)} %get-tuple-element.31.after.refs_0_), channel_id=1, source_target_pairs={{0,8},{4,12},{8,0},{12,4},{1,9},{5,13},{9,1},{13,5},{2,10},{6,14},... | collective-permute-start | bytes 98312 | tf_op jit(solution)/shard_map/ppermute | solution.py:579
  27.3 5.7 %collective-permute-start.6 = (bf16[8,2048]{1,0:T(8,128)(2,1)S(1)}, bf16[8,2048]{1,0:T(8,128)(2,1)S(1)}, u32[]{:S(2)}, u32[]{:S(2)}) collective-permute-start(bf16[8,2048]{1,0:T(8,128)(2,1)S(1)} %get-tuple-element.31.after.refs_0_), channel_id=1, source_target_pairs={{0,4},{4,8},{8,12},{12,0},{1,5},{5,9},{9,13},{13,1},{2,6},{6,10},{... | collective-permute-start | bytes 98312 | tf_op jit(solution)/shard_map/ppermute | solution.py:579
  36.0 1.9 %collective-permute-start.9 = (bf16[2,4,4096]{2,1,0:T(4,128)(2,1)S(1)}, bf16[2,4,4096]{2,1,0:T(4,128)(2,1)S(1)}, u32[]{:S(2)}, u32[]{:S(2)}) collective-permute-start(bf16[2,4,4096]{2,1,0:T(4,128)(2,1)S(1)} %get-tuple-element.34), channel_id=1, source_target_pairs={{0,1},{1,0},{2,3},{3,2},{4,5},{5,4},{6,7},{7,6},{8,9},{9,8},{10,11... | collective-permute-start | bytes 196616 | tf_op jit(solution)/shard_map/ppermute | solution.py:584
  36.1 4.5 %collective-permute-start.10 = (bf16[2,4,4096]{2,1,0:T(4,128)(2,1)S(1)}, bf16[2,4,4096]{2,1,0:T(4,128)(2,1)S(1)}, u32[]{:S(2)}, u32[]{:S(2)}) collective-permute-start(bf16[2,4,4096]{2,1,0:T(4,128)(2,1)S(1)} %get-tuple-element.35), channel_id=1, source_target_pairs={{0,2},{1,3},{2,0},{3,1},{4,6},{5,7},{6,4},{7,5},{8,10},{9,11},{10,... | collective-permute-start | bytes 196616 | tf_op jit(solution)/shard_map/ppermute | solution.py:584
  37.6 4.0 %collective-permute-start.11 = (bf16[2,4,4096]{2,1,0:T(4,128)(2,1)S(1)}, bf16[2,4,4096]{2,1,0:T(4,128)(2,1)S(1)}, u32[]{:S(2)}, u32[]{:S(2)}) collective-permute-start(bf16[2,4,4096]{2,1,0:T(4,128)(2,1)S(1)} %get-tuple-element.36), channel_id=1, source_target_pairs={{0,3},{1,2},{2,1},{3,0},{4,7},{5,6},{6,5},{7,4},{8,11},{9,10},{10,... | collective-permute-start | bytes 196616 | tf_op jit(solution)/shard_map/ppermute | solution.py:584

commit v3 on v2

--- a/solution.py
+++ b/solution.py
@@ -16,6 +16,7 @@
 ATTEND_LIMIT = 10 * MIB
 OUTPUT_LIMIT = 10 * MIB
 FETCH_LIMIT = 1 * MIB
+EARLY, MIDDLE, LATE = 2, 3, 3
 HBM = pl.BlockSpec(memory_space=pltpu.HBM)
 ANY = pl.BlockSpec(memory_space=pl.ANY)
 VMEM = pl.BlockSpec(memory_space=pltpu.VMEM)
@@ -178,7 +179,7 @@
     scale_copy.start()
     for copy in others:
         copy.start()
-    for i in range(4):
+    for i in range(3):
         fetch(i).start()
 
     acc_ref[...] = jnp.zeros_like(acc_ref)
@@ -196,7 +197,7 @@
     for copy in others:
         copy.wait()
 
-    chunk = 256
+    chunk = 512
 
     def step(i, carry):
         here = pl.ds(pl.multiple_of(i * block, block), block)
@@ -217,11 +218,11 @@
         ]
         fetch(i).wait()
 
-        @pl.when(i + 4 < blocks)
+        @pl.when(i + 3 < blocks)
         def _():
-            fetch(i + 4).start()
-
-        @pl.when(i == 1)
+            fetch(i + 3).start()
+
+        @pl.when(i == 0)
         def _():
             for copy in kvs:
                 copy.start()
@@ -257,10 +258,10 @@
         acc_ref[:, 2 * words : 2 * words + 2 * HEAD] += new[:rows] + new[rows:]
         return carry
 
-    lax.fori_loop(0, blocks // 2, step, 0, unroll=2)
+    lax.fori_loop(0, blocks // 2, step, 0, unroll=4)
     for copy in kvs:
         copy.wait()
-    lax.fori_loop(blocks // 2, blocks - 1, step_kv, 0)
+    lax.fori_loop(blocks // 2, blocks - 1, step_kv, 0, unroll=3)
     step_kv(blocks - 1, 0)
     lane = lax.broadcasted_iota(jnp.int32, (rows, 128), 1)
     a, m, l = split3(jnp.sum(ss_ref[...], axis=1, keepdims=True))
@@ -289,7 +290,7 @@
     rows = steps * seqs
     words = wq_packed.shape[1] // nb
     groups = wq_scales.shape[0]
-    block = 256
+    block = 512
     blocks = depth // block
     cols = 2 * words + 3 * HEAD
     out_rows = rows // nw
@@ -360,7 +361,7 @@
 def attend_kernel(heads, nw, start, len_ref, own_ref, *rest):
     parts = rest[: nw - 1]
     (
-        table_ref, k_own, k_mate, v_own, v_mate, wo_hbm, _, out_ref, wo_ref, k_buf, v_buf, q_ref,
+        cq_ref, sq_ref, ck_ref, sk_ref, k_own, k_mate, v_own, v_mate, wo_hbm, _, out_ref, wo_ref, k_buf, v_buf, q_ref,
         m_ref, sems, wo_sems,
     ) = rest[nw - 1 :]
     each, slots, _ = k_own.shape
@@ -395,8 +396,7 @@
         o = total[:, half + m * HEAD : half + (m + 1) * HEAD]
         tiles.append(jnp.where(left, e, pltpu.roll(o, HEAD // 2, 1)))
         tiles.append(jnp.where(left, pltpu.roll(e, HEAD // 2, 1), o))
-    cos_q, sin_q = table_ref[0], table_ref[1]
-    cos_k, sin_k = table_ref[2], table_ref[3]
+    cos_q, sin_q, cos_k, sin_k = cq_ref[...], sq_ref[...], ck_ref[...], sk_ref[...]
     near = (lane & (HEAD // 2 - 1)) < HEAD // 4
     turned = []
     for q in tiles:
@@ -451,7 +451,7 @@
     body = lambda *refs: attend_kernel(heads, nw, start, *refs)
     return pl.pallas_call(
         body,
-        in_specs=[pl.BlockSpec(memory_space=pltpu.SMEM)] + [VMEM] * (nw + 1) + [ANY] * 4 + [HBM, ANY],
+        in_specs=[pl.BlockSpec(memory_space=pltpu.SMEM)] + [VMEM] * (nw + 4) + [ANY] * 4 + [HBM, ANY],
         out_specs=[VMEM, VMEM],
         out_shape=[
             jax.ShapeDtypeStruct((rows, heads * HEAD), BF16),
@@ -468,7 +468,7 @@
         compiler_params=pltpu.CompilerParams(vmem_limit_bytes=ATTEND_LIMIT),
 
         name="attend",
-    )(lengths, own, *parts, table, in_hbm(k_own), k_mate, in_hbm(v_own), v_mate, in_hbm(wo_weight), after)
+    )(lengths, own, *parts, *table, in_hbm(k_own), k_mate, in_hbm(v_own), v_mate, in_hbm(wo_weight), after)
 
 
 def output_kernel(nw, count, *refs):
@@ -509,8 +509,7 @@
         body,
         in_specs=[VMEM] * (nw + count),
         out_specs=[VMEM] * nw,
-        out_shape=[jax.ShapeDtypeStruct(shape, F32)]
-        + [jax.ShapeDtypeStruct(shape, BF16)] * (nw - 1),
+        out_shape=[jax.ShapeDtypeStruct(shape, dtype) for dtype in (F32, BF16, F32, BF16)],
         scratch_shapes=[
             pltpu.VMEM((nw, rows, depth), F32),
             pltpu.VMEM((nw, rows, cols), F32),
@@ -530,7 +529,7 @@
         angle = positions.astype(F32)[:, None] * freq[None, :]
         sign = jnp.where(dim < HEAD // 2, -1.0, 1.0)[None, :]
         out += [jnp.cos(angle), jnp.sin(angle) * sign]
-    return jnp.stack(out)
+    return out
 
 
 def split_heads(
@@ -567,8 +566,7 @@
     ]
     heads = 2 * wq_packed.shape[1] // nb // HEAD
     depth = heads * HEAD
-    early, late = depth // 4, depth // 4
-    middle = depth - early - late
+    early, middle, late = EARLY * depth // 8, MIDDLE * depth // 8, LATE * depth // 8
     w_early = fetch_weight(wo_weight, 0, early, depth, own)
     mixed, w_middle = attend(
         own, parts, table, len_all, key_cache, k_mate, value_cache, v_mate, wo_weight, early, middle,
@@ -578,11 +576,12 @@
     pieces = [mixed] + [
         lax.ppermute(mixed, "width", [(i, (i + s) % nw) for i in range(nw)]) for s in range(1, nw)
     ]
-    head_own, *head_sends = output(pieces, [w_early, w_middle, w_late])
-    sums = head_own
-    for s, piece in enumerate(head_sends, 1):
-        got = lax.ppermute(piece, ("hidden", "batch"), [(i, i ^ s) for i in range(nh * nb)])
-        sums = sums + got.astype(F32)
+    here, across_core, across_chip, across_both = output(pieces, [w_early, w_middle, w_late])
+    relay = lax.ppermute(across_both, "batch", swap)
+    near = lax.ppermute(across_core, "batch", swap)
+    leaving = (across_chip + relay.astype(F32)).astype(BF16)
+    far = lax.ppermute(leaving, "hidden", swap)
+    sums = here + near.astype(F32) + far.astype(F32)
     return sums.astype(BF16)
 
 
@@ -593,6 +592,7 @@
         kv_local = args[4].shape[1] // HEAD
         fits = (
             sizes["batch"] == 2
+            and sizes["hidden"] == 2
             and kv_local == 2
             and sizes["width"] == sizes["hidden"] * sizes["batch"]
             and args[0].shape[1] // sizes["width"] == 2 * args[9].shape[0]

time: 42.5 us -> 40.8 us (0.960)
  waiting for transfers between devices: 6.94 us -> 5.93 us
  Pallas kernels: 21 us -> 20.1 us
    pallas_call x1, Pallas kernels: 8.98 us -> 8.06 us  [project(): pl.pallas_call(project_kernel, in_specs=[HBM] * 6, out_specs=[VMEM] * nw,...]
    pallas_call x2, Pallas kernels: 4.48 us -> 5.13 us  [fetch_weight(): pl.pallas_call(body, in_specs=[HBM, ANY], out_specs=VMEM, out_shape=pltpu...]
    ppermute x3, waiting for transfers between devices: 2.82 us -> 2.17 us  [split_heads(): lax.ppermute(mixed, 'width', [(i, (i + s) % nw) for i in range(nw)])]
    pallas_call x1, Pallas kernels: 4.56 us -> 3.96 us  [attend(): pl.pallas_call(body, in_specs=[pl.BlockSpec(memory_space=pltpu.SMEM)] + [...]
where the time goes in v3:
time: 40.8 us; the launch traced here: 40.7 us
  Pallas kernels  20.1 us (49%)
  starting transfers between devices  13.5 us (33%)
  waiting for transfers between devices  5.93 us (15%)
  other arithmetic  1.02 us (2%)
    pallas_call x1, Pallas kernels, project(): pl.pallas_call(project_kernel, in_specs=[HBM] * 6, out_specs=[VMEM] * nw,...  8.06 us
    ppermute x3, starting transfers between devices, split_heads(): lax.ppermute(piece, 'width', [(i, (i + s) % nw) for i in range(nw)])  6.53 us
    pallas_call x2, Pallas kernels, fetch_weight(): pl.pallas_call(body, in_specs=[HBM, ANY], out_specs=VMEM, out_shape=pltpu...  5.13 us
    pallas_call x1, Pallas kernels, attend(): pl.pallas_call(body, in_specs=[pl.BlockSpec(memory_space=pltpu.SMEM)] + [...  3.96 us
    ppermute x3, starting transfers between devices, split_heads(): lax.ppermute(mixed, 'width', [(i, (i + s) % nw) for i in range(nw)])  3.84 us
    pallas_call x1, Pallas kernels, output(): pl.pallas_call(body, in_specs=[VMEM] * (nw + count), out_specs=[VMEM] * n...  3 us
    ppermute x1, waiting for transfers between devices, split_heads(): far = lax.ppermute(leaving, 'hidden', swap)  2.76 us
    ppermute x3, waiting for transfers between devices, split_heads(): lax.ppermute(mixed, 'width', [(i, (i + s) % nw) for i in range(nw)])  2.17 us
  transfers between devices with their start and end apart: 12, of which 5 were waited for; matrix products, arithmetic and copies ran while one was open for 1% of the time, Pallas kernels for 32%

profile of v3, /device:TPU:0, one launch (start us, length us, event | category | flops | bytes accessed | tf_op | source)
XLA Modules:
  0.0 40.7 jit_solution(18225678739050952932)
XLA Ops:
  0.0 0.5 %collective-permute-start.1 = (bf16[2,1024,256]{2,1,0:T(8,128)(2,1)}, bf16[2,1024,256]{2,1,0:T(8,128)(2,1)S(1)}, u32[]{:S(2)}, u32[]{:S(2)}) collective-permute-start(bf16[2,1024,256]{2,1,0:T(8,128)(2,1)} %refs_9_.1), channel_id=1, source_target_pairs={{0,1},{1,0},{2,3},{3,2},{4,5},{5,4},{6,7},{7,6},{8,9},{9,8},{10,11... | collective-permute-start | bytes 3145736 | tf_op jit(solution)/shard_map/ppermute | solution.py:549
  0.5 0.1 collective-permute-start.2
  0.5 0.5 %collective-permute-start = (s32[2]{0:T(128)}, s32[2]{0:T(128)S(1)}, u32[]{:S(2)}, u32[]{:S(2)}) collective-permute-start(s32[2]{0:T(128)} %param.19), channel_id=1, source_target_pairs={{0,1},{1,0},{2,3},{3,2},{4,5},{5,4},{6,7},{7,6},{8,9},{9,8},{10,11... | collective-permute-start | bytes 32 | tf_op jit(solution)/shard_map/ppermute | solution.py:551
  1.0 8.1 %project.1 = (f32[8,2432]{1,0:T(8,128)S(1)}, bf16[8,2432]{1,0:T(8,128)(2,1)S(1)}, bf16[8,2432]{1,0:T(8,128)(2,1)S(1)}, bf16[8,2432]{1,0:T(8,128)(2,1)S(1)}) custom-call(bf16[2,16,4096]{2,1,0:T(8,128)(2,1)} %x_hbm.1, f32[1,4096]{1,0:T(1,128)} %bitcast.1, s32[4096,2048]{1,0:T(8,128)} %wq_hbm.1, f32[32,4096]{1,0:T(8,128)} %scale_hbm.1, ...), custom_call_target="tpu_custom_call" | custom-call | tf_op jit(solution)/shard_map/project/pallas_call | solution.py:297
  9.1 0.0 collective-permute-done
  9.1 0.1 broadcast_add_fusion
  9.2 0.1 add_convert_fusion.2
  9.2 0.0 collective-permute-done.1.refs_10_
  9.2 0.0 collective-permute-done.2.refs_12_
  9.2 2.6 %collective-permute-start.3 = (bf16[8,2432]{1,0:T(8,128)(2,1)S(1)}, bf16[8,2432]{1,0:T(8,128)(2,1)S(1)}, u32[]{:S(2)}, u32[]{:S(2)}) collective-permute-start(bf16[8,2432]{1,0:T(8,128)(2,1)S(1)} %get-tuple-element.26), channel_id=1, source_target_pairs={{0,4},{4,8},{8,12},{12,0},{1,5},{5,9},{9,13},{13,1},{2,6},{6,10},{... | collective-permute-start | bytes 116744 | tf_op jit(solution)/shard_map/ppermute | solution.py:564
  11.8 2.6 %collective-permute-start.4 = (bf16[8,2432]{1,0:T(8,128)(2,1)S(1)}, bf16[8,2432]{1,0:T(8,128)(2,1)S(1)}, u32[]{:S(2)}, u32[]{:S(2)}) collective-permute-start(bf16[8,2432]{1,0:T(8,128)(2,1)S(1)} %get-tuple-element.27), channel_id=1, source_target_pairs={{0,8},{4,12},{8,0},{12,4},{1,9},{5,13},{9,1},{13,5},{2,10},{6,14},... | collective-permute-start | bytes 116744 | tf_op jit(solution)/shard_map/ppermute | solution.py:564
  14.4 1.3 %collective-permute-start.5 = (bf16[8,2432]{1,0:T(8,128)(2,1)S(1)}, bf16[8,2432]{1,0:T(8,128)(2,1)S(1)}, u32[]{:S(2)}, u32[]{:S(2)}) collective-permute-start(bf16[8,2432]{1,0:T(8,128)(2,1)S(1)} %get-tuple-element.28), channel_id=1, source_target_pairs={{0,12},{4,0},{8,4},{12,8},{1,13},{5,1},{9,5},{13,9},{2,14},{6,2},{... | collective-permute-start | bytes 116744 | tf_op jit(solution)/shard_map/ppermute | solution.py:564
  15.8 0.1 fusion.1
  15.9 2.2 %fetch.2.refs_14_.refs_4_ = bf16[512,4096]{1,0:T(8,128)(2,1)S(1)} custom-call(bf16[4096,4096]{1,0:T(8,128)(2,1)} %src.3, f32[8,2432]{1,0:T(8,128)S(1)} %get-tuple-element.25.after.refs_1_), custom_call_target="tpu_custom_call" | custom-call | tf_op jit(solution)/shard_map/fetch/pallas_call | solution.py:350
  18.2 0.0 collective-permute-done.3.refs_2_
  18.2 0.0 collective-permute-done.4.refs_3_
  18.2 0.2 collective-permute-done.5.refs_4_
  18.4 4.0 %attend.1 = (bf16[8,2048]{1,0:T(8,128)(2,1)S(1)}, bf16[768,4096]{1,0:T(8,128)(2,1)S(1)}) custom-call(s32[4]{0:T(128)S(1)} %get-tuple-element.38.refs_0_, f32[8,2432]{1,0:T(8,128)S(1)} %get-tuple-element.25.after.refs_1_, bf16[8,2432]{1,0:T(8,128)(2,1)S(1)} %collective-permute-done.3.refs_2_, bf16[8,2432]{1,0:T(8,128)(2,1)S(1)} %collective-permute-done.4.refs_3_, ...), custom_call_target="tpu_custom_call" | custom-call | tf_op jit(solution)/shard_map/attend/pallas_call | solution.py:452
  22.4 3.2 %collective-permute-start.8 = (bf16[8,2048]{1,0:T(8,128)(2,1)S(1)}, bf16[8,2048]{1,0:T(8,128)(2,1)S(1)}, u32[]{:S(2)}, u32[]{:S(2)}) collective-permute-start(bf16[8,2048]{1,0:T(8,128)(2,1)S(1)} %get-tuple-element.31.after.refs_0_), channel_id=1, source_target_pairs={{0,12},{4,0},{8,4},{12,8},{1,13},{5,1},{9,5},{13,9},{2,14},{6,2},{... | collective-permute-start | bytes 98312 | tf_op jit(solution)/shard_map/ppermute | solution.py:577
  25.6 0.0 collective-permute-start.7
  25.6 0.6 %collective-permute-start.6 = (bf16[8,2048]{1,0:T(8,128)(2,1)S(1)}, bf16[8,2048]{1,0:T(8,128)(2,1)S(1)}, u32[]{:S(2)}, u32[]{:S(2)}) collective-permute-start(bf16[8,2048]{1,0:T(8,128)(2,1)S(1)} %get-tuple-element.31.after.refs_0_), channel_id=1, source_target_pairs={{0,4},{4,8},{8,12},{12,0},{1,5},{5,9},{9,13},{13,1},{2,6},{6,10},{... | collective-permute-start | bytes 98312 | tf_op jit(solution)/shard_map/ppermute | solution.py:577
  26.2 2.9 %fetch.3.refs_6_ = bf16[768,4096]{1,0:T(8,128)(2,1)S(1)} custom-call(bf16[4096,4096]{1,0:T(8,128)(2,1)} %src.3, bf16[8,2048]{1,0:T(8,128)(2,1)S(1)} %get-tuple-element.31.after.refs_0_), custom_call_target="tpu_custom_call" | custom-call | tf_op jit(solution)/shard_map/fetch/pallas_call | solution.py:350
  29.1 1.3 %collective-permute-done.7.refs_2_ = bf16[8,2048]{1,0:T(8,128)(2,1)S(1)} collective-permute-done((bf16[8,2048]{1,0:T(8,128)(2,1)S(1)}, bf16[8,2048]{1,0:T(8,128)(2,1)S(1)}, u32[]{:S(2)}, u32[]{:S(2)}) %collective-permute-start.7) | collective-permute-done | bytes 32800 | tf_op jit(solution)/shard_map/ppermute | solution.py:577
  30.4 0.9 %collective-permute-done.6.refs_1_ = bf16[8,2048]{1,0:T(8,128)(2,1)S(1)} collective-permute-done((bf16[8,2048]{1,0:T(8,128)(2,1)S(1)}, bf16[8,2048]{1,0:T(8,128)(2,1)S(1)}, u32[]{:S(2)}, u32[]{:S(2)}) %collective-permute-start.6) | collective-permute-done | bytes 32800 | tf_op jit(solution)/shard_map/ppermute | solution.py:577
  31.3 3.0 %output.1 = (f32[2,4,4096]{2,1,0:T(4,128)S(1)}, bf16[2,4,4096]{2,1,0:T(4,128)(2,1)S(1)}, f32[2,4,4096]{2,1,0:T(4,128)S(1)}, bf16[2,4,4096]{2,1,0:T(4,128)(2,1)S(1)}) custom-call(bf16[8,2048]{1,0:T(8,128)(2,1)S(1)} %get-tuple-element.31.after.refs_0_, bf16[8,2048]{1,0:T(8,128)(2,1)S(1)} %collective-permute-done.6.refs_1_, ...), custom_call_target="tpu_custom_call" | custom-call | tf_op jit(solution)/shard_map/output/pallas_call | solution.py:508
  34.3 0.1 collective-permute-start.10
  34.4 0.5 %collective-permute-start.9 = (bf16[2,4,4096]{2,1,0:T(4,128)(2,1)S(1)}, bf16[2,4,4096]{2,1,0:T(4,128)(2,1)S(1)}, u32[]{:S(2)}, u32[]{:S(2)}) collective-permute-start(bf16[2,4,4096]{2,1,0:T(4,128)(2,1)S(1)} %get-tuple-element.34), channel_id=1, source_target_pairs={{0,1},{1,0},{2,3},{3,2},{4,5},{5,4},{6,7},{7,6},{8,9},{9,8},{10,11... | collective-permute-start | bytes 196616 | tf_op jit(solution)/shard_map/ppermute | solution.py:581
  34.9 0.7 %collective-permute-done.10 = bf16[2,4,4096]{2,1,0:T(4,128)(2,1)S(1)} collective-permute-done((bf16[2,4,4096]{2,1,0:T(4,128)(2,1)S(1)}, bf16[2,4,4096]{2,1,0:T(4,128)(2,1)S(1)}, u32[]{:S(2)}, u32[]{:S(2)}) %collective-permute-start.10) | collective-permute-done | bytes 65568 | tf_op jit(solution)/shard_map/ppermute | solution.py:580
  35.7 1.6 %collective-permute-start.11 = (bf16[2,4,4096]{2,1,0:T(4,128)(2,1)S(1)}, bf16[2,4,4096]{2,1,0:T(4,128)(2,1)S(1)}, u32[]{:S(2)}, u32[]{:S(2)}) collective-permute-start(bf16[2,4,4096]{2,1,0:T(4,128)(2,1)S(1)} %add_convert_fusion.1), channel_id=1, source_target_pairs={{0,2},{2,0},{1,3},{3,1},{4,6},{6,4},{5,7},{7,5},{8,10},{10,8},{9,1... | collective-permute-start | bytes 196616 | tf_op jit(solution)/shard_map/ppermute | solution.py:583
  37.2 0.0 collective-permute-done.9
  37.2 2.8 %collective-permute-done.11 = bf16[2,4,4096]{2,1,0:T(4,128)(2,1)S(1)} collective-permute-done((bf16[2,4,4096]{2,1,0:T(4,128)(2,1)S(1)}, bf16[2,4,4096]{2,1,0:T(4,128)(2,1)S(1)}, u32[]{:S(2)}, u32[]{:S(2)}) %collective-permute-start.11) | collective-permute-done | bytes 65568 | tf_op jit(solution)/shard_map/ppermute | solution.py:583
  40.0 0.7 %add_convert_fusion = bf16[2,4,4096]{2,1,0:T(4,128)(2,1)} fusion(bf16[2,4,4096]{2,1,0:T(4,128)(2,1)S(1)} %collective-permute-done.11, f32[2,4,4096]{2,1,0:T(4,128)S(1)} %get-tuple-element.33, bf16[2,4,4096]{2,1,0:T(4,128)(2,1)S(1)} %collective-permute-done.9), kind=kLoop, calls=%fused_computation | loop fusion | flops 163840 | bytes 327680 | tf_op jit(solution)/shard_map/convert_element_type | solution.py:585
  (6 shorter events, 0.1 us)
Async XLA Ops:
  0.0 9.2 %collective-permute-start.1 = (bf16[2,1024,256]{2,1,0:T(8,128)(2,1)}, bf16[2,1024,256]{2,1,0:T(8,128)(2,1)S(1)}, u32[]{:S(2)}, u32[]{:S(2)}) collective-permute-start(bf16[2,1024,256]{2,1,0:T(8,128)(2,1)} %refs_9_.1), channel_id=1, source_target_pairs={{0,1},{1,0},{2,3},{3,2},{4,5},{5,4},{6,7},{7,6},{8,9},{9,8},{10,11... | collective-permute-start | bytes 3145736 | tf_op jit(solution)/shard_map/ppermute | solution.py:549
  0.5 8.8 %collective-permute-start.2 = (bf16[2,1024,256]{2,1,0:T(8,128)(2,1)}, bf16[2,1024,256]{2,1,0:T(8,128)(2,1)S(1)}, u32[]{:S(2)}, u32[]{:S(2)}) collective-permute-start(bf16[2,1024,256]{2,1,0:T(8,128)(2,1)} %refs_11_.1), channel_id=1, source_target_pairs={{0,1},{1,0},{2,3},{3,2},{4,5},{5,4},{6,7},{7,6},{8,9},{9,8},{10,11... | collective-permute-start | bytes 3145736 | tf_op jit(solution)/shard_map/ppermute | solution.py:550
  0.5 8.6 %collective-permute-start = (s32[2]{0:T(128)}, s32[2]{0:T(128)S(1)}, u32[]{:S(2)}, u32[]{:S(2)}) collective-permute-start(s32[2]{0:T(128)} %param.19), channel_id=1, source_target_pairs={{0,1},{1,0},{2,3},{3,2},{4,5},{5,4},{6,7},{7,6},{8,9},{9,8},{10,11... | collective-permute-start | bytes 32 | tf_op jit(solution)/shard_map/ppermute | solution.py:551
  1.0 8.1 %copy-start = (s32[2]{0:T(128)S(1)}, s32[2]{0:T(128)}, u32[]{:S(2)}) copy-start(s32[2]{0:T(128)} %param.19) | copy-start | bytes 28
  9.2 8.9 %collective-permute-start.3 = (bf16[8,2432]{1,0:T(8,128)(2,1)S(1)}, bf16[8,2432]{1,0:T(8,128)(2,1)S(1)}, u32[]{:S(2)}, u32[]{:S(2)}) collective-permute-start(bf16[8,2432]{1,0:T(8,128)(2,1)S(1)} %get-tuple-element.26), channel_id=1, source_target_pairs={{0,4},{4,8},{8,12},{12,0},{1,5},{5,9},{9,13},{13,1},{2,6},{6,10},{... | collective-permute-start | bytes 116744 | tf_op jit(solution)/shard_map/ppermute | solution.py:564
  11.8 6.3 %collective-permute-start.4 = (bf16[8,2432]{1,0:T(8,128)(2,1)S(1)}, bf16[8,2432]{1,0:T(8,128)(2,1)S(1)}, u32[]{:S(2)}, u32[]{:S(2)}) collective-permute-start(bf16[8,2432]{1,0:T(8,128)(2,1)S(1)} %get-tuple-element.27), channel_id=1, source_target_pairs={{0,8},{4,12},{8,0},{12,4},{1,9},{5,13},{9,1},{13,5},{2,10},{6,14},... | collective-permute-start | bytes 116744 | tf_op jit(solution)/shard_map/ppermute | solution.py:564
  14.4 4.0 %collective-permute-start.5 = (bf16[8,2432]{1,0:T(8,128)(2,1)S(1)}, bf16[8,2432]{1,0:T(8,128)(2,1)S(1)}, u32[]{:S(2)}, u32[]{:S(2)}) collective-permute-start(bf16[8,2432]{1,0:T(8,128)(2,1)S(1)} %get-tuple-element.28), channel_id=1, source_target_pairs={{0,12},{4,0},{8,4},{12,8},{1,13},{5,1},{9,5},{13,9},{2,14},{6,2},{... | collective-permute-start | bytes 116744 | tf_op jit(solution)/shard_map/ppermute | solution.py:564
  22.4 6.7 %collective-permute-start.8 = (bf16[8,2048]{1,0:T(8,128)(2,1)S(1)}, bf16[8,2048]{1,0:T(8,128)(2,1)S(1)}, u32[]{:S(2)}, u32[]{:S(2)}) collective-permute-start(bf16[8,2048]{1,0:T(8,128)(2,1)S(1)} %get-tuple-element.31.after.refs_0_), channel_id=1, source_target_pairs={{0,12},{4,0},{8,4},{12,8},{1,13},{5,1},{9,5},{13,9},{2,14},{6,2},{... | collective-permute-start | bytes 98312 | tf_op jit(solution)/shard_map/ppermute | solution.py:577
  25.6 4.8 %collective-permute-start.7 = (bf16[8,2048]{1,0:T(8,128)(2,1)S(1)}, bf16[8,2048]{1,0:T(8,128)(2,1)S(1)}, u32[]{:S(2)}, u32[]{:S(2)}) collective-permute-start(bf16[8,2048]{1,0:T(8,128)(2,1)S(1)} %get-tuple-element.31.after.refs_0_), channel_id=1, source_target_pairs={{0,8},{4,12},{8,0},{12,4},{1,9},{5,13},{9,1},{13,5},{2,10},{6,14},... | collective-permute-start | bytes 98312 | tf_op jit(solution)/shard_map/ppermute | solution.py:577
  25.6 5.7 %collective-permute-start.6 = (bf16[8,2048]{1,0:T(8,128)(2,1)S(1)}, bf16[8,2048]{1,0:T(8,128)(2,1)S(1)}, u32[]{:S(2)}, u32[]{:S(2)}) collective-permute-start(bf16[8,2048]{1,0:T(8,128)(2,1)S(1)} %get-tuple-element.31.after.refs_0_), channel_id=1, source_target_pairs={{0,4},{4,8},{8,12},{12,0},{1,5},{5,9},{9,13},{13,1},{2,6},{6,10},{... | collective-permute-start | bytes 98312 | tf_op jit(solution)/shard_map/ppermute | solution.py:577
  34.3 1.3 %collective-permute-start.10 = (bf16[2,4,4096]{2,1,0:T(4,128)(2,1)S(1)}, bf16[2,4,4096]{2,1,0:T(4,128)(2,1)S(1)}, u32[]{:S(2)}, u32[]{:S(2)}) collective-permute-start(bf16[2,4,4096]{2,1,0:T(4,128)(2,1)S(1)} %get-tuple-element.36), channel_id=1, source_target_pairs={{0,1},{1,0},{2,3},{3,2},{4,5},{5,4},{6,7},{7,6},{8,9},{9,8},{10,11... | collective-permute-start | bytes 196616 | tf_op jit(solution)/shard_map/ppermute | solution.py:580
  34.4 2.9 %collective-permute-start.9 = (bf16[2,4,4096]{2,1,0:T(4,128)(2,1)S(1)}, bf16[2,4,4096]{2,1,0:T(4,128)(2,1)S(1)}, u32[]{:S(2)}, u32[]{:S(2)}) collective-permute-start(bf16[2,4,4096]{2,1,0:T(4,128)(2,1)S(1)} %get-tuple-element.34), channel_id=1, source_target_pairs={{0,1},{1,0},{2,3},{3,2},{4,5},{5,4},{6,7},{7,6},{8,9},{9,8},{10,11... | collective-permute-start | bytes 196616 | tf_op jit(solution)/shard_map/ppermute | solution.py:581
  35.7 4.3 %collective-permute-start.11 = (bf16[2,4,4096]{2,1,0:T(4,128)(2,1)S(1)}, bf16[2,4,4096]{2,1,0:T(4,128)(2,1)S(1)}, u32[]{:S(2)}, u32[]{:S(2)}) collective-permute-start(bf16[2,4,4096]{2,1,0:T(4,128)(2,1)S(1)} %add_convert_fusion.1), channel_id=1, source_target_pairs={{0,2},{2,0},{1,3},{3,1},{4,6},{6,4},{5,7},{7,5},{8,10},{10,8},{9,1... | collective-permute-start | bytes 196616 | tf_op jit(solution)/shard_map/ppermute | solution.py:583

commit v4 on v3

--- a/solution.py
+++ b/solution.py
@@ -274,7 +274,7 @@
     share = rows // nw
 
     def piece(s):
-        return acc_ref[pl.ds(pl.multiple_of(lax.rem(me + s, nw) * share, share), share)]
+        return acc_ref[pl.ds(pl.multiple_of((me ^ s) * share, share), share)]
 
     own_ref[...] = piece(0)
     for s in range(1, nw):
@@ -364,12 +364,12 @@
         cq_ref, sq_ref, ck_ref, sk_ref, k_own, k_mate, v_own, v_mate, wo_hbm, _, out_ref, wo_ref, k_buf, v_buf, q_ref,
         m_ref, sems, wo_sems,
     ) = rest[nw - 1 :]
-    each, slots, _ = k_own.shape
+    held, slots, _ = k_own.shape
     b = lax.axis_index("batch")
     column = pl.ds(pl.multiple_of(b * HEAD, HEAD), HEAD)
     copies = [
         pltpu.make_async_copy(
-            src.at[:, :, column], buf.at[pl.ds(place * each, each)], sems.at[n]
+            src.at[:, :, column], buf.at[pl.ds(place * held, held)], sems.at[n]
         )
         for n, (src, buf, place) in enumerate(
             ((k_own, k_buf, b), (k_mate, k_buf, 1 - b), (v_own, v_buf, b), (v_mate, v_buf, 1 - b))
@@ -414,28 +414,52 @@
     for copy in copies:
         copy.wait()
 
-    slot = lax.broadcasted_iota(jnp.int32, (STEPS * heads, slots), 1)
-    later = lax.broadcasted_iota(jnp.int32, (STEPS * heads, 1), 0) >= heads
+    each = STEPS * heads
+    queries = [
+        jnp.concatenate(
+            [q_ref[pl.ds(t * seqs + j, heads, stride=rows), :] for t in range(STEPS)], axis=0
+        )
+        for j in range(seqs)
+    ]
+    scores = jnp.concatenate(
+        [
+            lax.dot_general(
+                queries[j].astype(BF16), k_buf[j], (((1,), (1,)), ((), ())),
+                preferred_element_type=F32,
+            )
+            for j in range(seqs)
+        ],
+        axis=0,
+    ) * HEAD ** (-0.5)
+    row = lax.broadcasted_iota(jnp.int32, (seqs * each, 1), 0)
+    filled = jnp.full((seqs * each, 1), len_ref[seqs - 1], jnp.int32)
+    for j in range(seqs - 1, 0, -1):
+        filled = jnp.where(row < j * each, len_ref[j - 1], filled)
+    slot = lax.broadcasted_iota(jnp.int32, (seqs * each, slots), 1)
+    scores = jnp.where(slot < filled, scores, -1e30)
+
+    def fresh(t):
+        dots = [
+            jnp.sum(queries[j] * k_new[t * seqs + j : t * seqs + j + 1], axis=1, keepdims=True)
+            for j in range(seqs)
+        ]
+        return jnp.concatenate(dots, axis=0) * HEAD ** (-0.5)
+
+    first = fresh(0)
+    second = jnp.where(lax.rem(row, each) >= heads, fresh(1), -1e30)
+    peak = jnp.maximum(jnp.max(scores, axis=1, keepdims=True), jnp.maximum(first, second))
+    weights = jnp.exp(scores - peak)
+    first = jnp.exp(first - peak)
+    second = jnp.exp(second - peak)
+    inverse = 1.0 / (jnp.sum(weights, axis=1, keepdims=True) + first + second)
+    probs = (weights * inverse).astype(BF16)
+    first = (first * inverse).astype(BF16).astype(F32)
+    second = (second * inverse).astype(BF16).astype(F32)
     for j in range(seqs):
-        q = jnp.concatenate(
-            [q_ref[pl.ds(t * seqs + j, heads, stride=rows), :] for t in range(STEPS)], axis=0
-        )
-        scores = lax.dot_general(
-            q.astype(BF16), k_buf[j], (((1,), (1,)), ((), ())), preferred_element_type=F32
-        ) * HEAD ** (-0.5)
-        scores = jnp.where(slot < len_ref[j], scores, -1e30)
-        first = jnp.sum(q * k_new[j : j + 1], axis=1, keepdims=True) * HEAD ** (-0.5)
-        second = jnp.sum(q * k_new[seqs + j : seqs + j + 1], axis=1, keepdims=True) * HEAD ** (-0.5)
-        second = jnp.where(later, second, -1e30)
-        peak = jnp.maximum(jnp.max(scores, axis=1, keepdims=True), jnp.maximum(first, second))
-        weights = jnp.exp(scores - peak)
-        first = jnp.exp(first - peak)
-        second = jnp.exp(second - peak)
-        inverse = 1.0 / (jnp.sum(weights, axis=1, keepdims=True) + first + second)
-        probs = (weights * inverse).astype(BF16)
-        mixed = jnp.dot(probs, v_buf[j], preferred_element_type=F32)
-        mixed = mixed + (first * inverse).astype(BF16).astype(F32) * v_new[j : j + 1]
-        mixed = mixed + (second * inverse).astype(BF16).astype(F32) * v_new[seqs + j : seqs + j + 1]
+        span = slice(j * each, (j + 1) * each)
+        mixed = jnp.dot(probs[span], v_buf[j], preferred_element_type=F32)
+        mixed = mixed + first[span] * v_new[j : j + 1]
+        mixed = mixed + second[span] * v_new[seqs + j : seqs + j + 1]
         for t in range(STEPS):
             m_ref[pl.ds(t * seqs + j, heads, stride=rows), :] = mixed[t * heads : (t + 1) * heads]
     for n in range(heads):
@@ -480,7 +504,7 @@
     cols = weights[0].shape[1]
     place = lax.axis_index("width")
     for s in range(nw):
-        piece_ref[lax.rem(place + nw - s, nw)] = pieces[s][...].astype(F32)
+        piece_ref[place ^ s] = pieces[s][...].astype(F32)
     lhs = piece_ref[...].reshape(nw * rows, depth).astype(BF16)
     block = 512
     for n in range(cols // block):
@@ -561,7 +585,7 @@
     )
     own, k_mate, v_mate, *sends = lax.optimization_barrier((own, k_mate, v_mate, *sends))
     parts = [
-        lax.ppermute(piece, "width", [(i, (i + s) % nw) for i in range(nw)])
+        lax.ppermute(piece, "width", [(i, i ^ s) for i in range(nw)])
         for s, piece in enumerate(sends, 1)
     ]
     heads = 2 * wq_packed.shape[1] // nb // HEAD
@@ -569,12 +593,12 @@
     early, middle, late = EARLY * depth // 8, MIDDLE * depth // 8, LATE * depth // 8
     w_early = fetch_weight(wo_weight, 0, early, depth, own)
     mixed, w_middle = attend(
-        own, parts, table, len_all, key_cache, k_mate, value_cache, v_mate, wo_weight, early, middle,
+        own, parts[::-1], table, len_all, key_cache, k_mate, value_cache, v_mate, wo_weight, early, middle,
         w_early, heads,
     )
     w_late = fetch_weight(wo_weight, early + middle, late, depth, mixed)
     pieces = [mixed] + [
-        lax.ppermute(mixed, "width", [(i, (i + s) % nw) for i in range(nw)]) for s in range(1, nw)
+        lax.ppermute(mixed, "width", [(i, i ^ s) for i in range(nw)]) for s in range(1, nw)
     ]
     here, across_core, across_chip, across_both = output(pieces, [w_early, w_middle, w_late])
     relay = lax.ppermute(across_both, "batch", swap)

time: 40.8 us -> 39.6 us (0.971)
  starting transfers between devices: 13.5 us -> 12.8 us
  waiting for transfers between devices: 5.93 us -> 5.38 us
    ppermute x6, starting transfers between devices: 10.4 us -> 9.74 us  [the longest x3 5.28 us: split_heads(): lax.ppermute(piece, 'width', [(i, i ^ s) for i in range(nw)])]
    ppermute x6, waiting for transfers between devices: 2.41 us -> 1.86 us  [the longest x3 1.85 us: split_heads(): lax.ppermute(piece, 'width', [(i, i ^ s) for i in range(nw)])]
  transfers between devices with their start and end apart: 12 -> 12, of which waited for: 5 -> 3; matrix products, arithmetic and copies ran while one was open for 1% -> 1% of each run, Pallas kernels for 32% -> 33%
where the time goes in v4:
time: 39.6 us; the launch traced here: 39.5 us
  Pallas kernels  20.1 us (51%)
  starting transfers between devices  12.8 us (32%)
  waiting for transfers between devices  5.38 us (14%)
  other arithmetic  1.02 us (3%)
    pallas_call x1, Pallas kernels, project(): pl.pallas_call(project_kernel, in_specs=[HBM] * 6, out_specs=[VMEM] * nw,...  8.04 us
    ppermute x3, starting transfers between devices, split_heads(): lax.ppermute(piece, 'width', [(i, i ^ s) for i in range(nw)])  5.28 us
    pallas_call x2, Pallas kernels, fetch_weight(): pl.pallas_call(body, in_specs=[HBM, ANY], out_specs=VMEM, out_shape=pltpu...  5.13 us
    ppermute x3, starting transfers between devices, split_heads(): lax.ppermute(mixed, 'width', [(i, i ^ s) for i in range(nw)])  4.45 us
    pallas_call x1, Pallas kernels, attend(): pl.pallas_call(body, in_specs=[pl.BlockSpec(memory_space=pltpu.SMEM)] + [...  3.96 us
    pallas_call x1, Pallas kernels, output(): pl.pallas_call(body, in_specs=[VMEM] * (nw + count), out_specs=[VMEM] * n...  3 us
    ppermute x1, waiting for transfers between devices, split_heads(): far = lax.ppermute(leaving, 'hidden', swap)  2.76 us
    ppermute x3, waiting for transfers between devices, split_heads(): lax.ppermute(piece, 'width', [(i, i ^ s) for i in range(nw)])  1.85 us
  transfers between devices with their start and end apart: 12, of which 3 were waited for; matrix products, arithmetic and copies ran while one was open for 1% of the time, Pallas kernels for 33%

profile of v4, /device:TPU:0, one launch (start us, length us, event | category | flops | bytes accessed | tf_op | source)
XLA Modules:
  0.0 39.5 jit_solution(982468488758023409)
XLA Ops:
  0.0 0.5 %collective-permute-start.1 = (bf16[2,1024,256]{2,1,0:T(8,128)(2,1)}, bf16[2,1024,256]{2,1,0:T(8,128)(2,1)S(1)}, u32[]{:S(2)}, u32[]{:S(2)}) collective-permute-start(bf16[2,1024,256]{2,1,0:T(8,128)(2,1)} %refs_9_.1), channel_id=1, source_target_pairs={{0,1},{1,0},{2,3},{3,2},{4,5},{5,4},{6,7},{7,6},{8,9},{9,8},{10,11... | collective-permute-start | bytes 3145736 | tf_op jit(solution)/shard_map/ppermute | solution.py:573
  0.5 0.1 collective-permute-start.2
  0.5 0.5 %collective-permute-start = (s32[2]{0:T(128)}, s32[2]{0:T(128)S(1)}, u32[]{:S(2)}, u32[]{:S(2)}) collective-permute-start(s32[2]{0:T(128)} %param.19), channel_id=1, source_target_pairs={{0,1},{1,0},{2,3},{3,2},{4,5},{5,4},{6,7},{7,6},{8,9},{9,8},{10,11... | collective-permute-start | bytes 32 | tf_op jit(solution)/shard_map/ppermute | solution.py:575
  1.0 8.0 %project.1 = (f32[8,2432]{1,0:T(8,128)S(1)}, bf16[8,2432]{1,0:T(8,128)(2,1)S(1)}, bf16[8,2432]{1,0:T(8,128)(2,1)S(1)}, bf16[8,2432]{1,0:T(8,128)(2,1)S(1)}) custom-call(bf16[2,16,4096]{2,1,0:T(8,128)(2,1)} %x_hbm.1, f32[1,4096]{1,0:T(1,128)} %bitcast.1, s32[4096,2048]{1,0:T(8,128)} %wq_hbm.1, f32[32,4096]{1,0:T(8,128)} %scale_hbm.1, ...), custom_call_target="tpu_custom_call" | custom-call | tf_op jit(solution)/shard_map/project/pallas_call | solution.py:297
  9.0 0.0 collective-permute-done
  9.1 0.1 broadcast_add_fusion
  9.1 0.1 add_convert_fusion.2
  9.2 0.0 collective-permute-done.1.refs_10_
  9.2 0.0 collective-permute-done.2.refs_12_
  9.2 4.6 %collective-permute-start.3 = (bf16[8,2432]{1,0:T(8,128)(2,1)S(1)}, bf16[8,2432]{1,0:T(8,128)(2,1)S(1)}, u32[]{:S(2)}, u32[]{:S(2)}) collective-permute-start(bf16[8,2432]{1,0:T(8,128)(2,1)S(1)} %get-tuple-element.26), channel_id=1, source_target_pairs={{0,12},{4,8},{8,4},{12,0},{1,13},{5,9},{9,5},{13,1},{2,14},{6,10},... | collective-permute-start | bytes 116744 | tf_op jit(solution)/shard_map/ppermute | solution.py:588
  13.9 0.0 collective-permute-start.4
  13.9 0.6 %collective-permute-start.5 = (bf16[8,2432]{1,0:T(8,128)(2,1)S(1)}, bf16[8,2432]{1,0:T(8,128)(2,1)S(1)}, u32[]{:S(2)}, u32[]{:S(2)}) collective-permute-start(bf16[8,2432]{1,0:T(8,128)(2,1)S(1)} %get-tuple-element.28), channel_id=1, source_target_pairs={{0,4},{4,0},{8,12},{12,8},{1,5},{5,1},{9,13},{13,9},{2,6},{6,2},{1... | collective-permute-start | bytes 116744 | tf_op jit(solution)/shard_map/ppermute | solution.py:588
  14.5 0.1 fusion.1
  14.6 2.2 %fetch.2.refs_14_.refs_4_ = bf16[512,4096]{1,0:T(8,128)(2,1)S(1)} custom-call(bf16[4096,4096]{1,0:T(8,128)(2,1)} %src.3, f32[8,2432]{1,0:T(8,128)S(1)} %get-tuple-element.25.after.refs_1_), custom_call_target="tpu_custom_call" | custom-call | tf_op jit(solution)/shard_map/fetch/pallas_call | solution.py:350
  16.9 0.0 collective-permute-done.3.refs_2_
  16.9 1.8 %collective-permute-done.4.refs_3_ = bf16[8,2432]{1,0:T(8,128)(2,1)S(1)} collective-permute-done((bf16[8,2432]{1,0:T(8,128)(2,1)S(1)}, bf16[8,2432]{1,0:T(8,128)(2,1)S(1)}, u32[]{:S(2)}, u32[]{:S(2)}) %collective-permute-start.4) | collective-permute-done | bytes 38944 | tf_op jit(solution)/shard_map/ppermute | solution.py:588
  18.8 0.0 collective-permute-done.5.refs_4_
  18.8 4.0 %attend.1 = (bf16[8,2048]{1,0:T(8,128)(2,1)S(1)}, bf16[768,4096]{1,0:T(8,128)(2,1)S(1)}) custom-call(s32[4]{0:T(128)S(1)} %get-tuple-element.38.refs_0_, f32[8,2432]{1,0:T(8,128)S(1)} %get-tuple-element.25.after.refs_1_, bf16[8,2432]{1,0:T(8,128)(2,1)S(1)} %collective-permute-done.3.refs_2_, bf16[8,2432]{1,0:T(8,128)(2,1)S(1)} %collective-permute-done.4.refs_3_, ...), custom_call_target="tpu_custom_call" | custom-call | tf_op jit(solution)/shard_map/attend/pallas_call | solution.py:476
  22.7 2.0 %collective-permute-start.8 = (bf16[8,2048]{1,0:T(8,128)(2,1)S(1)}, bf16[8,2048]{1,0:T(8,128)(2,1)S(1)}, u32[]{:S(2)}, u32[]{:S(2)}) collective-permute-start(bf16[8,2048]{1,0:T(8,128)(2,1)S(1)} %get-tuple-element.31.after.refs_0_), channel_id=1, source_target_pairs={{0,12},{4,8},{8,4},{12,0},{1,13},{5,9},{9,5},{13,1},{2,14},{6,10},... | collective-permute-start | bytes 98312 | tf_op jit(solution)/shard_map/ppermute | solution.py:601
  24.7 0.3 collective-permute-start.7
  25.0 2.2 %collective-permute-start.6 = (bf16[8,2048]{1,0:T(8,128)(2,1)S(1)}, bf16[8,2048]{1,0:T(8,128)(2,1)S(1)}, u32[]{:S(2)}, u32[]{:S(2)}) collective-permute-start(bf16[8,2048]{1,0:T(8,128)(2,1)S(1)} %get-tuple-element.31.after.refs_0_), channel_id=1, source_target_pairs={{0,4},{4,0},{8,12},{12,8},{1,5},{5,1},{9,13},{13,9},{2,6},{6,2},{1... | collective-permute-start | bytes 98312 | tf_op jit(solution)/shard_map/ppermute | solution.py:601
  27.2 2.9 %fetch.3.refs_6_ = bf16[768,4096]{1,0:T(8,128)(2,1)S(1)} custom-call(bf16[4096,4096]{1,0:T(8,128)(2,1)} %src.3, bf16[8,2048]{1,0:T(8,128)(2,1)S(1)} %get-tuple-element.31.after.refs_0_), custom_call_target="tpu_custom_call" | custom-call | tf_op jit(solution)/shard_map/fetch/pallas_call | solution.py:350
  30.1 0.0 collective-permute-done.8.refs_3_
  30.1 0.0 collective-permute-done.7.refs_2_
  30.1 0.0 collective-permute-done.6.refs_1_
  30.1 3.0 %output.1 = (f32[2,4,4096]{2,1,0:T(4,128)S(1)}, bf16[2,4,4096]{2,1,0:T(4,128)(2,1)S(1)}, f32[2,4,4096]{2,1,0:T(4,128)S(1)}, bf16[2,4,4096]{2,1,0:T(4,128)(2,1)S(1)}) custom-call(bf16[8,2048]{1,0:T(8,128)(2,1)S(1)} %get-tuple-element.31.after.refs_0_, bf16[8,2048]{1,0:T(8,128)(2,1)S(1)} %collective-permute-done.6.refs_1_, ...), custom_call_target="tpu_custom_call" | custom-call | tf_op jit(solution)/shard_map/output/pallas_call | solution.py:532
  33.1 0.1 collective-permute-start.10
  33.2 0.5 %collective-permute-start.9 = (bf16[2,4,4096]{2,1,0:T(4,128)(2,1)S(1)}, bf16[2,4,4096]{2,1,0:T(4,128)(2,1)S(1)}, u32[]{:S(2)}, u32[]{:S(2)}) collective-permute-start(bf16[2,4,4096]{2,1,0:T(4,128)(2,1)S(1)} %get-tuple-element.34), channel_id=1, source_target_pairs={{0,1},{1,0},{2,3},{3,2},{4,5},{5,4},{6,7},{7,6},{8,9},{9,8},{10,11... | collective-permute-start | bytes 196616 | tf_op jit(solution)/shard_map/ppermute | solution.py:605
  33.7 0.7 %collective-permute-done.10 = bf16[2,4,4096]{2,1,0:T(4,128)(2,1)S(1)} collective-permute-done((bf16[2,4,4096]{2,1,0:T(4,128)(2,1)S(1)}, bf16[2,4,4096]{2,1,0:T(4,128)(2,1)S(1)}, u32[]{:S(2)}, u32[]{:S(2)}) %collective-permute-start.10) | collective-permute-done | bytes 65568 | tf_op jit(solution)/shard_map/ppermute | solution.py:604
  34.5 1.6 %collective-permute-start.11 = (bf16[2,4,4096]{2,1,0:T(4,128)(2,1)S(1)}, bf16[2,4,4096]{2,1,0:T(4,128)(2,1)S(1)}, u32[]{:S(2)}, u32[]{:S(2)}) collective-permute-start(bf16[2,4,4096]{2,1,0:T(4,128)(2,1)S(1)} %add_convert_fusion.1), channel_id=1, source_target_pairs={{0,2},{2,0},{1,3},{3,1},{4,6},{6,4},{5,7},{7,5},{8,10},{10,8},{9,1... | collective-permute-start | bytes 196616 | tf_op jit(solution)/shard_map/ppermute | solution.py:607
  36.1 2.8 %collective-permute-done.11 = bf16[2,4,4096]{2,1,0:T(4,128)(2,1)S(1)} collective-permute-done((bf16[2,4,4096]{2,1,0:T(4,128)(2,1)S(1)}, bf16[2,4,4096]{2,1,0:T(4,128)(2,1)S(1)}, u32[]{:S(2)}, u32[]{:S(2)}) %collective-permute-start.11) | collective-permute-done | bytes 65568 | tf_op jit(solution)/shard_map/ppermute | solution.py:607
  38.8 0.7 %add_convert_fusion = bf16[2,4,4096]{2,1,0:T(4,128)(2,1)} fusion(bf16[2,4,4096]{2,1,0:T(4,128)(2,1)S(1)} %collective-permute-done.11, f32[2,4,4096]{2,1,0:T(4,128)S(1)} %get-tuple-element.33, bf16[2,4,4096]{2,1,0:T(4,128)(2,1)S(1)} %collective-permute-done.9), kind=kLoop, calls=%fused_computation | loop fusion | flops 163840 | bytes 327680 | tf_op jit(solution)/shard_map/convert_element_type | solution.py:609
  (6 shorter events, 0.1 us)
Async XLA Ops:
  0.0 9.2 %collective-permute-start.1 = (bf16[2,1024,256]{2,1,0:T(8,128)(2,1)}, bf16[2,1024,256]{2,1,0:T(8,128)(2,1)S(1)}, u32[]{:S(2)}, u32[]{:S(2)}) collective-permute-start(bf16[2,1024,256]{2,1,0:T(8,128)(2,1)} %refs_9_.1), channel_id=1, source_target_pairs={{0,1},{1,0},{2,3},{3,2},{4,5},{5,4},{6,7},{7,6},{8,9},{9,8},{10,11... | collective-permute-start | bytes 3145736 | tf_op jit(solution)/shard_map/ppermute | solution.py:573
  0.5 8.8 %collective-permute-start.2 = (bf16[2,1024,256]{2,1,0:T(8,128)(2,1)}, bf16[2,1024,256]{2,1,0:T(8,128)(2,1)S(1)}, u32[]{:S(2)}, u32[]{:S(2)}) collective-permute-start(bf16[2,1024,256]{2,1,0:T(8,128)(2,1)} %refs_11_.1), channel_id=1, source_target_pairs={{0,1},{1,0},{2,3},{3,2},{4,5},{5,4},{6,7},{7,6},{8,9},{9,8},{10,11... | collective-permute-start | bytes 3145736 | tf_op jit(solution)/shard_map/ppermute | solution.py:574
  0.5 8.5 %collective-permute-start = (s32[2]{0:T(128)}, s32[2]{0:T(128)S(1)}, u32[]{:S(2)}, u32[]{:S(2)}) collective-permute-start(s32[2]{0:T(128)} %param.19), channel_id=1, source_target_pairs={{0,1},{1,0},{2,3},{3,2},{4,5},{5,4},{6,7},{7,6},{8,9},{9,8},{10,11... | collective-permute-start | bytes 32 | tf_op jit(solution)/shard_map/ppermute | solution.py:575
  1.0 8.1 %copy-start = (s32[2]{0:T(128)S(1)}, s32[2]{0:T(128)}, u32[]{:S(2)}) copy-start(s32[2]{0:T(128)} %param.19) | copy-start | bytes 28
  9.2 7.7 %collective-permute-start.3 = (bf16[8,2432]{1,0:T(8,128)(2,1)S(1)}, bf16[8,2432]{1,0:T(8,128)(2,1)S(1)}, u32[]{:S(2)}, u32[]{:S(2)}) collective-permute-start(bf16[8,2432]{1,0:T(8,128)(2,1)S(1)} %get-tuple-element.26), channel_id=1, source_target_pairs={{0,12},{4,8},{8,4},{12,0},{1,13},{5,9},{9,5},{13,1},{2,14},{6,10},... | collective-permute-start | bytes 116744 | tf_op jit(solution)/shard_map/ppermute | solution.py:588
  13.9 4.9 %collective-permute-start.4 = (bf16[8,2432]{1,0:T(8,128)(2,1)S(1)}, bf16[8,2432]{1,0:T(8,128)(2,1)S(1)}, u32[]{:S(2)}, u32[]{:S(2)}) collective-permute-start(bf16[8,2432]{1,0:T(8,128)(2,1)S(1)} %get-tuple-element.27), channel_id=1, source_target_pairs={{0,8},{4,12},{8,0},{12,4},{1,9},{5,13},{9,1},{13,5},{2,10},{6,14},... | collective-permute-start | bytes 116744 | tf_op jit(solution)/shard_map/ppermute | solution.py:588
  13.9 4.9 %collective-permute-start.5 = (bf16[8,2432]{1,0:T(8,128)(2,1)S(1)}, bf16[8,2432]{1,0:T(8,128)(2,1)S(1)}, u32[]{:S(2)}, u32[]{:S(2)}) collective-permute-start(bf16[8,2432]{1,0:T(8,128)(2,1)S(1)} %get-tuple-element.28), channel_id=1, source_target_pairs={{0,4},{4,0},{8,12},{12,8},{1,5},{5,1},{9,13},{13,9},{2,6},{6,2},{1... | collective-permute-start | bytes 116744 | tf_op jit(solution)/shard_map/ppermute | solution.py:588
  22.7 7.3 %collective-permute-start.8 = (bf16[8,2048]{1,0:T(8,128)(2,1)S(1)}, bf16[8,2048]{1,0:T(8,128)(2,1)S(1)}, u32[]{:S(2)}, u32[]{:S(2)}) collective-permute-start(bf16[8,2048]{1,0:T(8,128)(2,1)S(1)} %get-tuple-element.31.after.refs_0_), channel_id=1, source_target_pairs={{0,12},{4,8},{8,4},{12,0},{1,13},{5,9},{9,5},{13,1},{2,14},{6,10},... | collective-permute-start | bytes 98312 | tf_op jit(solution)/shard_map/ppermute | solution.py:601
  24.7 5.4 %collective-permute-start.7 = (bf16[8,2048]{1,0:T(8,128)(2,1)S(1)}, bf16[8,2048]{1,0:T(8,128)(2,1)S(1)}, u32[]{:S(2)}, u32[]{:S(2)}) collective-permute-start(bf16[8,2048]{1,0:T(8,128)(2,1)S(1)} %get-tuple-element.31.after.refs_0_), channel_id=1, source_target_pairs={{0,8},{4,12},{8,0},{12,4},{1,9},{5,13},{9,1},{13,5},{2,10},{6,14},... | collective-permute-start | bytes 98312 | tf_op jit(solution)/shard_map/ppermute | solution.py:601
  25.0 5.1 %collective-permute-start.6 = (bf16[8,2048]{1,0:T(8,128)(2,1)S(1)}, bf16[8,2048]{1,0:T(8,128)(2,1)S(1)}, u32[]{:S(2)}, u32[]{:S(2)}) collective-permute-start(bf16[8,2048]{1,0:T(8,128)(2,1)S(1)} %get-tuple-element.31.after.refs_0_), channel_id=1, source_target_pairs={{0,4},{4,0},{8,12},{12,8},{1,5},{5,1},{9,13},{13,9},{2,6},{6,2},{1... | collective-permute-start | bytes 98312 | tf_op jit(solution)/shard_map/ppermute | solution.py:601
  33.1 1.3 %collective-permute-start.10 = (bf16[2,4,4096]{2,1,0:T(4,128)(2,1)S(1)}, bf16[2,4,4096]{2,1,0:T(4,128)(2,1)S(1)}, u32[]{:S(2)}, u32[]{:S(2)}) collective-permute-start(bf16[2,4,4096]{2,1,0:T(4,128)(2,1)S(1)} %get-tuple-element.36), channel_id=1, source_target_pairs={{0,1},{1,0},{2,3},{3,2},{4,5},{5,4},{6,7},{7,6},{8,9},{9,8},{10,11... | collective-permute-start | bytes 196616 | tf_op jit(solution)/shard_map/ppermute | solution.py:604
  33.2 2.9 %collective-permute-start.9 = (bf16[2,4,4096]{2,1,0:T(4,128)(2,1)S(1)}, bf16[2,4,4096]{2,1,0:T(4,128)(2,1)S(1)}, u32[]{:S(2)}, u32[]{:S(2)}) collective-permute-start(bf16[2,4,4096]{2,1,0:T(4,128)(2,1)S(1)} %get-tuple-element.34), channel_id=1, source_target_pairs={{0,1},{1,0},{2,3},{3,2},{4,5},{5,4},{6,7},{7,6},{8,9},{9,8},{10,11... | collective-permute-start | bytes 196616 | tf_op jit(solution)/shard_map/ppermute | solution.py:605
  34.5 4.3 %collective-permute-start.11 = (bf16[2,4,4096]{2,1,0:T(4,128)(2,1)S(1)}, bf16[2,4,4096]{2,1,0:T(4,128)(2,1)S(1)}, u32[]{:S(2)}, u32[]{:S(2)}) collective-permute-start(bf16[2,4,4096]{2,1,0:T(4,128)(2,1)S(1)} %add_convert_fusion.1), channel_id=1, source_target_pairs={{0,2},{2,0},{1,3},{3,1},{4,6},{6,4},{5,7},{7,5},{8,10},{10,8},{9,1... | collective-permute-start | bytes 196616 | tf_op jit(solution)/shard_map/ppermute | solution.py:607

commit v5 on v4

--- a/solution.py
+++ b/solution.py
@@ -573,17 +573,19 @@
     k_mate = lax.ppermute(key_cache, "batch", swap)
     v_mate = lax.ppermute(value_cache, "batch", swap)
     len_mate = lax.ppermute(lengths, "batch", swap)
+
+    own, *sends = project(
+        inputs, norm_gain, wq_packed, wq_scales, key_weight, value_weight, nw, nb
+    )
+    own, k_mate, v_mate, len_mate, *sends = lax.optimization_barrier(
+        (own, k_mate, v_mate, len_mate, *sends)
+    )
     first = lax.axis_index("batch") == 0
     len_all = jnp.where(
         first, jnp.concatenate([lengths, len_mate]), jnp.concatenate([len_mate, lengths])
     )
     positions = jnp.concatenate([len_all + step for step in range(STEPS)])
     table = rotary_tables(positions)
-
-    own, *sends = project(
-        inputs, norm_gain, wq_packed, wq_scales, key_weight, value_weight, nw, nb
-    )
-    own, k_mate, v_mate, *sends = lax.optimization_barrier((own, k_mate, v_mate, *sends))
     parts = [
         lax.ppermute(piece, "width", [(i, i ^ s) for i in range(nw)])
         for s, piece in enumerate(sends, 1)

time: 39.6 us -> 39.5 us (level)
  no operation moved by 1% of the time
where the time goes in v5:
time: 39.5 us; the launch traced here: 39.4 us
  Pallas kernels  20.1 us (51%)
  starting transfers between devices  12.9 us (33%)
  waiting for transfers between devices  5.21 us (13%)
  other arithmetic  1.03 us (3%)
    pallas_call x1, Pallas kernels, project(): pl.pallas_call(project_kernel, in_specs=[HBM] * 6, out_specs=[VMEM] * nw,...  8.04 us
    ppermute x3, starting transfers between devices, split_heads(): lax.ppermute(piece, 'width', [(i, i ^ s) for i in range(nw)])  5.31 us
    pallas_call x2, Pallas kernels, fetch_weight(): pl.pallas_call(body, in_specs=[HBM, ANY], out_specs=VMEM, out_shape=pltpu...  5.13 us
    ppermute x3, starting transfers between devices, split_heads(): lax.ppermute(mixed, 'width', [(i, i ^ s) for i in range(nw)])  4.45 us
    pallas_call x1, Pallas kernels, attend(): pl.pallas_call(body, in_specs=[pl.BlockSpec(memory_space=pltpu.SMEM)] + [...  3.96 us
    pallas_call x1, Pallas kernels, output(): pl.pallas_call(body, in_specs=[VMEM] * (nw + count), out_specs=[VMEM] * n...  3 us
    ppermute x1, waiting for transfers between devices, split_heads(): far = lax.ppermute(leaving, 'hidden', swap)  2.76 us
    ppermute x3, waiting for transfers between devices, split_heads(): lax.ppermute(piece, 'width', [(i, i ^ s) for i in range(nw)])  1.69 us
  transfers between devices with their start and end apart: 12, of which 3 were waited for; matrix products, arithmetic and copies ran while one was open for 1% of the time, Pallas kernels for 33%

profile of v5, /device:TPU:0, one launch (start us, length us, event | category | flops | bytes accessed | tf_op | source)
XLA Modules:
  0.0 39.4 jit_solution(8590108181866739331)
XLA Ops:
  0.0 0.5 %collective-permute-start = (bf16[2,1024,256]{2,1,0:T(8,128)(2,1)}, bf16[2,1024,256]{2,1,0:T(8,128)(2,1)S(1)}, u32[]{:S(2)}, u32[]{:S(2)}) collective-permute-start(bf16[2,1024,256]{2,1,0:T(8,128)(2,1)} %refs_9_.1), channel_id=1, source_target_pairs={{0,1},{1,0},{2,3},{3,2},{4,5},{5,4},{6,7},{7,6},{8,9},{9,8},{10,11... | collective-permute-start | bytes 3145736 | tf_op jit(solution)/shard_map/ppermute | solution.py:573
  0.5 0.1 collective-permute-start.1
  0.5 0.5 %collective-permute-start.2 = (s32[2]{0:T(128)}, s32[2]{0:T(128)S(1)}, u32[]{:S(2)}, u32[]{:S(2)}) collective-permute-start(s32[2]{0:T(128)} %param.19), channel_id=1, source_target_pairs={{0,1},{1,0},{2,3},{3,2},{4,5},{5,4},{6,7},{7,6},{8,9},{9,8},{10,11... | collective-permute-start | bytes 32 | tf_op jit(solution)/shard_map/ppermute | solution.py:575
  1.0 8.0 %project.1 = (f32[8,2432]{1,0:T(8,128)S(1)}, bf16[8,2432]{1,0:T(8,128)(2,1)S(1)}, bf16[8,2432]{1,0:T(8,128)(2,1)S(1)}, bf16[8,2432]{1,0:T(8,128)(2,1)S(1)}) custom-call(bf16[2,16,4096]{2,1,0:T(8,128)(2,1)} %x_hbm.1, f32[1,4096]{1,0:T(1,128)} %bitcast.1, s32[4096,2048]{1,0:T(8,128)} %wq_hbm.1, f32[32,4096]{1,0:T(8,128)} %scale_hbm.1, ...), custom_call_target="tpu_custom_call" | custom-call | tf_op jit(solution)/shard_map/project/pallas_call | solution.py:297
  9.0 0.0 collective-permute-done.2
  9.1 0.0 collective-permute-done.refs_10_
  9.1 0.0 collective-permute-done.1.refs_12_
  9.1 4.7 %collective-permute-start.3 = (bf16[8,2432]{1,0:T(8,128)(2,1)S(1)}, bf16[8,2432]{1,0:T(8,128)(2,1)S(1)}, u32[]{:S(2)}, u32[]{:S(2)}) collective-permute-start(bf16[8,2432]{1,0:T(8,128)(2,1)S(1)} %get-tuple-element.28), channel_id=1, source_target_pairs={{0,12},{4,8},{8,4},{12,0},{1,13},{5,9},{9,5},{13,1},{2,14},{6,10},... | collective-permute-start | bytes 116744 | tf_op jit(solution)/shard_map/ppermute | solution.py:590
  13.8 0.0 collective-permute-start.4
  13.8 0.6 %collective-permute-start.5 = (bf16[8,2432]{1,0:T(8,128)(2,1)S(1)}, bf16[8,2432]{1,0:T(8,128)(2,1)S(1)}, u32[]{:S(2)}, u32[]{:S(2)}) collective-permute-start(bf16[8,2432]{1,0:T(8,128)(2,1)S(1)} %get-tuple-element.30), channel_id=1, source_target_pairs={{0,4},{4,0},{8,12},{12,8},{1,5},{5,1},{9,13},{13,9},{2,6},{6,2},{1... | collective-permute-start | bytes 116744 | tf_op jit(solution)/shard_map/ppermute | solution.py:590
  14.4 0.1 broadcast_add_fusion
  14.5 0.1 add_convert_fusion.2
  14.6 0.1 fusion.1
  14.7 2.2 %fetch.2.refs_14_.refs_4_ = bf16[512,4096]{1,0:T(8,128)(2,1)S(1)} custom-call(bf16[4096,4096]{1,0:T(8,128)(2,1)} %src.3, f32[8,2432]{1,0:T(8,128)S(1)} %get-tuple-element.27.after.refs_1_), custom_call_target="tpu_custom_call" | custom-call | tf_op jit(solution)/shard_map/fetch/pallas_call | solution.py:350
  16.9 0.0 collective-permute-done.3.refs_2_
  16.9 1.7 %collective-permute-done.4.refs_3_ = bf16[8,2432]{1,0:T(8,128)(2,1)S(1)} collective-permute-done((bf16[8,2432]{1,0:T(8,128)(2,1)S(1)}, bf16[8,2432]{1,0:T(8,128)(2,1)S(1)}, u32[]{:S(2)}, u32[]{:S(2)}) %collective-permute-start.4) | collective-permute-done | bytes 38944 | tf_op jit(solution)/shard_map/ppermute | solution.py:590
  18.6 0.0 collective-permute-done.5.refs_4_
  18.6 4.0 %attend.1 = (bf16[8,2048]{1,0:T(8,128)(2,1)S(1)}, bf16[768,4096]{1,0:T(8,128)(2,1)S(1)}) custom-call(s32[4]{0:T(128)S(1)} %get-tuple-element.40.refs_0_, f32[8,2432]{1,0:T(8,128)S(1)} %get-tuple-element.27.after.refs_1_, bf16[8,2432]{1,0:T(8,128)(2,1)S(1)} %collective-permute-done.3.refs_2_, bf16[8,2432]{1,0:T(8,128)(2,1)S(1)} %collective-permute-done.4.refs_3_, ...), custom_call_target="tpu_custom_call" | custom-call | tf_op jit(solution)/shard_map/attend/pallas_call | solution.py:476
  22.6 2.2 %collective-permute-start.8 = (bf16[8,2048]{1,0:T(8,128)(2,1)S(1)}, bf16[8,2048]{1,0:T(8,128)(2,1)S(1)}, u32[]{:S(2)}, u32[]{:S(2)}) collective-permute-start(bf16[8,2048]{1,0:T(8,128)(2,1)S(1)} %get-tuple-element.33.after.refs_0_), channel_id=1, source_target_pairs={{0,12},{4,8},{8,4},{12,0},{1,13},{5,9},{9,5},{13,1},{2,14},{6,10},... | collective-permute-start | bytes 98312 | tf_op jit(solution)/shard_map/ppermute | solution.py:603
  24.8 0.1 collective-permute-start.7
  24.9 2.2 %collective-permute-start.6 = (bf16[8,2048]{1,0:T(8,128)(2,1)S(1)}, bf16[8,2048]{1,0:T(8,128)(2,1)S(1)}, u32[]{:S(2)}, u32[]{:S(2)}) collective-permute-start(bf16[8,2048]{1,0:T(8,128)(2,1)S(1)} %get-tuple-element.33.after.refs_0_), channel_id=1, source_target_pairs={{0,4},{4,0},{8,12},{12,8},{1,5},{5,1},{9,13},{13,9},{2,6},{6,2},{1... | collective-permute-start | bytes 98312 | tf_op jit(solution)/shard_map/ppermute | solution.py:603
  27.1 2.9 %fetch.3.refs_6_ = bf16[768,4096]{1,0:T(8,128)(2,1)S(1)} custom-call(bf16[4096,4096]{1,0:T(8,128)(2,1)} %src.3, bf16[8,2048]{1,0:T(8,128)(2,1)S(1)} %get-tuple-element.33.after.refs_0_), custom_call_target="tpu_custom_call" | custom-call | tf_op jit(solution)/shard_map/fetch/pallas_call | solution.py:350
  29.9 0.0 collective-permute-done.8.refs_3_
  30.0 0.0 collective-permute-done.7.refs_2_
  30.0 0.0 collective-permute-done.6.refs_1_
  30.0 3.0 %output.1 = (f32[2,4,4096]{2,1,0:T(4,128)S(1)}, bf16[2,4,4096]{2,1,0:T(4,128)(2,1)S(1)}, f32[2,4,4096]{2,1,0:T(4,128)S(1)}, bf16[2,4,4096]{2,1,0:T(4,128)(2,1)S(1)}) custom-call(bf16[8,2048]{1,0:T(8,128)(2,1)S(1)} %get-tuple-element.33.after.refs_0_, bf16[8,2048]{1,0:T(8,128)(2,1)S(1)} %collective-permute-done.6.refs_1_, ...), custom_call_target="tpu_custom_call" | custom-call | tf_op jit(solution)/shard_map/output/pallas_call | solution.py:532
  33.0 0.1 collective-permute-start.10
  33.1 0.5 %collective-permute-start.9 = (bf16[2,4,4096]{2,1,0:T(4,128)(2,1)S(1)}, bf16[2,4,4096]{2,1,0:T(4,128)(2,1)S(1)}, u32[]{:S(2)}, u32[]{:S(2)}) collective-permute-start(bf16[2,4,4096]{2,1,0:T(4,128)(2,1)S(1)} %get-tuple-element.36), channel_id=1, source_target_pairs={{0,1},{1,0},{2,3},{3,2},{4,5},{5,4},{6,7},{7,6},{8,9},{9,8},{10,11... | collective-permute-start | bytes 196616 | tf_op jit(solution)/shard_map/ppermute | solution.py:607
  33.6 0.7 %collective-permute-done.10 = bf16[2,4,4096]{2,1,0:T(4,128)(2,1)S(1)} collective-permute-done((bf16[2,4,4096]{2,1,0:T(4,128)(2,1)S(1)}, bf16[2,4,4096]{2,1,0:T(4,128)(2,1)S(1)}, u32[]{:S(2)}, u32[]{:S(2)}) %collective-permute-start.10) | collective-permute-done | bytes 65568 | tf_op jit(solution)/shard_map/ppermute | solution.py:606
  34.4 1.6 %collective-permute-start.11 = (bf16[2,4,4096]{2,1,0:T(4,128)(2,1)S(1)}, bf16[2,4,4096]{2,1,0:T(4,128)(2,1)S(1)}, u32[]{:S(2)}, u32[]{:S(2)}) collective-permute-start(bf16[2,4,4096]{2,1,0:T(4,128)(2,1)S(1)} %add_convert_fusion.1), channel_id=1, source_target_pairs={{0,2},{2,0},{1,3},{3,1},{4,6},{6,4},{5,7},{7,5},{8,10},{10,8},{9,1... | collective-permute-start | bytes 196616 | tf_op jit(solution)/shard_map/ppermute | solution.py:609
  35.9 2.8 %collective-permute-done.11 = bf16[2,4,4096]{2,1,0:T(4,128)(2,1)S(1)} collective-permute-done((bf16[2,4,4096]{2,1,0:T(4,128)(2,1)S(1)}, bf16[2,4,4096]{2,1,0:T(4,128)(2,1)S(1)}, u32[]{:S(2)}, u32[]{:S(2)}) %collective-permute-start.11) | collective-permute-done | bytes 65568 | tf_op jit(solution)/shard_map/ppermute | solution.py:609
  38.7 0.7 %add_convert_fusion = bf16[2,4,4096]{2,1,0:T(4,128)(2,1)} fusion(bf16[2,4,4096]{2,1,0:T(4,128)(2,1)S(1)} %collective-permute-done.11, f32[2,4,4096]{2,1,0:T(4,128)S(1)} %get-tuple-element.35, bf16[2,4,4096]{2,1,0:T(4,128)(2,1)S(1)} %collective-permute-done.9), kind=kLoop, calls=%fused_computation | loop fusion | flops 163840 | bytes 327680 | tf_op jit(solution)/shard_map/convert_element_type | solution.py:611
  (6 shorter events, 0.1 us)
Async XLA Ops:
  0.0 9.1 %collective-permute-start = (bf16[2,1024,256]{2,1,0:T(8,128)(2,1)}, bf16[2,1024,256]{2,1,0:T(8,128)(2,1)S(1)}, u32[]{:S(2)}, u32[]{:S(2)}) collective-permute-start(bf16[2,1024,256]{2,1,0:T(8,128)(2,1)} %refs_9_.1), channel_id=1, source_target_pairs={{0,1},{1,0},{2,3},{3,2},{4,5},{5,4},{6,7},{7,6},{8,9},{9,8},{10,11... | collective-permute-start | bytes 3145736 | tf_op jit(solution)/shard_map/ppermute | solution.py:573
  0.5 8.6 %collective-permute-start.1 = (bf16[2,1024,256]{2,1,0:T(8,128)(2,1)}, bf16[2,1024,256]{2,1,0:T(8,128)(2,1)S(1)}, u32[]{:S(2)}, u32[]{:S(2)}) collective-permute-start(bf16[2,1024,256]{2,1,0:T(8,128)(2,1)} %refs_11_.1), channel_id=1, source_target_pairs={{0,1},{1,0},{2,3},{3,2},{4,5},{5,4},{6,7},{7,6},{8,9},{9,8},{10,11... | collective-permute-start | bytes 3145736 | tf_op jit(solution)/shard_map/ppermute | solution.py:574
  0.5 8.5 %collective-permute-start.2 = (s32[2]{0:T(128)}, s32[2]{0:T(128)S(1)}, u32[]{:S(2)}, u32[]{:S(2)}) collective-permute-start(s32[2]{0:T(128)} %param.19), channel_id=1, source_target_pairs={{0,1},{1,0},{2,3},{3,2},{4,5},{5,4},{6,7},{7,6},{8,9},{9,8},{10,11... | collective-permute-start | bytes 32 | tf_op jit(solution)/shard_map/ppermute | solution.py:575
  1.0 13.4 %copy-start = (s32[2]{0:T(128)S(1)}, s32[2]{0:T(128)}, u32[]{:S(2)}) copy-start(s32[2]{0:T(128)} %param.19) | copy-start | bytes 28
  9.1 7.9 %collective-permute-start.3 = (bf16[8,2432]{1,0:T(8,128)(2,1)S(1)}, bf16[8,2432]{1,0:T(8,128)(2,1)S(1)}, u32[]{:S(2)}, u32[]{:S(2)}) collective-permute-start(bf16[8,2432]{1,0:T(8,128)(2,1)S(1)} %get-tuple-element.28), channel_id=1, source_target_pairs={{0,12},{4,8},{8,4},{12,0},{1,13},{5,9},{9,5},{13,1},{2,14},{6,10},... | collective-permute-start | bytes 116744 | tf_op jit(solution)/shard_map/ppermute | solution.py:590
  13.8 4.9 %collective-permute-start.4 = (bf16[8,2432]{1,0:T(8,128)(2,1)S(1)}, bf16[8,2432]{1,0:T(8,128)(2,1)S(1)}, u32[]{:S(2)}, u32[]{:S(2)}) collective-permute-start(bf16[8,2432]{1,0:T(8,128)(2,1)S(1)} %get-tuple-element.29), channel_id=1, source_target_pairs={{0,8},{4,12},{8,0},{12,4},{1,9},{5,13},{9,1},{13,5},{2,10},{6,14},... | collective-permute-start | bytes 116744 | tf_op jit(solution)/shard_map/ppermute | solution.py:590
  13.8 4.9 %collective-permute-start.5 = (bf16[8,2432]{1,0:T(8,128)(2,1)S(1)}, bf16[8,2432]{1,0:T(8,128)(2,1)S(1)}, u32[]{:S(2)}, u32[]{:S(2)}) collective-permute-start(bf16[8,2432]{1,0:T(8,128)(2,1)S(1)} %get-tuple-element.30), channel_id=1, source_target_pairs={{0,4},{4,0},{8,12},{12,8},{1,5},{5,1},{9,13},{13,9},{2,6},{6,2},{1... | collective-permute-start | bytes 116744 | tf_op jit(solution)/shard_map/ppermute | solution.py:590
  22.6 7.3 %collective-permute-start.8 = (bf16[8,2048]{1,0:T(8,128)(2,1)S(1)}, bf16[8,2048]{1,0:T(8,128)(2,1)S(1)}, u32[]{:S(2)}, u32[]{:S(2)}) collective-permute-start(bf16[8,2048]{1,0:T(8,128)(2,1)S(1)} %get-tuple-element.33.after.refs_0_), channel_id=1, source_target_pairs={{0,12},{4,8},{8,4},{12,0},{1,13},{5,9},{9,5},{13,1},{2,14},{6,10},... | collective-permute-start | bytes 98312 | tf_op jit(solution)/shard_map/ppermute | solution.py:603
  24.8 5.2 %collective-permute-start.7 = (bf16[8,2048]{1,0:T(8,128)(2,1)S(1)}, bf16[8,2048]{1,0:T(8,128)(2,1)S(1)}, u32[]{:S(2)}, u32[]{:S(2)}) collective-permute-start(bf16[8,2048]{1,0:T(8,128)(2,1)S(1)} %get-tuple-element.33.after.refs_0_), channel_id=1, source_target_pairs={{0,8},{4,12},{8,0},{12,4},{1,9},{5,13},{9,1},{13,5},{2,10},{6,14},... | collective-permute-start | bytes 98312 | tf_op jit(solution)/shard_map/ppermute | solution.py:603
  24.9 5.1 %collective-permute-start.6 = (bf16[8,2048]{1,0:T(8,128)(2,1)S(1)}, bf16[8,2048]{1,0:T(8,128)(2,1)S(1)}, u32[]{:S(2)}, u32[]{:S(2)}) collective-permute-start(bf16[8,2048]{1,0:T(8,128)(2,1)S(1)} %get-tuple-element.33.after.refs_0_), channel_id=1, source_target_pairs={{0,4},{4,0},{8,12},{12,8},{1,5},{5,1},{9,13},{13,9},{2,6},{6,2},{1... | collective-permute-start | bytes 98312 | tf_op jit(solution)/shard_map/ppermute | solution.py:603
  33.0 1.3 %collective-permute-start.10 = (bf16[2,4,4096]{2,1,0:T(4,128)(2,1)S(1)}, bf16[2,4,4096]{2,1,0:T(4,128)(2,1)S(1)}, u32[]{:S(2)}, u32[]{:S(2)}) collective-permute-start(bf16[2,4,4096]{2,1,0:T(4,128)(2,1)S(1)} %get-tuple-element.38), channel_id=1, source_target_pairs={{0,1},{1,0},{2,3},{3,2},{4,5},{5,4},{6,7},{7,6},{8,9},{9,8},{10,11... | collective-permute-start | bytes 196616 | tf_op jit(solution)/shard_map/ppermute | solution.py:606
  33.1 2.9 %collective-permute-start.9 = (bf16[2,4,4096]{2,1,0:T(4,128)(2,1)S(1)}, bf16[2,4,4096]{2,1,0:T(4,128)(2,1)S(1)}, u32[]{:S(2)}, u32[]{:S(2)}) collective-permute-start(bf16[2,4,4096]{2,1,0:T(4,128)(2,1)S(1)} %get-tuple-element.36), channel_id=1, source_target_pairs={{0,1},{1,0},{2,3},{3,2},{4,5},{5,4},{6,7},{7,6},{8,9},{9,8},{10,11... | collective-permute-start | bytes 196616 | tf_op jit(solution)/shard_map/ppermute | solution.py:607
  34.4 4.3 %collective-permute-start.11 = (bf16[2,4,4096]{2,1,0:T(4,128)(2,1)S(1)}, bf16[2,4,4096]{2,1,0:T(4,128)(2,1)S(1)}, u32[]{:S(2)}, u32[]{:S(2)}) collective-permute-start(bf16[2,4,4096]{2,1,0:T(4,128)(2,1)S(1)} %add_convert_fusion.1), channel_id=1, source_target_pairs={{0,2},{2,0},{1,3},{3,1},{4,6},{6,4},{5,7},{7,5},{8,10},{10,8},{9,1... | collective-permute-start | bytes 196616 | tf_op jit(solution)/shard_map/ppermute | solution.py:609

commit v6 on v5

--- a/solution.py
+++ b/solution.py
@@ -604,10 +604,11 @@
     ]
     here, across_core, across_chip, across_both = output(pieces, [w_early, w_middle, w_late])
     relay = lax.ppermute(across_both, "batch", swap)
+    leaving = (across_chip + relay.astype(F32)).astype(BF16)
+    leaving, across_core = lax.optimization_barrier((leaving, across_core))
+    far = lax.ppermute(leaving, "hidden", swap)
     near = lax.ppermute(across_core, "batch", swap)
-    leaving = (across_chip + relay.astype(F32)).astype(BF16)
-    far = lax.ppermute(leaving, "hidden", swap)
-    sums = here + near.astype(F32) + far.astype(F32)
+    sums = here + far.astype(F32) + near.astype(F32)
     return sums.astype(BF16)
 
 

time: 39.5 us -> 39.5 us (level)
  starting transfers between devices: 12.9 us -> 12.4 us
  waiting for transfers between devices: 5.21 us -> 5.71 us
    ppermute x1, waiting for transfers between devices: 0.74 us -> 1.24 us  [split_heads(): relay = lax.ppermute(across_both, 'batch', swap)]
    ppermute x1, starting transfers between devices: 0.5 us -> 0.01 us  [split_heads(): near = lax.ppermute(across_core, 'batch', swap)]
where the time goes in v6:
time: 39.5 us; the launch traced here: 39.4 us
  Pallas kernels  20.1 us (51%)
  starting transfers between devices  12.4 us (31%)
  waiting for transfers between devices  5.71 us (14%)
  other arithmetic  1.03 us (3%)
    pallas_call x1, Pallas kernels, project(): pl.pallas_call(project_kernel, in_specs=[HBM] * 6, out_specs=[VMEM] * nw,...  8.04 us
    ppermute x3, starting transfers between devices, split_heads(): lax.ppermute(piece, 'width', [(i, i ^ s) for i in range(nw)])  5.31 us
    pallas_call x2, Pallas kernels, fetch_weight(): pl.pallas_call(body, in_specs=[HBM, ANY], out_specs=VMEM, out_shape=pltpu...  5.13 us
    ppermute x3, starting transfers between devices, split_heads(): lax.ppermute(mixed, 'width', [(i, i ^ s) for i in range(nw)])  4.45 us
    pallas_call x1, Pallas kernels, attend(): pl.pallas_call(body, in_specs=[pl.BlockSpec(memory_space=pltpu.SMEM)] + [...  3.96 us
    pallas_call x1, Pallas kernels, output(): pl.pallas_call(body, in_specs=[VMEM] * (nw + count), out_specs=[VMEM] * n...  3 us
    ppermute x1, waiting for transfers between devices, split_heads(): far = lax.ppermute(leaving, 'hidden', swap)  2.76 us
    ppermute x3, waiting for transfers between devices, split_heads(): lax.ppermute(piece, 'width', [(i, i ^ s) for i in range(nw)])  1.69 us
  transfers between devices with their start and end apart: 12, of which 3 were waited for; matrix products, arithmetic and copies ran while one was open for 1% of the time, Pallas kernels for 33%

profile of v6, /device:TPU:0, one launch (start us, length us, event | category | flops | bytes accessed | tf_op | source)
XLA Modules:
  0.0 39.4 jit_solution(16253969606922838489)
XLA Ops:
  0.0 0.5 %collective-permute-start = (bf16[2,1024,256]{2,1,0:T(8,128)(2,1)}, bf16[2,1024,256]{2,1,0:T(8,128)(2,1)S(1)}, u32[]{:S(2)}, u32[]{:S(2)}) collective-permute-start(bf16[2,1024,256]{2,1,0:T(8,128)(2,1)} %refs_9_.1), channel_id=1, source_target_pairs={{0,1},{1,0},{2,3},{3,2},{4,5},{5,4},{6,7},{7,6},{8,9},{9,8},{10,11... | collective-permute-start | bytes 3145736 | tf_op jit(solution)/shard_map/ppermute | solution.py:573
  0.5 0.1 collective-permute-start.1
  0.5 0.5 %collective-permute-start.2 = (s32[2]{0:T(128)}, s32[2]{0:T(128)S(1)}, u32[]{:S(2)}, u32[]{:S(2)}) collective-permute-start(s32[2]{0:T(128)} %param.19), channel_id=1, source_target_pairs={{0,1},{1,0},{2,3},{3,2},{4,5},{5,4},{6,7},{7,6},{8,9},{9,8},{10,11... | collective-permute-start | bytes 32 | tf_op jit(solution)/shard_map/ppermute | solution.py:575
  1.0 8.0 %project.1 = (f32[8,2432]{1,0:T(8,128)S(1)}, bf16[8,2432]{1,0:T(8,128)(2,1)S(1)}, bf16[8,2432]{1,0:T(8,128)(2,1)S(1)}, bf16[8,2432]{1,0:T(8,128)(2,1)S(1)}) custom-call(bf16[2,16,4096]{2,1,0:T(8,128)(2,1)} %x_hbm.1, f32[1,4096]{1,0:T(1,128)} %bitcast.1, s32[4096,2048]{1,0:T(8,128)} %wq_hbm.1, f32[32,4096]{1,0:T(8,128)} %scale_hbm.1, ...), custom_call_target="tpu_custom_call" | custom-call | tf_op jit(solution)/shard_map/project/pallas_call | solution.py:297
  9.0 0.0 collective-permute-done.2
  9.1 0.0 collective-permute-done.refs_10_
  9.1 0.0 collective-permute-done.1.refs_12_
  9.1 4.7 %collective-permute-start.3 = (bf16[8,2432]{1,0:T(8,128)(2,1)S(1)}, bf16[8,2432]{1,0:T(8,128)(2,1)S(1)}, u32[]{:S(2)}, u32[]{:S(2)}) collective-permute-start(bf16[8,2432]{1,0:T(8,128)(2,1)S(1)} %get-tuple-element.30), channel_id=1, source_target_pairs={{0,12},{4,8},{8,4},{12,0},{1,13},{5,9},{9,5},{13,1},{2,14},{6,10},... | collective-permute-start | bytes 116744 | tf_op jit(solution)/shard_map/ppermute | solution.py:590
  13.8 0.0 collective-permute-start.4
  13.8 0.6 %collective-permute-start.5 = (bf16[8,2432]{1,0:T(8,128)(2,1)S(1)}, bf16[8,2432]{1,0:T(8,128)(2,1)S(1)}, u32[]{:S(2)}, u32[]{:S(2)}) collective-permute-start(bf16[8,2432]{1,0:T(8,128)(2,1)S(1)} %get-tuple-element.32), channel_id=1, source_target_pairs={{0,4},{4,0},{8,12},{12,8},{1,5},{5,1},{9,13},{13,9},{2,6},{6,2},{1... | collective-permute-start | bytes 116744 | tf_op jit(solution)/shard_map/ppermute | solution.py:590
  14.4 0.1 broadcast_add_fusion
  14.5 0.1 add_convert_fusion.2
  14.6 0.1 fusion.1
  14.7 2.2 %fetch.2.refs_14_.refs_4_ = bf16[512,4096]{1,0:T(8,128)(2,1)S(1)} custom-call(bf16[4096,4096]{1,0:T(8,128)(2,1)} %src.3, f32[8,2432]{1,0:T(8,128)S(1)} %get-tuple-element.29.after.refs_1_), custom_call_target="tpu_custom_call" | custom-call | tf_op jit(solution)/shard_map/fetch/pallas_call | solution.py:350
  16.9 0.0 collective-permute-done.3.refs_2_
  16.9 1.7 %collective-permute-done.4.refs_3_ = bf16[8,2432]{1,0:T(8,128)(2,1)S(1)} collective-permute-done((bf16[8,2432]{1,0:T(8,128)(2,1)S(1)}, bf16[8,2432]{1,0:T(8,128)(2,1)S(1)}, u32[]{:S(2)}, u32[]{:S(2)}) %collective-permute-start.4) | collective-permute-done | bytes 38944 | tf_op jit(solution)/shard_map/ppermute | solution.py:590
  18.6 0.0 collective-permute-done.5.refs_4_
  18.6 4.0 %attend.1 = (bf16[8,2048]{1,0:T(8,128)(2,1)S(1)}, bf16[768,4096]{1,0:T(8,128)(2,1)S(1)}) custom-call(s32[4]{0:T(128)S(1)} %get-tuple-element.44.refs_0_, f32[8,2432]{1,0:T(8,128)S(1)} %get-tuple-element.29.after.refs_1_, bf16[8,2432]{1,0:T(8,128)(2,1)S(1)} %collective-permute-done.3.refs_2_, bf16[8,2432]{1,0:T(8,128)(2,1)S(1)} %collective-permute-done.4.refs_3_, ...), custom_call_target="tpu_custom_call" | custom-call | tf_op jit(solution)/shard_map/attend/pallas_call | solution.py:476
  22.6 2.2 %collective-permute-start.8 = (bf16[8,2048]{1,0:T(8,128)(2,1)S(1)}, bf16[8,2048]{1,0:T(8,128)(2,1)S(1)}, u32[]{:S(2)}, u32[]{:S(2)}) collective-permute-start(bf16[8,2048]{1,0:T(8,128)(2,1)S(1)} %get-tuple-element.35.after.refs_0_), channel_id=1, source_target_pairs={{0,12},{4,8},{8,4},{12,0},{1,13},{5,9},{9,5},{13,1},{2,14},{6,10},... | collective-permute-start | bytes 98312 | tf_op jit(solution)/shard_map/ppermute | solution.py:603
  24.8 0.1 collective-permute-start.7
  24.9 2.2 %collective-permute-start.6 = (bf16[8,2048]{1,0:T(8,128)(2,1)S(1)}, bf16[8,2048]{1,0:T(8,128)(2,1)S(1)}, u32[]{:S(2)}, u32[]{:S(2)}) collective-permute-start(bf16[8,2048]{1,0:T(8,128)(2,1)S(1)} %get-tuple-element.35.after.refs_0_), channel_id=1, source_target_pairs={{0,4},{4,0},{8,12},{12,8},{1,5},{5,1},{9,13},{13,9},{2,6},{6,2},{1... | collective-permute-start | bytes 98312 | tf_op jit(solution)/shard_map/ppermute | solution.py:603
  27.1 2.9 %fetch.3.refs_6_ = bf16[768,4096]{1,0:T(8,128)(2,1)S(1)} custom-call(bf16[4096,4096]{1,0:T(8,128)(2,1)} %src.3, bf16[8,2048]{1,0:T(8,128)(2,1)S(1)} %get-tuple-element.35.after.refs_0_), custom_call_target="tpu_custom_call" | custom-call | tf_op jit(solution)/shard_map/fetch/pallas_call | solution.py:350
  29.9 0.0 collective-permute-done.8.refs_3_
  30.0 0.0 collective-permute-done.7.refs_2_
  30.0 0.0 collective-permute-done.6.refs_1_
  30.0 3.0 %output.1 = (f32[2,4,4096]{2,1,0:T(4,128)S(1)}, bf16[2,4,4096]{2,1,0:T(4,128)(2,1)S(1)}, f32[2,4,4096]{2,1,0:T(4,128)S(1)}, bf16[2,4,4096]{2,1,0:T(4,128)(2,1)S(1)}) custom-call(bf16[8,2048]{1,0:T(8,128)(2,1)S(1)} %get-tuple-element.35.after.refs_0_, bf16[8,2048]{1,0:T(8,128)(2,1)S(1)} %collective-permute-done.6.refs_1_, ...), custom_call_target="tpu_custom_call" | custom-call | tf_op jit(solution)/shard_map/output/pallas_call | solution.py:532
  33.0 0.1 collective-permute-start.9
  33.1 1.2 %collective-permute-done.9 = bf16[2,4,4096]{2,1,0:T(4,128)(2,1)S(1)} collective-permute-done((bf16[2,4,4096]{2,1,0:T(4,128)(2,1)S(1)}, bf16[2,4,4096]{2,1,0:T(4,128)(2,1)S(1)}, u32[]{:S(2)}, u32[]{:S(2)}) %collective-permute-start.9) | collective-permute-done | bytes 65568 | tf_op jit(solution)/shard_map/ppermute | solution.py:606
  34.4 1.6 %collective-permute-start.10 = (bf16[2,4,4096]{2,1,0:T(4,128)(2,1)S(1)}, bf16[2,4,4096]{2,1,0:T(4,128)(2,1)S(1)}, u32[]{:S(2)}, u32[]{:S(2)}) collective-permute-start(bf16[2,4,4096]{2,1,0:T(4,128)(2,1)S(1)} %add_convert_fusion.1), channel_id=1, source_target_pairs={{0,2},{2,0},{1,3},{3,1},{4,6},{6,4},{5,7},{7,5},{8,10},{10,8},{9,1... | collective-permute-start | bytes 196616 | tf_op jit(solution)/shard_map/ppermute | solution.py:609
  35.9 0.0 collective-permute-start.11
  35.9 2.8 %collective-permute-done.10 = bf16[2,4,4096]{2,1,0:T(4,128)(2,1)S(1)} collective-permute-done((bf16[2,4,4096]{2,1,0:T(4,128)(2,1)S(1)}, bf16[2,4,4096]{2,1,0:T(4,128)(2,1)S(1)}, u32[]{:S(2)}, u32[]{:S(2)}) %collective-permute-start.10) | collective-permute-done | bytes 65568 | tf_op jit(solution)/shard_map/ppermute | solution.py:609
  38.7 0.7 %add_convert_fusion = bf16[2,4,4096]{2,1,0:T(4,128)(2,1)} fusion(bf16[2,4,4096]{2,1,0:T(4,128)(2,1)S(1)} %collective-permute-done.11, f32[2,4,4096]{2,1,0:T(4,128)S(1)} %get-tuple-element.37, bf16[2,4,4096]{2,1,0:T(4,128)(2,1)S(1)} %collective-permute-done.10), kind=kLoop, calls=%fused_computation | loop fusion | flops 163840 | bytes 327680 | tf_op jit(solution)/shard_map/convert_element_type | solution.py:612
  (6 shorter events, 0.1 us)
Async XLA Ops:
  0.0 9.1 %collective-permute-start = (bf16[2,1024,256]{2,1,0:T(8,128)(2,1)}, bf16[2,1024,256]{2,1,0:T(8,128)(2,1)S(1)}, u32[]{:S(2)}, u32[]{:S(2)}) collective-permute-start(bf16[2,1024,256]{2,1,0:T(8,128)(2,1)} %refs_9_.1), channel_id=1, source_target_pairs={{0,1},{1,0},{2,3},{3,2},{4,5},{5,4},{6,7},{7,6},{8,9},{9,8},{10,11... | collective-permute-start | bytes 3145736 | tf_op jit(solution)/shard_map/ppermute | solution.py:573
  0.5 8.6 %collective-permute-start.1 = (bf16[2,1024,256]{2,1,0:T(8,128)(2,1)}, bf16[2,1024,256]{2,1,0:T(8,128)(2,1)S(1)}, u32[]{:S(2)}, u32[]{:S(2)}) collective-permute-start(bf16[2,1024,256]{2,1,0:T(8,128)(2,1)} %refs_11_.1), channel_id=1, source_target_pairs={{0,1},{1,0},{2,3},{3,2},{4,5},{5,4},{6,7},{7,6},{8,9},{9,8},{10,11... | collective-permute-start | bytes 3145736 | tf_op jit(solution)/shard_map/ppermute | solution.py:574
  0.5 8.5 %collective-permute-start.2 = (s32[2]{0:T(128)}, s32[2]{0:T(128)S(1)}, u32[]{:S(2)}, u32[]{:S(2)}) collective-permute-start(s32[2]{0:T(128)} %param.19), channel_id=1, source_target_pairs={{0,1},{1,0},{2,3},{3,2},{4,5},{5,4},{6,7},{7,6},{8,9},{9,8},{10,11... | collective-permute-start | bytes 32 | tf_op jit(solution)/shard_map/ppermute | solution.py:575
  1.0 13.4 %copy-start = (s32[2]{0:T(128)S(1)}, s32[2]{0:T(128)}, u32[]{:S(2)}) copy-start(s32[2]{0:T(128)} %param.19) | copy-start | bytes 28
  9.1 7.9 %collective-permute-start.3 = (bf16[8,2432]{1,0:T(8,128)(2,1)S(1)}, bf16[8,2432]{1,0:T(8,128)(2,1)S(1)}, u32[]{:S(2)}, u32[]{:S(2)}) collective-permute-start(bf16[8,2432]{1,0:T(8,128)(2,1)S(1)} %get-tuple-element.30), channel_id=1, source_target_pairs={{0,12},{4,8},{8,4},{12,0},{1,13},{5,9},{9,5},{13,1},{2,14},{6,10},... | collective-permute-start | bytes 116744 | tf_op jit(solution)/shard_map/ppermute | solution.py:590
  13.8 4.9 %collective-permute-start.4 = (bf16[8,2432]{1,0:T(8,128)(2,1)S(1)}, bf16[8,2432]{1,0:T(8,128)(2,1)S(1)}, u32[]{:S(2)}, u32[]{:S(2)}) collective-permute-start(bf16[8,2432]{1,0:T(8,128)(2,1)S(1)} %get-tuple-element.31), channel_id=1, source_target_pairs={{0,8},{4,12},{8,0},{12,4},{1,9},{5,13},{9,1},{13,5},{2,10},{6,14},... | collective-permute-start | bytes 116744 | tf_op jit(solution)/shard_map/ppermute | solution.py:590
  13.8 4.9 %collective-permute-start.5 = (bf16[8,2432]{1,0:T(8,128)(2,1)S(1)}, bf16[8,2432]{1,0:T(8,128)(2,1)S(1)}, u32[]{:S(2)}, u32[]{:S(2)}) collective-permute-start(bf16[8,2432]{1,0:T(8,128)(2,1)S(1)} %get-tuple-element.32), channel_id=1, source_target_pairs={{0,4},{4,0},{8,12},{12,8},{1,5},{5,1},{9,13},{13,9},{2,6},{6,2},{1... | collective-permute-start | bytes 116744 | tf_op jit(solution)/shard_map/ppermute | solution.py:590
  22.6 7.3 %collective-permute-start.8 = (bf16[8,2048]{1,0:T(8,128)(2,1)S(1)}, bf16[8,2048]{1,0:T(8,128)(2,1)S(1)}, u32[]{:S(2)}, u32[]{:S(2)}) collective-permute-start(bf16[8,2048]{1,0:T(8,128)(2,1)S(1)} %get-tuple-element.35.after.refs_0_), channel_id=1, source_target_pairs={{0,12},{4,8},{8,4},{12,0},{1,13},{5,9},{9,5},{13,1},{2,14},{6,10},... | collective-permute-start | bytes 98312 | tf_op jit(solution)/shard_map/ppermute | solution.py:603
  24.8 5.2 %collective-permute-start.7 = (bf16[8,2048]{1,0:T(8,128)(2,1)S(1)}, bf16[8,2048]{1,0:T(8,128)(2,1)S(1)}, u32[]{:S(2)}, u32[]{:S(2)}) collective-permute-start(bf16[8,2048]{1,0:T(8,128)(2,1)S(1)} %get-tuple-element.35.after.refs_0_), channel_id=1, source_target_pairs={{0,8},{4,12},{8,0},{12,4},{1,9},{5,13},{9,1},{13,5},{2,10},{6,14},... | collective-permute-start | bytes 98312 | tf_op jit(solution)/shard_map/ppermute | solution.py:603
  24.9 5.1 %collective-permute-start.6 = (bf16[8,2048]{1,0:T(8,128)(2,1)S(1)}, bf16[8,2048]{1,0:T(8,128)(2,1)S(1)}, u32[]{:S(2)}, u32[]{:S(2)}) collective-permute-start(bf16[8,2048]{1,0:T(8,128)(2,1)S(1)} %get-tuple-element.35.after.refs_0_), channel_id=1, source_target_pairs={{0,4},{4,0},{8,12},{12,8},{1,5},{5,1},{9,13},{13,9},{2,6},{6,2},{1... | collective-permute-start | bytes 98312 | tf_op jit(solution)/shard_map/ppermute | solution.py:603
  33.0 1.3 %collective-permute-start.9 = (bf16[2,4,4096]{2,1,0:T(4,128)(2,1)S(1)}, bf16[2,4,4096]{2,1,0:T(4,128)(2,1)S(1)}, u32[]{:S(2)}, u32[]{:S(2)}) collective-permute-start(bf16[2,4,4096]{2,1,0:T(4,128)(2,1)S(1)} %get-tuple-element.39), channel_id=1, source_target_pairs={{0,1},{1,0},{2,3},{3,2},{4,5},{5,4},{6,7},{7,6},{8,9},{9,8},{10,11... | collective-permute-start | bytes 196616 | tf_op jit(solution)/shard_map/ppermute | solution.py:606
  34.4 4.3 %collective-permute-start.10 = (bf16[2,4,4096]{2,1,0:T(4,128)(2,1)S(1)}, bf16[2,4,4096]{2,1,0:T(4,128)(2,1)S(1)}, u32[]{:S(2)}, u32[]{:S(2)}) collective-permute-start(bf16[2,4,4096]{2,1,0:T(4,128)(2,1)S(1)} %add_convert_fusion.1), channel_id=1, source_target_pairs={{0,2},{2,0},{1,3},{3,1},{4,6},{6,4},{5,7},{7,5},{8,10},{10,8},{9,1... | collective-permute-start | bytes 196616 | tf_op jit(solution)/shard_map/ppermute | solution.py:609
  35.9 2.8 %collective-permute-start.11 = (bf16[2,4,4096]{2,1,0:T(4,128)(2,1)S(1)}, bf16[2,4,4096]{2,1,0:T(4,128)(2,1)S(1)}, u32[]{:S(2)}, u32[]{:S(2)}) collective-permute-start(bf16[2,4,4096]{2,1,0:T(4,128)(2,1)S(1)} %get-tuple-element.42), channel_id=1, source_target_pairs={{0,1},{1,0},{2,3},{3,2},{4,5},{5,4},{6,7},{7,6},{8,9},{9,8},{10,11... | collective-permute-start | bytes 196616 | tf_op jit(solution)/shard_map/ppermute | solution.py:610
